TPU v7x, 256 devices: a whole 4x4x8 slice. The times are simulated.
256 devices in a mesh: req: 32 (over z, x_lo, core), tp: 8 (over x_hi, y).
Axes of the slice: x: 4 (x_hi: 2, x_lo: 2; x = x_hi * 2 + x_lo), y: 4, z: 8, core: 2. Of those that a mesh axis runs over, the one named last changes fastest.
Arguments:
- suffix_query: bfloat16 [8192, 5120], P('req', 'tp')
- suffix_key: bfloat16 [8192, 1024], P('req', 'tp')
- suffix_value: bfloat16 [8192, 1024], P('req', 'tp'), may hold values from -6 to 6
- prefix_key: bfloat16 [32, 1024, 1024], P('req', None, 'tp')
- prefix_value: bfloat16 [32, 1024, 1024], P('req', None, 'tp'), may hold values from -6 to 6
- residual: bfloat16 [8192, 5120], P('req'), may hold values from -6 to 6
- out_weight: bfloat16 [5120, 5120], P('tp'), may hold values from -0.15625 to 0.15625
- norm_gain: bfloat16 [5120], P('tp'), may hold values from 0.099609375 to 1.8984375
- lengths: int32 [32], replicated, may hold values from 1 to 256, 4915 in all
- request_slot: int32 [32], replicated, may hold values from 0 to 31, each once
- prefix_owner: int32 [32], replicated, may hold values from 0 to 31, each once
- request_group: int32 [32, 1], replicated, may hold values from 0 to 3
Outputs:
- hidden: bfloat16 [8192, 5120], P('req', 'tp')
- normed: bfloat16 [8192, 5120], P('req', 'tp')
- cache_key: bfloat16 [8192, 1024], P('req', 'tp')
Inputs may be any that keep to these rules, and one draw needn't show every extreme that they name: `request_slot`: a permutation. `prefix_owner`: a permutation. `request_group`: every group has one request or more. `lengths`: some request has all 256 slots live.
All inputs are finite; a program needn't handle non-finite values.
Results may differ from a plain program's by a relative error of at most 0.0067.
Values may be sent and summed in bfloat16 or wider, within the bound.
No kernel may reach another device: no remote copies, remote signals or barrier semaphores. Data moves between devices by JAX's collectives and lax.ppermute only.
A program may use at most 128 MiB of HBM per device.

v0:
```python
import jax
import jax.numpy as jnp
from jax import lax
from jax.experimental import pallas as pl
from jax.experimental.pallas import tpu as pltpu
from jax.sharding import PartitionSpec as P


HD = 128
GROUPS = 4
PLANE = 4
TILE = 128
THETA = 1000000.0
NEGATIVE = -1e30
EPSILON = 1e-06
LOG2E = 1.4426950408889634
PATHS = (6, 2, 4, 7, 5, 3, 1, 0)


SMEM = pltpu.SMEM
VMEM = pltpu.VMEM


def full(space=VMEM):
    return pl.BlockSpec(memory_space=space)


def params(limit=26):
    return pltpu.CompilerParams(vmem_limit_bytes=limit * 1024 * 1024)


RATE = HD ** (-0.5) * LOG2E
NT = (((1,), (1,)), ((), ()))


def turn(x, cosines, sines):
    return x * cosines + pltpu.roll(x, HD // 2, 1) * sines


def turn_tiles(q_in, q_ref, at, cosines, sines):
    for j in range(q_in.shape[0] // TILE):
        rows = slice(j * TILE, (j + 1) * TILE)
        for h in range(q_ref.shape[1] // TILE):
            x = q_in[rows, h * HD : (h + 1) * HD].astype(jnp.float32)
            q_ref[at + j, h * TILE : (h + 1) * TILE] = turn(x, cosines[rows], sines[rows]).astype(
                jnp.bfloat16
            )


def spans(width):
    return [(low, min(low + 2 * TILE, width)) for low in range(0, width, 2 * TILE)]


def own_kernel(meta, q_in, k_in, v_in, cos_in, sin_in, q_out, key_out, acc_ref, max_ref, sum_ref):
    tiles, lines = q_out.shape[:2]
    slots = k_in.shape[0]
    length = meta[0]
    cosines = cos_in[...]
    sines = sin_in[...]
    turn_tiles(q_in, q_out, 0, cosines, sines)
    turned = turn(k_in[...].astype(jnp.float32), cosines, sines)
    place = lax.broadcasted_iota(jnp.int32, turned.shape, 0)
    key_out[...] = jnp.where(place < length, turned, 0.0).astype(jnp.bfloat16)
    k = key_out[...]
    v = v_in[...].T
    u = lax.broadcasted_iota(jnp.int32, (slots, TILE), 0)
    t = lax.broadcasted_iota(jnp.int32, (slots, TILE), 1)
    for j in range(tiles):
        visible = (u <= t + j * TILE) & (u < length)
        for low in range(0, lines, TILE):
            high = low + TILE
            scores = lax.dot_general(
                k, q_out[j, low:high], NT, preferred_element_type=jnp.float32
            )
            scores = jnp.where(visible, scores, NEGATIVE)
            top = jnp.max(scores, axis=0, keepdims=True)
            weights = jnp.exp2((scores - top) * RATE)
            max_ref[j, :, low:high] = top
            sum_ref[j, :, low:high] = jnp.sum(weights, axis=0, keepdims=True)
            acc_ref[j, :, low:high] = jnp.dot(
                v, weights.astype(jnp.bfloat16), preferred_element_type=jnp.float32
            )


def visit(meta, base, count, q_ref, kv_ref, vt_ref, s_ref, p_ref, top_ref, keep_ref, acc_ref, max_ref, sum_ref, items):
    spare = q_ref.shape[0] - 1
    tiles = spare // PLANE
    part = kv_ref.shape[2]
    cuts = spans(q_ref.shape[1])
    for e in range(count):
        vt_ref[e, :HD] = kv_ref[e, 1].T
        vt_ref[e, HD:] = jnp.ones((16, part), jnp.bfloat16)
    for x in range(2):
        items[x, 0] = 0
        items[x, 1] = spare
    n = jnp.int32(2)
    for e in range(count):
        for i in range(PLANE):
            for j in range(tiles):
                live = (meta[2 * PLANE + (base + e) * PLANE + i] == 1) & (j < meta[PLANE + i])

                @pl.when(live)
                def _(n=n, e=e, i=i, j=j):
                    items[n, 0] = e
                    items[n, 1] = i * tiles + j

                n = n + live.astype(jnp.int32)
    for x in range(4):
        items[n + x, 0] = 0
        items[n + x, 1] = spare

    def score(step, slot):
        k = kv_ref[items[step, 0], 0]
        at = items[step, 1]
        for low, high in cuts:
            scores = lax.dot_general(
                k, q_ref[at, low:high], NT, preferred_element_type=jnp.float32
            )
            s_ref[slot, :, low:high] = scores
            top_ref[slot, :, low:high] = jnp.max(scores, axis=0, keepdims=True)

    def weigh(step, slot):
        at = items[step, 1]
        old = max_ref[at]
        new = jnp.maximum(old, top_ref[slot])
        max_ref[at] = new
        keep_ref[slot] = jnp.exp2((old - new) * RATE)
        for low, high in cuts:
            p_ref[slot, :, low:high] = jnp.exp2(
                (s_ref[slot, :, low:high] - new[:, low:high]) * RATE
            ).astype(jnp.bfloat16)

    def gather(step, slot):
        v = vt_ref[items[step, 0]]
        at = items[step, 1]
        for low, high in cuts:
            keep = keep_ref[slot, :, low:high]
            mixed = jnp.dot(v, p_ref[slot, :, low:high], preferred_element_type=jnp.float32)
            acc_ref[at, :, low:high] = acc_ref[at, :, low:high] * keep + mixed[:HD]
            sum_ref[at, :, low:high] = sum_ref[at, :, low:high] * keep + mixed[HD : HD + 1]

    @pl.when(n > 2)
    def _():
        def body(t, carry):
            for x in range(2):
                step = 2 * t + x
                gather(step, x)
                weigh(step + 1, 1 - x)
                score(step + 2, x)
            return carry

        lax.fori_loop(0, (n + 1) // 2, body, 0)


def fetch(pairs, sems):
    copies = [
        pltpu.make_async_copy(source, target, sems.at[n])
        for n, (source, target) in enumerate(pairs)
    ]
    for copy in copies:
        copy.start()
    return copies


def make_first(base, count):
    def kernel(meta, q_own, acc_own, max_own, sum_own, q1, q2, q3, cos_in, sin_in, *rest):
        kv_in = rest[:count]
        q_ref, acc_ref, max_ref, sum_ref, sems, kv_ref, vt_ref, s_ref, p_ref, top_ref, keep_ref, items = rest[count:]
        copies = fetch([(kv, kv_ref.at[e]) for e, kv in enumerate(kv_in)], sems)
        tiles = q_own.shape[0]
        acc_ref[tiles:] = jnp.zeros_like(acc_ref[tiles:])
        max_ref[tiles:] = jnp.full_like(max_ref[tiles:], NEGATIVE)
        sum_ref[tiles:] = jnp.zeros_like(sum_ref[tiles:])
        q_ref[:tiles] = q_own[...]
        q_ref[PLANE * tiles] = q_own[0]
        acc_ref[:tiles] = acc_own[...]
        max_ref[:tiles] = max_own[...]
        sum_ref[:tiles] = sum_own[...]
        cosines = cos_in[...]
        sines = sin_in[...]
        for i, q_in in enumerate((q1, q2, q3)):
            turn_tiles(q_in, q_ref, (i + 1) * tiles, cosines, sines)
        for copy in copies:
            copy.wait()
        visit(meta, base, count, q_ref, kv_ref, vt_ref, s_ref, p_ref, top_ref, keep_ref, acc_ref, max_ref, sum_ref, items)

    return kernel


def make_middle(base, count):
    def kernel(meta, q_ref, acc_in, max_in, sum_in, *rest):
        kv_in = rest[:count]
        acc_ref, max_ref, sum_ref, sems, kv_ref, vt_ref, s_ref, p_ref, top_ref, keep_ref, items = rest[count:]
        pairs = [(kv, kv_ref.at[e]) for e, kv in enumerate(kv_in)]
        copies = fetch(pairs + [(acc_in, acc_ref)], sems)
        max_ref[...] = max_in[...]
        sum_ref[...] = sum_in[...]
        for copy in copies:
            copy.wait()
        visit(meta, base, count, q_ref, kv_ref, vt_ref, s_ref, p_ref, top_ref, keep_ref, acc_ref, max_ref, sum_ref, items)

    return kernel


def stack(maxima, sums):
    rows = []
    for line in (maxima, sums):
        heads = line.shape[1] // TILE
        rows += [line[:, h * TILE : (h + 1) * TILE] for h in range(heads)]
        rows.append(jnp.zeros((8 - heads, TILE), jnp.float32))
    return jnp.concatenate(rows, axis=0)


def pack(out, at, stats):
    high = stats.astype(jnp.bfloat16)
    left = stats - high.astype(jnp.float32)
    middle = left.astype(jnp.bfloat16)
    low = (left - middle.astype(jnp.float32)).astype(jnp.bfloat16)
    for n, piece in enumerate((high, middle, low)):
        out[at + 16 * n : at + 16 * (n + 1)] = piece


def unpack(part, at):
    pieces = [part[at + 16 * n : at + 16 * (n + 1)].astype(jnp.float32) for n in range(3)]
    stats = pieces[0] + pieces[1] + pieces[2]
    return stats[:8], stats[8:]


def safe(total):
    return jnp.where(total > 0, 1.0 / jnp.where(total > 0, total, 1.0), 0.0)


def make_last(base, count):
    def kernel(meta, q_ref, acc_in, max_in, sum_in, *rest):
        kv_in = rest[:count]
        tiles = (q_ref.shape[0] - 1) // PLANE
        outs = rest[count : count + 5 * tiles]
        acc_ref, max_ref, sum_ref, sems, kv_ref, vt_ref, s_ref, p_ref, top_ref, keep_ref, items = rest[count + 5 * tiles :]
        pairs = [(kv, kv_ref.at[e]) for e, kv in enumerate(kv_in)]
        copies = fetch(pairs + [(acc_in, acc_ref)], sems)
        max_ref[...] = max_in[...]
        sum_ref[...] = sum_in[...]
        for copy in copies:
            copy.wait()
        visit(meta, base, count, q_ref, kv_ref, vt_ref, s_ref, p_ref, top_ref, keep_ref, acc_ref, max_ref, sum_ref, items)
        heads = q_ref.shape[1] // TILE
        for j in range(tiles):
            acc_own, stats_own, acc_two, stats_two, swap = outs[5 * j : 5 * j + 5]
            acc_own[...] = acc_ref[j]
            stats_own[...] = stack(max_ref[j], sum_ref[j])
            two = 2 * tiles + j
            acc_two[...] = acc_ref[two]
            stats_two[...] = stack(max_ref[two], sum_ref[two])
            for slot, i in enumerate((1, 3)):
                at = i * tiles + j
                inverse = safe(sum_ref[at])
                for h in range(heads):
                    lanes = slice(h * TILE, (h + 1) * TILE)
                    swap[slot, h * HD : (h + 1) * HD] = (
                        acc_ref[at, :, lanes] * inverse[:, lanes]
                    ).astype(jnp.bfloat16)
                pack(swap.at[slot], heads * HD, stack(max_ref[at], sum_ref[at]))

    return kernel


def merge_kernel(acc_two, stats_two, swapped, out):
    heads = acc_two.shape[1] // TILE
    other = swapped.at[1]
    max_a, sum_a = stats_two[:8], stats_two[8:]
    max_b, sum_b = unpack(other, heads * HD)
    top = jnp.maximum(max_a, max_b)
    scale_a = jnp.exp2((max_a - top) * RATE)
    mass_b = sum_b * jnp.exp2((max_b - top) * RATE)
    total = sum_a * scale_a + mass_b
    inverse = safe(total)
    share_a = scale_a * inverse
    share_b = mass_b * inverse
    for h in range(heads):
        lanes = slice(h * TILE, (h + 1) * TILE)
        rows = slice(h * HD, (h + 1) * HD)
        value = acc_two[:, lanes] * share_a[h : h + 1]
        value = value + other[rows].astype(jnp.float32) * share_b[h : h + 1]
        out[rows] = value.astype(jnp.bfloat16)
    pack(out, heads * HD, jnp.concatenate([top, total], axis=0))


def make_combine(j):
    def kernel(meta, where, acc_own, stats_own, swapped, crossed, weight_in, *rest):
        ways = len(rest) - 3
        outs = rest[:ways]
        attn_ref, weight_ref, sems = rest[ways:]
        columns = weight_ref.shape[2]
        copies = []
        for k in range(ways):
            at = pl.multiple_of((where[0] ^ k) * columns, HD)
            copies.append(
                pltpu.make_async_copy(
                    weight_in.at[:, pl.ds(at, columns)], weight_ref.at[k], sems.at[k]
                )
            )
        for k in PATHS:
            copies[k].start()
        heads = acc_own.shape[1] // TILE
        parts = (swapped.at[0], crossed)
        maxima = [stats_own[:8]]
        sums = [stats_own[8:]]
        for part in parts:
            found = unpack(part, heads * HD)
            maxima.append(found[0])
            sums.append(found[1])
        top = jnp.maximum(jnp.maximum(maxima[0], maxima[1]), maxima[2])
        factor = [jnp.exp2((m - top) * RATE) for m in maxima]
        mass = [f * s for f, s in zip(factor, sums)]
        inverse = safe(mass[0] + mass[1] + mass[2])
        shares = [factor[0] * inverse] + [m * inverse for m in mass[1:]]
        live = lax.broadcasted_iota(jnp.int32, (HD, TILE), 1) + j * TILE < meta[0]
        for h in range(heads):
            lanes = slice(h * TILE, (h + 1) * TILE)
            value = acc_own[:, lanes] * shares[0][h : h + 1]
            for w, part in zip(shares[1:], parts):
                value = value + w[h : h + 1] * part[h * HD : (h + 1) * HD].astype(jnp.float32)
            value = jnp.transpose(jnp.where(live, value, 0.0))
            attn_ref[:, h * HD : (h + 1) * HD] = value.astype(jnp.bfloat16)
        for k in PATHS:
            copies[k].wait()
            outs[k][...] = jnp.dot(
                attn_ref[...], weight_ref[k], preferred_element_type=jnp.float32
            ).astype(outs[k].dtype)

    return kernel


def cost(blocks, bytes_accessed):
    pairs = blocks * 1280 * 512
    return pl.CostEstimate(
        flops=4 * pairs * HD, bytes_accessed=bytes_accessed, transcendentals=pairs
    )


def shards(
    suffix_query,
    suffix_key,
    suffix_value,
    prefix_key,
    prefix_value,
    residual,
    out_weight,
    norm_gain,
    lengths,
    request_slot,
    prefix_owner,
    request_group,
):
    slots = suffix_query.shape[0]
    heads = suffix_query.shape[1] // HD
    devices = lax.axis_size("req")
    planes = devices // PLANE
    place = lax.axis_index("req")
    tensor = lax.axis_index("tp")
    ways = lax.axis_size("tp")
    per_group = devices // GROUPS
    block = prefix_key.shape[1]
    part = block // 2
    prefix_length = block * per_group
    bf16 = jnp.bfloat16
    f32 = jnp.float32

    def beside(k):
        return [(i, i ^ k) for i in range(devices)]

    up_pairs = [(i, (i + PLANE) % devices) for i in range(devices)]
    down_pairs = [(i, (i - PLANE) % devices) for i in range(devices)]

    core = place % 2
    both = jnp.concatenate([prefix_key, prefix_value], axis=0)
    mine = lax.dynamic_slice_in_dim(both, core * part, part, 1)
    theirs = lax.dynamic_slice_in_dim(both, (1 - core) * part, part, 1)
    lanes = [mine, lax.ppermute(theirs, "req", beside(1))]
    queries = []
    for k in range(1, PLANE):
        queries.append(lax.ppermute(suffix_query, "req", beside(k)))

    entries = {(0, 0): lanes[0], (0, 1): lanes[1]}
    half_way = planes // 2
    for lane in range(2):
        moving_up = lanes[lane]
        moving_down = lanes[lane]
        for step in range(1, half_way):
            moving_up = lax.ppermute(moving_up, "req", up_pairs)
            moving_down = lax.ppermute(moving_down, "req", down_pairs)
            entries[(-step, lane)] = moving_up
            entries[(step, lane)] = moving_down
        if lane == 0:
            entries[(-half_way, 0)] = lax.ppermute(moving_up, "req", up_pairs)
        else:
            entries[(half_way, 1)] = lax.ppermute(moving_down, "req", down_pairs)

    batches = [
        [(0, 0), (0, 1), (-1, 0), (1, 0), (-1, 1), (1, 1)],
        [(-2, 0), (2, 0), (-2, 1), (2, 1)],
        [(-3, 0), (3, 0), (-3, 1), (3, 1)],
        [(-half_way, 0), (half_way, 1)],
    ]
    order = [key for batch in batches for key in batch]

    numbers = jnp.arange(devices, dtype=jnp.int32)
    owner_match = prefix_owner[None, :] == numbers[:, None]
    holder_group = jnp.sum(jnp.where(owner_match, numbers[None, :], 0), axis=1) // per_group
    slot_match = request_slot[:, None] == numbers[None, :]
    asker_group = jnp.sum(jnp.where(slot_match, request_group[:, 0][None, :], 0), axis=1)
    asker_length = jnp.sum(jnp.where(slot_match, lengths[None, :], 0), axis=1)
    nearby = place ^ jnp.arange(PLANE, dtype=jnp.int32)
    near = nearby[:, None] == numbers[None, :]
    near_group = jnp.sum(jnp.where(near, asker_group[None, :], 0), axis=1)
    near_length = jnp.sum(jnp.where(near, asker_length[None, :], 0), axis=1)
    shift = jnp.array([key[0] for key in order], jnp.int32)
    twist = jnp.array([key[1] for key in order], jnp.int32)
    source = ((place // PLANE + shift) % planes) * PLANE + ((place % PLANE) ^ twist)
    from_there = source[:, None] == numbers[None, :]
    source_group = jnp.sum(jnp.where(from_there, holder_group[None, :], 0), axis=1)
    match = (source_group[:, None] == near_group[None, :]).astype(jnp.int32)
    tiles = (near_length + TILE - 1) // TILE
    meta = jnp.concatenate([near_length, tiles, match.reshape(-1)])

    half_dim = HD // 2
    positions = (prefix_length + jnp.arange(slots)).astype(f32)
    frequency = THETA ** (-(jnp.arange(half_dim).astype(f32) * 2.0 / HD))
    angles = positions[:, None] * frequency[None, :]
    cosines = jnp.cos(angles)
    sines = jnp.sin(angles)
    cosines = jnp.concatenate([cosines, cosines], axis=1)
    sines = jnp.concatenate([-sines, sines], axis=1)

    tiles_each = slots // TILE
    shape = jax.ShapeDtypeStruct
    q_own, cache_key, acc_own, max_own, sum_own = pl.pallas_call(
        own_kernel,
        out_shape=(
            shape((tiles_each, heads * TILE, HD), bf16),
            shape((slots, HD), bf16),
            shape((tiles_each, HD, heads * TILE), f32),
        shape((tiles_each, 1, heads * TILE), f32),
        shape((tiles_each, 1, heads * TILE), f32),
    ),
        in_specs=[full(SMEM)] + [full()] * 5,
        out_specs=(full(),) * 5,
        cost_estimate=cost(1, 3 << 20),
        compiler_params=params(),
        name="own",
    )(meta, suffix_query, suffix_key, suffix_value, cosines, sines)

    every = PLANE * tiles_each + 1
    lines = heads * TILE
    state_shapes = (
        shape((every, HD, lines), f32),
        shape((every, 1, lines), f32),
        shape((every, 1, lines), f32),
    )

    def work(count):
        return [
            pltpu.SemaphoreType.DMA((count + 1,)),
            pltpu.VMEM((count, 2, part, HD), bf16),
            pltpu.VMEM((count, HD + 16, part), bf16),
            pltpu.VMEM((2, part, lines), f32),
            pltpu.VMEM((2, part, lines), bf16),
            pltpu.VMEM((2, 1, lines), f32),
            pltpu.VMEM((2, 1, lines), f32),
            pltpu.SMEM((count * PLANE * tiles_each + 6, 2), jnp.int32),
        ]

    base = 0
    parts = [entries[key] for key in batches[0]]
    q_all, *state = pl.pallas_call(
        make_first(base, len(parts)),
        out_shape=(shape((every, lines, HD), bf16),) + state_shapes,
        in_specs=[full(SMEM)] + [full()] * 9 + [full(pl.ANY)] * len(parts),
        out_specs=(full(),) * 4,
        scratch_shapes=work(len(parts)),
        cost_estimate=cost(len(parts), 8 << 20),
        compiler_params=params(),
        name="first",
    )(meta, q_own, acc_own, max_own, sum_own, *queries, cosines, sines, *parts)
    base += len(parts)
    for batch in batches[1:-1]:
        parts = [entries[key] for key in batch]
        state = pl.pallas_call(
            make_middle(base, len(parts)),
            out_shape=state_shapes,
            in_specs=[full(SMEM), full(), full(pl.ANY), full(), full()] + [full(pl.ANY)] * len(parts),
            out_specs=(full(),) * 3,
            scratch_shapes=work(len(parts)),
            cost_estimate=cost(len(parts), 8 << 20),
            compiler_params=params(),
            name="middle",
        )(meta, q_all, *state, *parts)
        base += len(parts)
    parts = [entries[key] for key in batches[-1]]
    packed = heads * HD + 3 * 16
    last = pl.pallas_call(
        make_last(base, len(parts)),
        out_shape=(
            shape((HD, lines), f32),
            shape((16, TILE), f32),
            shape((HD, lines), f32),
            shape((16, TILE), f32),
            shape((2, packed, TILE), bf16),
        )
        * tiles_each,
        in_specs=[full(SMEM), full(), full(pl.ANY), full(), full()] + [full(pl.ANY)] * len(parts),
        out_specs=(full(),) * (5 * tiles_each),
        scratch_shapes=[
            pltpu.VMEM((every, HD, lines), f32),
            pltpu.VMEM((every, 1, lines), f32),
            pltpu.VMEM((every, 1, lines), f32),
        ]
        + work(len(parts)),
        cost_estimate=cost(len(parts), 8 << 20),
        compiler_params=params(),
        name="last",
    )(meta, q_all, *state, *parts)

    width = residual.shape[1]
    columns = width // ways
    where = tensor.astype(jnp.int32).reshape(1)
    swapped = []
    for j in range(tiles_each):
        swapped.append(lax.ppermute(last[5 * j + 4], "req", beside(1)))
    crossed = []
    for j in range(tiles_each):
        merged = pl.pallas_call(
            merge_kernel,
            out_shape=shape((packed, TILE), bf16),
            in_specs=[full()] * 3,
            out_specs=full(),
            cost_estimate=pl.CostEstimate(flops=1 << 20, bytes_accessed=1 << 20, transcendentals=0),
            compiler_params=params(),
            name="merge",
        )(last[5 * j + 2], last[5 * j + 3], swapped[j])
        crossed.append(lax.ppermute(merged, "req", beside(2)))
    shared = []
    for j in range(tiles_each):
        pieces = pl.pallas_call(
            make_combine(j),
            out_shape=tuple(
                shape((TILE, columns), bf16 if k else f32) for k in range(ways)
            ),
            in_specs=[full(SMEM)] * 2 + [full()] * 4 + [full(pl.ANY)],
            out_specs=(full(),) * ways,
            scratch_shapes=[
                pltpu.VMEM((TILE, heads * HD), bf16),
                pltpu.VMEM((ways, heads * HD, columns), bf16),
                pltpu.SemaphoreType.DMA((ways,)),
            ],
            cost_estimate=pl.CostEstimate(
                flops=2 * TILE * heads * HD * width,
                bytes_accessed=8 << 20,
                transcendentals=0,
            ),
            compiler_params=params(50),
            name="combine",
        )(meta, where, last[5 * j], last[5 * j + 1], swapped[j], crossed[j], out_weight)
        total = pieces[0]
        for k in range(1, ways):
            piece = lax.ppermute(pieces[k], "tp", [(i, i ^ k) for i in range(ways)])
            total = total + piece.astype(f32)
        shared.append(total)
    shared = jnp.concatenate(shared, axis=0)
    own_residual = lax.dynamic_slice_in_dim(residual, tensor * columns, columns, 1)
    hidden = (own_residual.astype(f32) + shared).astype(bf16)
    widened = hidden.astype(f32)
    squares = jnp.sum(widened * widened, axis=1).reshape(slots // HD, HD)
    squares = jnp.pad(squares, ((0, 8 - slots // HD), (0, 0)))
    spread = lax.all_to_all(jnp.broadcast_to(squares[None], (ways, 8, HD)), "tp", 0, 0)
    row_squares = jnp.sum(spread, axis=0)[: slots // HD].reshape(slots)
    scale_rows = lax.rsqrt(row_squares / width + EPSILON)
    normed = (widened * scale_rows[:, None] * norm_gain.astype(f32)[None, :]).astype(bf16)
    return (hidden, normed, cache_key)


def solution(mesh):
    return jax.shard_map(
        shards,
        mesh=mesh,
        in_specs=(
            P("req", "tp"),
            P("req", "tp"),
            P("req", "tp"),
            P("req", None, "tp"),
            P("req", None, "tp"),
            P("req", None),
            P("tp", None),
            P("tp"),
            P(),
            P(),
            P(),
            P(),
        ),
        out_specs=(P("req", "tp"), P("req", "tp"), P("req", "tp")),
        check_vma=False,
    )
```

profile of v0, /device:TPU:2, one launch (start us, length us, event | category | flops | bytes accessed | tf_op | source)
XLA Modules:
  0.0 143.2 jit_solution(623307427932578921)
XLA Ops:
  0.7 1.0 constant_dynamic-update-slice_fusion.1
  1.7 1.0 constant_dynamic-update-slice_fusion
  2.7 2.0 %collective-permute-start.4 = (bf16[2,512,128]{2,1,0:T(8,128)(2,1)S(1)}, bf16[2,512,128]{2,1,0:T(8,128)(2,1)S(1)}, u32[]{:S(2)}, u32[]{:S(2)}) collective-permute-start(bf16[2,512,128]{2,1,0:T(8,128)(2,1)S(1)} %get-tuple-element.92.rest_0_), channel_id=1, source_target_pairs={{0,32},{8,40},{16,48},{24,56},{32,64},{40,72},{48,80},{56,88},{64,... | collective-permute-start | bytes 786440 | tf_op jit(solution)/shard_map/ppermute | solution.py:390
  4.7 4.0 %collective-permute-start.5 = (bf16[2,512,128]{2,1,0:T(8,128)(2,1)S(1)}, bf16[2,512,128]{2,1,0:T(8,128)(2,1)S(1)}, u32[]{:S(2)}, u32[]{:S(2)}) collective-permute-start(bf16[2,512,128]{2,1,0:T(8,128)(2,1)S(1)} %get-tuple-element.92.rest_0_), channel_id=1, source_target_pairs={{0,224},{8,232},{16,240},{24,248},{32,0},{40,8},{48,16},{56,24},{6... | collective-permute-start | bytes 786440 | tf_op jit(solution)/shard_map/ppermute | solution.py:391
  8.8 0.5 collective-permute-start.1
  9.3 0.2 collective-permute-start.3
  9.5 0.8 select_reduce_fusion.1
  10.3 0.9 select_reduce_fusion.2
  11.2 0.7 fusion.7
  11.9 1.3 fusion.4
  13.2 1.9 %collective-permute-start.7 = (bf16[2,512,128]{2,1,0:T(8,128)(2,1)S(1)}, bf16[2,512,128]{2,1,0:T(8,128)(2,1)S(1)}, u32[]{:S(2)}, u32[]{:S(2)}) collective-permute-start(bf16[2,512,128]{2,1,0:T(8,128)(2,1)S(1)} %collective-permute-done.3.rest_1_), channel_id=1, source_target_pairs={{0,224},{8,232},{16,240},{24,248},{32,0},{40,8},{48,16},{56,24},{6... | collective-permute-start | bytes 786440 | tf_op jit(solution)/shard_map/ppermute | solution.py:391
  15.1 0.2 select_reduce_fusion.5
  15.3 0.2 select_reduce_fusion.3
  15.8 5.9 %collective-permute-done.7.rest_5_ = bf16[2,512,128]{2,1,0:T(8,128)(2,1)S(1)} collective-permute-done((bf16[2,512,128]{2,1,0:T(8,128)(2,1)S(1)}, bf16[2,512,128]{2,1,0:T(8,128)(2,1)S(1)}, u32[]{:S(2)}, u32[]{:S(2)}) %collective-permute-start.7) | collective-permute-done | bytes 262176 | tf_op jit(solution)/shard_map/ppermute | solution.py:391
  21.7 3.1 %collective-permute-start.11 = (bf16[2,512,128]{2,1,0:T(8,128)(2,1)S(1)}, bf16[2,512,128]{2,1,0:T(8,128)(2,1)S(1)}, u32[]{:S(2)}, u32[]{:S(2)}) collective-permute-start(bf16[2,512,128]{2,1,0:T(8,128)(2,1)S(1)} %collective-permute-done.7.rest_5_), channel_id=1, source_target_pairs={{0,224},{8,232},{16,240},{24,248},{32,0},{40,8},{48,16},{56,24},{6... | collective-permute-start | bytes 786440 | tf_op jit(solution)/shard_map/ppermute | solution.py:391
  24.9 0.3 collective-permute-start.2
  25.3 0.4 collective-permute-start.9
  25.6 0.3 collective-permute-done.6.rest_4_
  26.0 1.4 collective-permute-start.10
  27.4 3.2 %collective-permute-done.8.rest_0_ = bf16[2,512,128]{2,1,0:T(8,128)(2,1)S(1)} collective-permute-done((bf16[2,512,128]{2,1,0:T(8,128)(2,1)S(1)}, bf16[2,512,128]{2,1,0:T(8,128)(2,1)S(1)}, u32[]{:S(2)}, u32[]{:S(2)}) %collective-permute-start.8) | collective-permute-done | bytes 262176 | tf_op jit(solution)/shard_map/ppermute | solution.py:390
  30.6 0.9 collective-permute-done.11.rest_3_
  31.5 3.7 %collective-permute-start.15 = (bf16[2,512,128]{2,1,0:T(8,128)(2,1)S(1)}, bf16[2,512,128]{2,1,0:T(8,128)(2,1)S(1)}, u32[]{:S(2)}, u32[]{:S(2)}) collective-permute-start(bf16[2,512,128]{2,1,0:T(8,128)(2,1)S(1)} %collective-permute-done.11.rest_3_), channel_id=1, source_target_pairs={{0,224},{8,232},{16,240},{24,248},{32,0},{40,8},{48,16},{56,24},{6... | collective-permute-start | bytes 786440 | tf_op jit(solution)/shard_map/ppermute | solution.py:391
  35.3 1.2 pad_maximum_fusion
  36.6 0.8 copy-done.2
  37.4 1.5 %own.1 = (bf16[2,640,128]{2,1,0:T(8,128)(2,1)S(1)}, bf16[256,128]{1,0:T(8,128)(2,1)}, f32[2,128,640]{2,1,0:T(8,128)S(1)}, f32[2,1,640]{2,1,0:T(1,128)S(1)}, f32[2,1,640]{2,1,0:T(1,128)S(1)}) custom-call(s32[72]{0:T(128)S(1)} %pad_add_fusion.meta, bf16[256,640]{1,0:T(8,128)(2,1)S(1)} %copy-done, bf16[256,128]{1,0:T(8,128)(2,1)S(1)} %copy-done.1, ...), custom_call_target="tpu_custom_call" | custom-call | flops 335544320 | bytes 3145728 | tf_op jit(solution)/shard_map/own/pallas_call | solution.py:437
  38.9 1.9 %collective-permute-start.13 = (bf16[2,512,128]{2,1,0:T(8,128)(2,1)S(1)}, bf16[2,512,128]{2,1,0:T(8,128)(2,1)S(1)}, u32[]{:S(2)}, u32[]{:S(2)}) collective-permute-start(bf16[2,512,128]{2,1,0:T(8,128)(2,1)S(1)} %collective-permute-done.9.rest_1_), channel_id=1, source_target_pairs={{0,224},{8,232},{16,240},{24,248},{32,0},{40,8},{48,16},{56,24},{6... | collective-permute-start | bytes 786440 | tf_op jit(solution)/shard_map/ppermute | solution.py:391
  40.8 0.4 collective-permute-start.14
  41.2 0.8 collective-permute-done.12.rest_0_
  42.1 0.7 collective-permute-done.15.rest_3_
  42.8 3.7 %collective-permute-start.17 = (bf16[2,512,128]{2,1,0:T(8,128)(2,1)S(1)}, bf16[2,512,128]{2,1,0:T(8,128)(2,1)S(1)}, u32[]{:S(2)}, u32[]{:S(2)}) collective-permute-start(bf16[2,512,128]{2,1,0:T(8,128)(2,1)S(1)} %collective-permute-done.15.rest_3_), channel_id=1, source_target_pairs={{0,224},{8,232},{16,240},{24,248},{32,0},{40,8},{48,16},{56,24},{6... | collective-permute-start | bytes 786440 | tf_op jit(solution)/shard_map/ppermute | solution.py:397
  46.4 12.2 %first.1 = (bf16[9,640,128]{2,1,0:T(8,128)(2,1)S(1)}, f32[9,128,640]{2,1,0:T(8,128)S(1)}, f32[9,1,640]{2,1,0:T(1,128)S(1)}, f32[9,1,640]{2,1,0:T(1,128)S(1)}) custom-call(s32[72]{0:T(128)S(1)} %pad_add_fusion.meta, bf16[2,640,128]{2,1,0:T(8,128)(2,1)S(1)} %get-tuple-element.44.q_own, f32[2,128,640]{2,1,0:T(8,128)S(1)} %get-tuple-element.45.acc_own, ...), custom_call_target="tpu_custom_call" | custom-call | flops 2013265920 | bytes 8388608 | tf_op jit(solution)/shard_map/first/pallas_call | solution.py:475
  58.7 5.0 %middle.2 = (f32[9,128,640]{2,1,0:T(8,128)S(1)}, f32[9,1,640]{2,1,0:T(1,128)S(1)}, f32[9,1,640]{2,1,0:T(1,128)S(1)}) custom-call(s32[72]{0:T(128)S(1)} %pad_add_fusion.meta, bf16[9,640,128]{2,1,0:T(8,128)(2,1)S(1)} %get-tuple-element.48.q_ref, f32[9,128,640]{2,1,0:T(8,128)S(1)} %get-tuple-element.49.acc_in, f32[9,1,640]{2,1,0:T(1,128)S(1)} %get-tuple-element.50.max_in, ...), custom_call_target="tpu_custom_call" | custom-call | flops 1342177280 | bytes 8388608 | tf_op jit(solution)/shard_map/middle/pallas_call | solution.py:488
  63.7 5.0 %middle.3 = (f32[9,128,640]{2,1,0:T(8,128)S(1)}, f32[9,1,640]{2,1,0:T(1,128)S(1)}, f32[9,1,640]{2,1,0:T(1,128)S(1)}) custom-call(s32[72]{0:T(128)S(1)} %pad_add_fusion.meta, bf16[9,640,128]{2,1,0:T(8,128)(2,1)S(1)} %get-tuple-element.48.q_ref, f32[9,128,640]{2,1,0:T(8,128)S(1)} %get-tuple-element.52.acc_in, f32[9,1,640]{2,1,0:T(1,128)S(1)} %get-tuple-element.53.max_in, ...), custom_call_target="tpu_custom_call" | custom-call | flops 1342177280 | bytes 8388608 | tf_op jit(solution)/shard_map/middle/pallas_call | solution.py:488
  68.8 3.2 %last.1 = (f32[128,640]{1,0:T(8,128)S(1)}, f32[16,128]{1,0:T(8,128)S(1)}, f32[128,640]{1,0:T(8,128)S(1)}, f32[16,128]{1,0:T(8,128)S(1)}, bf16[2,688,128]{2,1,0:T...) custom-call(s32[72]{0:T(128)S(1)} %pad_add_fusion.meta, ...), custom_call_target="tpu_custom_call" | custom-call | flops 671088640 | bytes 8388608 | tf_op jit(solution)/shard_map/last/pallas_call | solution.py:501
  72.0 0.5 collective-permute-start.27
  72.5 1.2 collective-permute-done.18.swapped
  73.9 0.3 collective-permute-done.27.swapped
  74.3 2.0 %collective-permute-start.28 = (bf16[688,128]{1,0:T(8,128)(2,1)S(1)}, bf16[688,128]{1,0:T(8,128)(2,1)S(1)}, u32[]{:S(2)}, u32[]{:S(2)}) collective-permute-start(bf16[688,128]{1,0:T(8,128)(2,1)S(1)} %merge.3), channel_id=1, source_target_pairs={{0,16},{8,24},{16,0},{24,8},{32,48},{40,56},{48,32},{56,40},{64,80... | collective-permute-start | bytes 528392 | tf_op jit(solution)/shard_map/ppermute | solution.py:541
  76.3 4.9 %collective-permute-done.19.crossed = bf16[688,128]{1,0:T(8,128)(2,1)S(1)} collective-permute-done((bf16[688,128]{1,0:T(8,128)(2,1)S(1)}, bf16[688,128]{1,0:T(8,128)(2,1)S(1)}, u32[]{:S(2)}, u32[]{:S(2)}) %collective-permute-start.19) | collective-permute-done | bytes 176160 | tf_op jit(solution)/shard_map/ppermute | solution.py:541
  81.2 4.4 %combine.2 = (f32[128,640]{1,0:T(8,128)S(1)}, bf16[128,640]{1,0:T(8,128)(2,1)S(1)}, bf16[128,640]{1,0:T(8,128)(2,1)S(1)}, bf16[128,640]{1,0:T(8,128)(2,1)S(1)}, ...) custom-call(s32[72]{0:T(128)S(1)} %pad_add_fusion.meta, ...), custom_call_target="tpu_custom_call" | custom-call | flops 838860800 | bytes 8388608 | tf_op jit(solution)/shard_map/combine/pallas_call | solution.py:544
  85.6 1.7 %collective-permute-start.20 = (bf16[128,640]{1,0:T(8,128)(2,1)S(1)}, bf16[128,640]{1,0:T(8,128)(2,1)S(1)}, u32[]{:S(2)}, u32[]{:S(2)}) collective-permute-start(bf16[128,640]{1,0:T(8,128)(2,1)S(1)} %get-tuple-element.64), channel_id=1, source_target_pairs={{0,1},{1,0},{2,3},{3,2},{4,5},{5,4},{6,7},{7,6},{8,9},{9,8},{10,11... | collective-permute-start | bytes 491528 | tf_op jit(solution)/shard_map/ppermute | solution.py:566
  87.3 2.9 %collective-permute-start.21 = (bf16[128,640]{1,0:T(8,128)(2,1)S(1)}, bf16[128,640]{1,0:T(8,128)(2,1)S(1)}, u32[]{:S(2)}, u32[]{:S(2)}) collective-permute-start(bf16[128,640]{1,0:T(8,128)(2,1)S(1)} %get-tuple-element.65), channel_id=1, source_target_pairs={{0,2},{1,3},{2,0},{3,1},{4,6},{5,7},{6,4},{7,5},{8,10},{9,11},{10,... | collective-permute-start | bytes 491528 | tf_op jit(solution)/shard_map/ppermute | solution.py:566
  90.2 0.2 collective-permute-start.22
  90.4 2.5 %collective-permute-start.23 = (bf16[128,640]{1,0:T(8,128)(2,1)S(1)}, bf16[128,640]{1,0:T(8,128)(2,1)S(1)}, u32[]{:S(2)}, u32[]{:S(2)}) collective-permute-start(bf16[128,640]{1,0:T(8,128)(2,1)S(1)} %get-tuple-element.67), channel_id=1, source_target_pairs={{0,4},{1,5},{2,6},{3,7},{4,0},{5,1},{6,2},{7,3},{8,12},{9,13},{10,... | collective-permute-start | bytes 491528 | tf_op jit(solution)/shard_map/ppermute | solution.py:566
  92.9 0.9 collective-permute-start.24
  93.8 4.4 %combine.3 = (f32[128,640]{1,0:T(8,128)S(1)}, bf16[128,640]{1,0:T(8,128)(2,1)S(1)}, bf16[128,640]{1,0:T(8,128)(2,1)S(1)}, bf16[128,640]{1,0:T(8,128)(2,1)S(1)}, ...) custom-call(s32[72]{0:T(128)S(1)} %pad_add_fusion.meta, ...), custom_call_target="tpu_custom_call" | custom-call | flops 838860800 | bytes 8388608 | tf_op jit(solution)/shard_map/combine/pallas_call | solution.py:544
  98.3 6.0 %collective-permute-start.25 = (bf16[128,640]{1,0:T(8,128)(2,1)S(1)}, bf16[128,640]{1,0:T(8,128)(2,1)S(1)}, u32[]{:S(2)}, u32[]{:S(2)}) collective-permute-start(bf16[128,640]{1,0:T(8,128)(2,1)S(1)} %get-tuple-element.69), channel_id=1, source_target_pairs={{0,6},{1,7},{2,4},{3,5},{4,2},{5,3},{6,0},{7,1},{8,14},{9,15},{10,... | collective-permute-start | bytes 491528 | tf_op jit(solution)/shard_map/ppermute | solution.py:566
  104.3 0.8 collective-permute-start.26
  105.1 0.7 copy-done.4
  105.7 4.5 %collective-permute-start.30 = (bf16[128,640]{1,0:T(8,128)(2,1)S(1)}, bf16[128,640]{1,0:T(8,128)(2,1)S(1)}, u32[]{:S(2)}, u32[]{:S(2)}) collective-permute-start(bf16[128,640]{1,0:T(8,128)(2,1)S(1)} %get-tuple-element.78), channel_id=1, source_target_pairs={{0,2},{1,3},{2,0},{3,1},{4,6},{5,7},{6,4},{7,5},{8,10},{9,11},{10,... | collective-permute-start | bytes 491528 | tf_op jit(solution)/shard_map/ppermute | solution.py:566
  110.2 0.2 collective-permute-start.31
  110.4 2.5 %collective-permute-start.32 = (bf16[128,640]{1,0:T(8,128)(2,1)S(1)}, bf16[128,640]{1,0:T(8,128)(2,1)S(1)}, u32[]{:S(2)}, u32[]{:S(2)}) collective-permute-start(bf16[128,640]{1,0:T(8,128)(2,1)S(1)} %get-tuple-element.80), channel_id=1, source_target_pairs={{0,4},{1,5},{2,6},{3,7},{4,0},{5,1},{6,2},{7,3},{8,12},{9,13},{10,... | collective-permute-start | bytes 491528 | tf_op jit(solution)/shard_map/ppermute | solution.py:566
  112.9 1.2 collective-permute-done.26
  114.3 5.5 %collective-permute-start.34 = (bf16[128,640]{1,0:T(8,128)(2,1)S(1)}, bf16[128,640]{1,0:T(8,128)(2,1)S(1)}, u32[]{:S(2)}, u32[]{:S(2)}) collective-permute-start(bf16[128,640]{1,0:T(8,128)(2,1)S(1)} %get-tuple-element.82), channel_id=1, source_target_pairs={{0,6},{1,7},{2,4},{3,5},{4,2},{5,3},{6,0},{7,1},{8,14},{9,15},{10,... | collective-permute-start | bytes 491528 | tf_op jit(solution)/shard_map/ppermute | solution.py:566
  119.8 2.1 %collective-permute-start.35 = (bf16[128,640]{1,0:T(8,128)(2,1)S(1)}, bf16[128,640]{1,0:T(8,128)(2,1)S(1)}, u32[]{:S(2)}, u32[]{:S(2)}) collective-permute-start(bf16[128,640]{1,0:T(8,128)(2,1)S(1)} %get-tuple-element.83), channel_id=1, source_target_pairs={{0,7},{1,6},{2,5},{3,4},{4,3},{5,2},{6,1},{7,0},{8,15},{9,14},{10,... | collective-permute-start | bytes 491528 | tf_op jit(solution)/shard_map/ppermute | solution.py:566
  121.9 1.3 convert_add_fusion.1
  123.2 0.4 collective-permute-done.33
  123.6 3.1 %collective-permute-done.34 = bf16[128,640]{1,0:T(8,128)(2,1)S(1)} collective-permute-done((bf16[128,640]{1,0:T(8,128)(2,1)S(1)}, bf16[128,640]{1,0:T(8,128)(2,1)S(1)}, u32[]{:S(2)}, u32[]{:S(2)}) %collective-permute-start.34) | collective-permute-done | bytes 163872 | tf_op jit(solution)/shard_map/ppermute | solution.py:566
  126.7 2.0 %collective-permute-done.35 = bf16[128,640]{1,0:T(8,128)(2,1)S(1)} collective-permute-done((bf16[128,640]{1,0:T(8,128)(2,1)S(1)}, bf16[128,640]{1,0:T(8,128)(2,1)S(1)}, u32[]{:S(2)}, u32[]{:S(2)}) %collective-permute-start.35) | collective-permute-done | bytes 163872 | tf_op jit(solution)/shard_map/ppermute | solution.py:566
  128.8 1.2 fusion
  130.0 0.7 broadcast_in_dim.88
  130.7 3.9 %all-to-all-start = ((f32[8,8,128]{2,1,0:T(8,128)}), f32[8,8,128]{2,1,0:T(8,128)S(1)}, u32[]{:S(2)}, u32[]{:S(2)}) async-start(f32[8,8,128]{2,1,0:T(8,128)} %broadcast_in_dim.88), calls=%async_computation | async-start | bytes 65536 | tf_op jit(solution)/shard_map/all_to_all | solution.py:575
  134.6 7.7 %all-to-all-done = f32[8,8,128]{2,1,0:T(8,128)S(1)} async-done(((f32[8,8,128]{2,1,0:T(8,128)}), f32[8,8,128]{2,1,0:T(8,128)S(1)}, u32[]{:S(2)}, u32[]{:S(2)}) %all-to-all-start) | async-done | bytes 32800 | tf_op jit(solution)/shard_map/all_to_all | solution.py:575
  142.4 0.9 fusion.2
  (60 shorter events, 1.4 us)
Async XLA Ops:
  0.6 35.9 %copy-start = (bf16[256,640]{1,0:T(8,128)(2,1)S(1)}, bf16[256,640]{1,0:T(8,128)(2,1)}, u32[]{:S(2)}) copy-start(bf16[256,640]{1,0:T(8,128)(2,1)} %q_in.1) | copy-start | bytes 983044
  0.6 35.9 %copy-start.1 = (bf16[256,128]{1,0:T(8,128)(2,1)S(1)}, bf16[256,128]{1,0:T(8,128)(2,1)}, u32[]{:S(2)}) copy-start(bf16[256,128]{1,0:T(8,128)(2,1)} %k_in.1) | copy-start | bytes 196612
  2.7 12.7 %collective-permute-start.4 = (bf16[2,512,128]{2,1,0:T(8,128)(2,1)S(1)}, bf16[2,512,128]{2,1,0:T(8,128)(2,1)S(1)}, u32[]{:S(2)}, u32[]{:S(2)}) collective-permute-start(bf16[2,512,128]{2,1,0:T(8,128)(2,1)S(1)} %get-tuple-element.92.rest_0_), channel_id=1, source_target_pairs={{0,32},{8,40},{16,48},{24,56},{32,64},{40,72},{48,80},{56,88},{64,... | collective-permute-start | bytes 786440 | tf_op jit(solution)/shard_map/ppermute | solution.py:390
  4.7 10.9 %collective-permute-start.5 = (bf16[2,512,128]{2,1,0:T(8,128)(2,1)S(1)}, bf16[2,512,128]{2,1,0:T(8,128)(2,1)S(1)}, u32[]{:S(2)}, u32[]{:S(2)}) collective-permute-start(bf16[2,512,128]{2,1,0:T(8,128)(2,1)S(1)} %get-tuple-element.92.rest_0_), channel_id=1, source_target_pairs={{0,224},{8,232},{16,240},{24,248},{32,0},{40,8},{48,16},{56,24},{6... | collective-permute-start | bytes 786440 | tf_op jit(solution)/shard_map/ppermute | solution.py:391
  8.8 16.1 %collective-permute-start = (bf16[256,640]{1,0:T(8,128)(2,1)}, bf16[256,640]{1,0:T(8,128)(2,1)S(1)}, u32[]{:S(2)}, u32[]{:S(2)}) collective-permute-start(bf16[256,640]{1,0:T(8,128)(2,1)} %q_in.1), channel_id=1, source_target_pairs={{0,8},{8,0},{16,24},{24,16},{32,40},{40,32},{48,56},{56,48},{64,72... | collective-permute-start | bytes 983048 | tf_op jit(solution)/shard_map/ppermute | solution.py:382
  8.8 16.5 %collective-permute-start.1 = (bf16[256,640]{1,0:T(8,128)(2,1)}, bf16[256,640]{1,0:T(8,128)(2,1)S(1)}, u32[]{:S(2)}, u32[]{:S(2)}) collective-permute-start(bf16[256,640]{1,0:T(8,128)(2,1)} %q_in.1), channel_id=1, source_target_pairs={{0,16},{8,24},{16,0},{24,8},{32,48},{40,56},{48,32},{56,40},{64,80... | collective-permute-start | bytes 983048 | tf_op jit(solution)/shard_map/ppermute | solution.py:382
  9.3 3.9 %collective-permute-start.3 = (bf16[2,512,128]{2,1,0:T(8,128)(2,1)S(1)}, bf16[2,512,128]{2,1,0:T(8,128)(2,1)S(1)}, u32[]{:S(2)}, u32[]{:S(2)}) collective-permute-start(bf16[2,512,128]{2,1,0:T(8,128)(2,1)S(1)} %get-tuple-element.91), channel_id=1, source_target_pairs={{0,8},{8,0},{16,24},{24,16},{32,40},{40,32},{48,56},{56,48},{64,72... | collective-permute-start | bytes 786440 | tf_op jit(solution)/shard_map/ppermute | solution.py:379
  13.2 8.5 %collective-permute-start.7 = (bf16[2,512,128]{2,1,0:T(8,128)(2,1)S(1)}, bf16[2,512,128]{2,1,0:T(8,128)(2,1)S(1)}, u32[]{:S(2)}, u32[]{:S(2)}) collective-permute-start(bf16[2,512,128]{2,1,0:T(8,128)(2,1)S(1)} %collective-permute-done.3.rest_1_), channel_id=1, source_target_pairs={{0,224},{8,232},{16,240},{24,248},{32,0},{40,8},{48,16},{56,24},{6... | collective-permute-start | bytes 786440 | tf_op jit(solution)/shard_map/ppermute | solution.py:391
  15.5 10.5 %collective-permute-start.6 = (bf16[2,512,128]{2,1,0:T(8,128)(2,1)S(1)}, bf16[2,512,128]{2,1,0:T(8,128)(2,1)S(1)}, u32[]{:S(2)}, u32[]{:S(2)}) collective-permute-start(bf16[2,512,128]{2,1,0:T(8,128)(2,1)S(1)} %collective-permute-done.3.rest_1_), channel_id=1, source_target_pairs={{0,32},{8,40},{16,48},{24,56},{32,64},{40,72},{48,80},{56,88},{64,... | collective-permute-start | bytes 786440 | tf_op jit(solution)/shard_map/ppermute | solution.py:390
  15.7 14.9 %collective-permute-start.8 = (bf16[2,512,128]{2,1,0:T(8,128)(2,1)S(1)}, bf16[2,512,128]{2,1,0:T(8,128)(2,1)S(1)}, u32[]{:S(2)}, u32[]{:S(2)}) collective-permute-start(bf16[2,512,128]{2,1,0:T(8,128)(2,1)S(1)} %collective-permute-done.4.rest_2_), channel_id=1, source_target_pairs={{0,32},{8,40},{16,48},{24,56},{32,64},{40,72},{48,80},{56,88},{64,... | collective-permute-start | bytes 786440 | tf_op jit(solution)/shard_map/ppermute | solution.py:390
  21.7 9.8 %collective-permute-start.11 = (bf16[2,512,128]{2,1,0:T(8,128)(2,1)S(1)}, bf16[2,512,128]{2,1,0:T(8,128)(2,1)S(1)}, u32[]{:S(2)}, u32[]{:S(2)}) collective-permute-start(bf16[2,512,128]{2,1,0:T(8,128)(2,1)S(1)} %collective-permute-done.7.rest_5_), channel_id=1, source_target_pairs={{0,224},{8,232},{16,240},{24,248},{32,0},{40,8},{48,16},{56,24},{6... | collective-permute-start | bytes 786440 | tf_op jit(solution)/shard_map/ppermute | solution.py:391
  24.9 21.6 %collective-permute-start.2 = (bf16[256,640]{1,0:T(8,128)(2,1)}, bf16[256,640]{1,0:T(8,128)(2,1)S(1)}, u32[]{:S(2)}, u32[]{:S(2)}) collective-permute-start(bf16[256,640]{1,0:T(8,128)(2,1)} %q_in.1), channel_id=1, source_target_pairs={{0,24},{8,16},{16,8},{24,0},{32,56},{40,48},{48,40},{56,32},{64,88... | collective-permute-start | bytes 983048 | tf_op jit(solution)/shard_map/ppermute | solution.py:382
  25.3 13.6 %collective-permute-start.9 = (bf16[2,512,128]{2,1,0:T(8,128)(2,1)S(1)}, bf16[2,512,128]{2,1,0:T(8,128)(2,1)S(1)}, u32[]{:S(2)}, u32[]{:S(2)}) collective-permute-start(bf16[2,512,128]{2,1,0:T(8,128)(2,1)S(1)} %collective-permute-done.5.rest_3_), channel_id=1, source_target_pairs={{0,224},{8,232},{16,240},{24,248},{32,0},{40,8},{48,16},{56,24},{6... | collective-permute-start | bytes 786440 | tf_op jit(solution)/shard_map/ppermute | solution.py:391
  26.0 14.9 %collective-permute-start.10 = (bf16[2,512,128]{2,1,0:T(8,128)(2,1)S(1)}, bf16[2,512,128]{2,1,0:T(8,128)(2,1)S(1)}, u32[]{:S(2)}, u32[]{:S(2)}) collective-permute-start(bf16[2,512,128]{2,1,0:T(8,128)(2,1)S(1)} %collective-permute-done.6.rest_4_), channel_id=1, source_target_pairs={{0,32},{8,40},{16,48},{24,56},{32,64},{40,72},{48,80},{56,88},{64,... | collective-permute-start | bytes 786440 | tf_op jit(solution)/shard_map/ppermute | solution.py:390
  30.6 11.4 %collective-permute-start.12 = (bf16[2,512,128]{2,1,0:T(8,128)(2,1)S(1)}, bf16[2,512,128]{2,1,0:T(8,128)(2,1)S(1)}, u32[]{:S(2)}, u32[]{:S(2)}) collective-permute-start(bf16[2,512,128]{2,1,0:T(8,128)(2,1)S(1)} %collective-permute-done.8.rest_0_), channel_id=1, source_target_pairs={{0,32},{8,40},{16,48},{24,56},{32,64},{40,72},{48,80},{56,88},{64,... | collective-permute-start | bytes 786440 | tf_op jit(solution)/shard_map/ppermute | solution.py:390
  31.5 11.2 %collective-permute-start.15 = (bf16[2,512,128]{2,1,0:T(8,128)(2,1)S(1)}, bf16[2,512,128]{2,1,0:T(8,128)(2,1)S(1)}, u32[]{:S(2)}, u32[]{:S(2)}) collective-permute-start(bf16[2,512,128]{2,1,0:T(8,128)(2,1)S(1)} %collective-permute-done.11.rest_3_), channel_id=1, source_target_pairs={{0,224},{8,232},{16,240},{24,248},{32,0},{40,8},{48,16},{56,24},{6... | collective-permute-start | bytes 786440 | tf_op jit(solution)/shard_map/ppermute | solution.py:391
  36.5 0.8 copy-start.2
  38.9 24.8 %collective-permute-start.13 = (bf16[2,512,128]{2,1,0:T(8,128)(2,1)S(1)}, bf16[2,512,128]{2,1,0:T(8,128)(2,1)S(1)}, u32[]{:S(2)}, u32[]{:S(2)}) collective-permute-start(bf16[2,512,128]{2,1,0:T(8,128)(2,1)S(1)} %collective-permute-done.9.rest_1_), channel_id=1, source_target_pairs={{0,224},{8,232},{16,240},{24,248},{32,0},{40,8},{48,16},{56,24},{6... | collective-permute-start | bytes 786440 | tf_op jit(solution)/shard_map/ppermute | solution.py:391
  40.8 22.9 %collective-permute-start.14 = (bf16[2,512,128]{2,1,0:T(8,128)(2,1)S(1)}, bf16[2,512,128]{2,1,0:T(8,128)(2,1)S(1)}, u32[]{:S(2)}, u32[]{:S(2)}) collective-permute-start(bf16[2,512,128]{2,1,0:T(8,128)(2,1)S(1)} %collective-permute-done.10.rest_2_), channel_id=1, source_target_pairs={{0,32},{8,40},{16,48},{24,56},{32,64},{40,72},{48,80},{56,88},{64,... | collective-permute-start | bytes 786440 | tf_op jit(solution)/shard_map/ppermute | solution.py:390
  42.0 26.8 %collective-permute-start.16 = (bf16[2,512,128]{2,1,0:T(8,128)(2,1)S(1)}, bf16[2,512,128]{2,1,0:T(8,128)(2,1)S(1)}, u32[]{:S(2)}, u32[]{:S(2)}) collective-permute-start(bf16[2,512,128]{2,1,0:T(8,128)(2,1)S(1)} %collective-permute-done.12.rest_0_), channel_id=1, source_target_pairs={{0,32},{8,40},{16,48},{24,56},{32,64},{40,72},{48,80},{56,88},{64,... | collective-permute-start | bytes 786440 | tf_op jit(solution)/shard_map/ppermute | solution.py:395
  42.8 26.0 %collective-permute-start.17 = (bf16[2,512,128]{2,1,0:T(8,128)(2,1)S(1)}, bf16[2,512,128]{2,1,0:T(8,128)(2,1)S(1)}, u32[]{:S(2)}, u32[]{:S(2)}) collective-permute-start(bf16[2,512,128]{2,1,0:T(8,128)(2,1)S(1)} %collective-permute-done.15.rest_3_), channel_id=1, source_target_pairs={{0,224},{8,232},{16,240},{24,248},{32,0},{40,8},{48,16},{56,24},{6... | collective-permute-start | bytes 786440 | tf_op jit(solution)/shard_map/ppermute | solution.py:397
  71.9 1.8 %collective-permute-start.18 = (bf16[2,688,128]{2,1,0:T(8,128)(2,1)S(1)}, bf16[2,688,128]{2,1,0:T(8,128)(2,1)S(1)}, u32[]{:S(2)}, u32[]{:S(2)}) collective-permute-start(bf16[2,688,128]{2,1,0:T(8,128)(2,1)S(1)} %get-tuple-element.60), channel_id=1, source_target_pairs={{0,8},{8,0},{16,24},{24,16},{32,40},{40,32},{48,56},{56,48},{64,72... | collective-permute-start | bytes 1056776 | tf_op jit(solution)/shard_map/ppermute | solution.py:529
  72.0 2.2 %collective-permute-start.27 = (bf16[2,688,128]{2,1,0:T(8,128)(2,1)S(1)}, bf16[2,688,128]{2,1,0:T(8,128)(2,1)S(1)}, u32[]{:S(2)}, u32[]{:S(2)}) collective-permute-start(bf16[2,688,128]{2,1,0:T(8,128)(2,1)S(1)} %get-tuple-element.73), channel_id=1, source_target_pairs={{0,8},{8,0},{16,24},{24,16},{32,40},{40,32},{48,56},{56,48},{64,72... | collective-permute-start | bytes 1056776 | tf_op jit(solution)/shard_map/ppermute | solution.py:529
  73.8 7.4 %collective-permute-start.19 = (bf16[688,128]{1,0:T(8,128)(2,1)S(1)}, bf16[688,128]{1,0:T(8,128)(2,1)S(1)}, u32[]{:S(2)}, u32[]{:S(2)}) collective-permute-start(bf16[688,128]{1,0:T(8,128)(2,1)S(1)} %merge.2), channel_id=1, source_target_pairs={{0,16},{8,24},{16,0},{24,8},{32,48},{40,56},{48,32},{56,40},{64,80... | collective-permute-start | bytes 528392 | tf_op jit(solution)/shard_map/ppermute | solution.py:541
  74.3 18.6 %collective-permute-start.28 = (bf16[688,128]{1,0:T(8,128)(2,1)S(1)}, bf16[688,128]{1,0:T(8,128)(2,1)S(1)}, u32[]{:S(2)}, u32[]{:S(2)}) collective-permute-start(bf16[688,128]{1,0:T(8,128)(2,1)S(1)} %merge.3), channel_id=1, source_target_pairs={{0,16},{8,24},{16,0},{24,8},{32,48},{40,56},{48,32},{56,40},{64,80... | collective-permute-start | bytes 528392 | tf_op jit(solution)/shard_map/ppermute | solution.py:541
  85.6 12.6 %collective-permute-start.20 = (bf16[128,640]{1,0:T(8,128)(2,1)S(1)}, bf16[128,640]{1,0:T(8,128)(2,1)S(1)}, u32[]{:S(2)}, u32[]{:S(2)}) collective-permute-start(bf16[128,640]{1,0:T(8,128)(2,1)S(1)} %get-tuple-element.64), channel_id=1, source_target_pairs={{0,1},{1,0},{2,3},{3,2},{4,5},{5,4},{6,7},{7,6},{8,9},{9,8},{10,11... | collective-permute-start | bytes 491528 | tf_op jit(solution)/shard_map/ppermute | solution.py:566
  87.3 17.0 %collective-permute-start.21 = (bf16[128,640]{1,0:T(8,128)(2,1)S(1)}, bf16[128,640]{1,0:T(8,128)(2,1)S(1)}, u32[]{:S(2)}, u32[]{:S(2)}) collective-permute-start(bf16[128,640]{1,0:T(8,128)(2,1)S(1)} %get-tuple-element.65), channel_id=1, source_target_pairs={{0,2},{1,3},{2,0},{3,1},{4,6},{5,7},{6,4},{7,5},{8,10},{9,11},{10,... | collective-permute-start | bytes 491528 | tf_op jit(solution)/shard_map/ppermute | solution.py:566
  90.2 14.8 %collective-permute-start.22 = (bf16[128,640]{1,0:T(8,128)(2,1)S(1)}, bf16[128,640]{1,0:T(8,128)(2,1)}, u32[]{:S(2)}, u32[]{:S(2)}) collective-permute-start(bf16[128,640]{1,0:T(8,128)(2,1)S(1)} %get-tuple-element.66), channel_id=1, source_target_pairs={{0,3},{1,2},{2,1},{3,0},{4,7},{5,6},{6,5},{7,4},{8,11},{9,10},{10,... | collective-permute-start | bytes 491528 | tf_op jit(solution)/shard_map/ppermute | solution.py:566
  90.4 14.6 %collective-permute-start.23 = (bf16[128,640]{1,0:T(8,128)(2,1)S(1)}, bf16[128,640]{1,0:T(8,128)(2,1)S(1)}, u32[]{:S(2)}, u32[]{:S(2)}) collective-permute-start(bf16[128,640]{1,0:T(8,128)(2,1)S(1)} %get-tuple-element.67), channel_id=1, source_target_pairs={{0,4},{1,5},{2,6},{3,7},{4,0},{5,1},{6,2},{7,3},{8,12},{9,13},{10,... | collective-permute-start | bytes 491528 | tf_op jit(solution)/shard_map/ppermute | solution.py:566
  92.9 17.4 %collective-permute-start.24 = (bf16[128,640]{1,0:T(8,128)(2,1)S(1)}, bf16[128,640]{1,0:T(8,128)(2,1)}, u32[]{:S(2)}, u32[]{:S(2)}) collective-permute-start(bf16[128,640]{1,0:T(8,128)(2,1)S(1)} %get-tuple-element.68), channel_id=1, source_target_pairs={{0,5},{1,4},{2,7},{3,6},{4,1},{5,0},{6,3},{7,2},{8,13},{9,12},{10,... | collective-permute-start | bytes 491528 | tf_op jit(solution)/shard_map/ppermute | solution.py:566
  98.2 36.3 %copy-start.6 = (bf16[640]{0:T(1024)(128)(2,1)S(1)}, bf16[640]{0:T(1024)(128)(2,1)}, u32[]{:S(2)}) copy-start(bf16[640]{0:T(1024)(128)(2,1)} %param.21) | copy-start | bytes 3844
  98.3 12.2 %collective-permute-start.25 = (bf16[128,640]{1,0:T(8,128)(2,1)S(1)}, bf16[128,640]{1,0:T(8,128)(2,1)S(1)}, u32[]{:S(2)}, u32[]{:S(2)}) collective-permute-start(bf16[128,640]{1,0:T(8,128)(2,1)S(1)} %get-tuple-element.69), channel_id=1, source_target_pairs={{0,6},{1,7},{2,4},{3,5},{4,2},{5,3},{6,0},{7,1},{8,14},{9,15},{10,... | collective-permute-start | bytes 491528 | tf_op jit(solution)/shard_map/ppermute | solution.py:566
  104.3 9.8 %collective-permute-start.26 = (bf16[128,640]{1,0:T(8,128)(2,1)S(1)}, bf16[128,640]{1,0:T(8,128)(2,1)S(1)}, u32[]{:S(2)}, u32[]{:S(2)}) collective-permute-start(bf16[128,640]{1,0:T(8,128)(2,1)S(1)} %get-tuple-element.70), channel_id=1, source_target_pairs={{0,7},{1,6},{2,5},{3,4},{4,3},{5,2},{6,1},{7,0},{8,15},{9,14},{10,... | collective-permute-start | bytes 491528 | tf_op jit(solution)/shard_map/ppermute | solution.py:566
  105.1 9.2 %collective-permute-start.29 = (bf16[128,640]{1,0:T(8,128)(2,1)S(1)}, bf16[128,640]{1,0:T(8,128)(2,1)S(1)}, u32[]{:S(2)}, u32[]{:S(2)}) collective-permute-start(bf16[128,640]{1,0:T(8,128)(2,1)S(1)} %get-tuple-element.77), channel_id=1, source_target_pairs={{0,1},{1,0},{2,3},{3,2},{4,5},{5,4},{6,7},{7,6},{8,9},{9,8},{10,11... | collective-permute-start | bytes 491528 | tf_op jit(solution)/shard_map/ppermute | solution.py:566
  105.1 0.7 copy-start.4
  105.7 14.0 %collective-permute-start.30 = (bf16[128,640]{1,0:T(8,128)(2,1)S(1)}, bf16[128,640]{1,0:T(8,128)(2,1)S(1)}, u32[]{:S(2)}, u32[]{:S(2)}) collective-permute-start(bf16[128,640]{1,0:T(8,128)(2,1)S(1)} %get-tuple-element.78), channel_id=1, source_target_pairs={{0,2},{1,3},{2,0},{3,1},{4,6},{5,7},{6,4},{7,5},{8,10},{9,11},{10,... | collective-permute-start | bytes 491528 | tf_op jit(solution)/shard_map/ppermute | solution.py:566
  110.2 12.9 %collective-permute-start.31 = (bf16[128,640]{1,0:T(8,128)(2,1)S(1)}, bf16[128,640]{1,0:T(8,128)(2,1)S(1)}, u32[]{:S(2)}, u32[]{:S(2)}) collective-permute-start(bf16[128,640]{1,0:T(8,128)(2,1)S(1)} %get-tuple-element.79), channel_id=1, source_target_pairs={{0,3},{1,2},{2,1},{3,0},{4,7},{5,6},{6,5},{7,4},{8,11},{9,10},{10,... | collective-permute-start | bytes 491528 | tf_op jit(solution)/shard_map/ppermute | solution.py:566
  110.4 12.8 %collective-permute-start.32 = (bf16[128,640]{1,0:T(8,128)(2,1)S(1)}, bf16[128,640]{1,0:T(8,128)(2,1)S(1)}, u32[]{:S(2)}, u32[]{:S(2)}) collective-permute-start(bf16[128,640]{1,0:T(8,128)(2,1)S(1)} %get-tuple-element.80), channel_id=1, source_target_pairs={{0,4},{1,5},{2,6},{3,7},{4,0},{5,1},{6,2},{7,3},{8,12},{9,13},{10,... | collective-permute-start | bytes 491528 | tf_op jit(solution)/shard_map/ppermute | solution.py:566
  114.1 7.8 %copy-start.5 = (bf16[128,640]{1,0:T(8,128)(2,1)}, bf16[128,640]{1,0:T(8,128)(2,1)S(1)}, u32[]{:S(2)}) copy-start(bf16[128,640]{1,0:T(8,128)(2,1)S(1)} %collective-permute-done.26) | copy-start | bytes 491524
  114.1 9.5 %collective-permute-start.33 = (bf16[128,640]{1,0:T(8,128)(2,1)S(1)}, bf16[128,640]{1,0:T(8,128)(2,1)S(1)}, u32[]{:S(2)}, u32[]{:S(2)}) collective-permute-start(bf16[128,640]{1,0:T(8,128)(2,1)S(1)} %get-tuple-element.81), channel_id=1, source_target_pairs={{0,5},{1,4},{2,7},{3,6},{4,1},{5,0},{6,3},{7,2},{8,13},{9,12},{10,... | collective-permute-start | bytes 491528 | tf_op jit(solution)/shard_map/ppermute | solution.py:566
  114.3 12.4 %collective-permute-start.34 = (bf16[128,640]{1,0:T(8,128)(2,1)S(1)}, bf16[128,640]{1,0:T(8,128)(2,1)S(1)}, u32[]{:S(2)}, u32[]{:S(2)}) collective-permute-start(bf16[128,640]{1,0:T(8,128)(2,1)S(1)} %get-tuple-element.82), channel_id=1, source_target_pairs={{0,6},{1,7},{2,4},{3,5},{4,2},{5,3},{6,0},{7,1},{8,14},{9,15},{10,... | collective-permute-start | bytes 491528 | tf_op jit(solution)/shard_map/ppermute | solution.py:566
  119.8 8.9 %collective-permute-start.35 = (bf16[128,640]{1,0:T(8,128)(2,1)S(1)}, bf16[128,640]{1,0:T(8,128)(2,1)S(1)}, u32[]{:S(2)}, u32[]{:S(2)}) collective-permute-start(bf16[128,640]{1,0:T(8,128)(2,1)S(1)} %get-tuple-element.83), channel_id=1, source_target_pairs={{0,7},{1,6},{2,5},{3,4},{4,3},{5,2},{6,1},{7,0},{8,15},{9,14},{10,... | collective-permute-start | bytes 491528 | tf_op jit(solution)/shard_map/ppermute | solution.py:566
  130.0 13.2 %copy-start.3 = (bf16[256,640]{1,0:T(8,128)(2,1)}, bf16[256,640]{1,0:T(8,128)(2,1)S(1)}, u32[]{:S(2)}) copy-start(bf16[256,640]{1,0:T(8,128)(2,1)S(1)} %get-tuple-element.90) | copy-start | bytes 983044
  130.7 11.6 %all-to-all-start = ((f32[8,8,128]{2,1,0:T(8,128)}), f32[8,8,128]{2,1,0:T(8,128)S(1)}, u32[]{:S(2)}, u32[]{:S(2)}) async-start(f32[8,8,128]{2,1,0:T(8,128)} %broadcast_in_dim.88), calls=%async_computation | async-start | bytes 65536 | tf_op jit(solution)/shard_map/all_to_all | solution.py:575
where the time goes:
time: 144 us; the launch traced here: 143 us
  starting transfers between devices  60.3 us (42%)
  Pallas kernels  35.9 us (25%)
  waiting for transfers between devices  32.7 us (23%)
  other arithmetic  8.92 us (6%)
  local copies, waits for them, and re-layouts  4.34 us (3%)
    ppermute x14, starting transfers between devices, shards(): piece = lax.ppermute(pieces[k], 'tp', [(i, i ^ k) for i in range(ways)])  29.8 us
    ppermute x6, starting transfers between devices, shards(): moving_down = lax.ppermute(moving_down, 'req', down_pairs)  15.1 us
    pallas_call x1, Pallas kernels, shards(): pl.pallas_call(make_first(base, len(parts)), out_shape=(shape((every, lin...  12.2 us
    pallas_call x2, Pallas kernels, shards(): pl.pallas_call(make_middle(base, len(parts)), out_shape=state_shapes, in_...  10 us
    pallas_call x2, Pallas kernels, shards(): pl.pallas_call(make_combine(j), out_shape=tuple((shape((TILE, columns), b...  8.88 us
    all_to_all x1, waiting for transfers between devices, shards(): lax.all_to_all(jnp.broadcast_to(squares[None], (ways, 8, HD)), 'tp', 0, 0)  7.75 us
    ppermute x6, waiting for transfers between devices, shards(): moving_down = lax.ppermute(moving_down, 'req', down_pairs)  7.52 us
    ppermute x14, waiting for transfers between devices, shards(): piece = lax.ppermute(pieces[k], 'tp', [(i, i ^ k) for i in range(ways)])  6.73 us
  transfers between devices with their start and end apart: 37, of which 14 were waited for; matrix products, arithmetic and copies ran while one was open for 5% of the time, Pallas kernels for 23%

commit v1 on v0

--- a/solution.py
+++ b/solution.py
@@ -14,7 +14,8 @@
 NEGATIVE = -1e30
 EPSILON = 1e-06
 LOG2E = 1.4426950408889634
-PATHS = (6, 2, 4, 7, 5, 3, 1, 0)
+PATHS = (2, 3, 1, 0)
+FAR = 4
 
 
 SMEM = pltpu.SMEM
@@ -286,21 +287,7 @@
 
 
 def make_combine(j):
-    def kernel(meta, where, acc_own, stats_own, swapped, crossed, weight_in, *rest):
-        ways = len(rest) - 3
-        outs = rest[:ways]
-        attn_ref, weight_ref, sems = rest[ways:]
-        columns = weight_ref.shape[2]
-        copies = []
-        for k in range(ways):
-            at = pl.multiple_of((where[0] ^ k) * columns, HD)
-            copies.append(
-                pltpu.make_async_copy(
-                    weight_in.at[:, pl.ds(at, columns)], weight_ref.at[k], sems.at[k]
-                )
-            )
-        for k in PATHS:
-            copies[k].start()
+    def kernel(meta, acc_own, stats_own, swapped, crossed, attn_ref):
         heads = acc_own.shape[1] // TILE
         parts = (swapped.at[0], crossed)
         maxima = [stats_own[:8]]
@@ -322,13 +309,43 @@
                 value = value + w[h : h + 1] * part[h * HD : (h + 1) * HD].astype(jnp.float32)
             value = jnp.transpose(jnp.where(live, value, 0.0))
             attn_ref[:, h * HD : (h + 1) * HD] = value.astype(jnp.bfloat16)
-        for k in PATHS:
-            copies[k].wait()
-            outs[k][...] = jnp.dot(
-                attn_ref[...], weight_ref[k], preferred_element_type=jnp.float32
-            ).astype(outs[k].dtype)
 
     return kernel
+
+
+def project_kernel(where, attn_near, attn_far, weight_in, mine_in, theirs_in, *rest):
+    paths = len(PATHS)
+    outs = rest[:paths]
+    near_ref, far_ref, sems = rest[paths:]
+    columns = near_ref.shape[2]
+    tensor, core = where[0], where[1]
+
+    def copy_near(k):
+        at = pl.multiple_of((tensor ^ k) * columns, HD)
+        return pltpu.make_async_copy(weight_in.at[:, pl.ds(at, columns)], near_ref.at[k], sems.at[0, k])
+
+    def copy_far(k, source):
+        at = pl.multiple_of(((tensor ^ k) % 2) * columns, HD)
+        return pltpu.make_async_copy(source.at[:, pl.ds(at, columns)], far_ref.at[k], sems.at[1, k])
+
+    for k in PATHS:
+        copy_near(k).start()
+        same = ((tensor ^ k) % FAR) // 2 == core
+
+        @pl.when(same)
+        def _(k=k):
+            copy_far(k, mine_in).start()
+
+        @pl.when(jnp.logical_not(same))
+        def _(k=k):
+            copy_far(k, theirs_in).start()
+
+    for k in PATHS:
+        copy_near(k).wait()
+        copy_far(k, mine_in).wait()
+        total = jnp.dot(attn_near[...], near_ref[k], preferred_element_type=jnp.float32)
+        total = total + jnp.dot(attn_far[...], far_ref[k], preferred_element_type=jnp.float32)
+        outs[k][...] = total.astype(outs[k].dtype)
 
 
 def cost(blocks, bytes_accessed):
@@ -373,6 +390,14 @@
     down_pairs = [(i, (i - PLANE) % devices) for i in range(devices)]
 
     core = place % 2
+    width = residual.shape[1]
+    columns = width // ways
+    where = jnp.stack([tensor, core]).astype(jnp.int32)
+    far_side = (tensor // FAR) ^ 1
+    outgoing = lax.dynamic_slice_in_dim(
+        out_weight, (far_side * FAR + 2 * core) * columns, 2 * columns, 1
+    )
+    weight_mine = lax.ppermute(outgoing, "tp", [(i, i ^ FAR) for i in range(ways)])
     both = jnp.concatenate([prefix_key, prefix_value], axis=0)
     mine = lax.dynamic_slice_in_dim(both, core * part, part, 1)
     theirs = lax.dynamic_slice_in_dim(both, (1 - core) * part, part, 1)
@@ -521,9 +546,6 @@
         name="last",
     )(meta, q_all, *state, *parts)
 
-    width = residual.shape[1]
-    columns = width // ways
-    where = tensor.astype(jnp.int32).reshape(1)
     swapped = []
     for j in range(tiles_each):
         swapped.append(lax.ppermute(last[5 * j + 4], "req", beside(1)))
@@ -539,19 +561,35 @@
             name="merge",
         )(last[5 * j + 2], last[5 * j + 3], swapped[j])
         crossed.append(lax.ppermute(merged, "req", beside(2)))
+    near = []
+    far = []
+    for j in range(tiles_each):
+        attn = pl.pallas_call(
+            make_combine(j),
+            out_shape=shape((TILE, heads * HD), bf16),
+            in_specs=[full(SMEM)] + [full()] * 4,
+            out_specs=full(),
+            cost_estimate=pl.CostEstimate(flops=1 << 20, bytes_accessed=1 << 20, transcendentals=0),
+            compiler_params=params(),
+            name="combine",
+        )(meta, last[5 * j], last[5 * j + 1], swapped[j], crossed[j])
+        near.append(attn)
+        far.append(lax.ppermute(attn, "tp", [(i, i ^ FAR) for i in range(ways)]))
+    weight_theirs = lax.ppermute(weight_mine, "req", beside(1))
     shared = []
+    paths = len(PATHS)
     for j in range(tiles_each):
         pieces = pl.pallas_call(
-            make_combine(j),
+            project_kernel,
             out_shape=tuple(
-                shape((TILE, columns), bf16 if k else f32) for k in range(ways)
+                shape((TILE, columns), bf16 if k else f32) for k in range(paths)
             ),
-            in_specs=[full(SMEM)] * 2 + [full()] * 4 + [full(pl.ANY)],
-            out_specs=(full(),) * ways,
+            in_specs=[full(SMEM), full(), full()] + [full(pl.ANY)] * 3,
+            out_specs=(full(),) * paths,
             scratch_shapes=[
-                pltpu.VMEM((TILE, heads * HD), bf16),
-                pltpu.VMEM((ways, heads * HD, columns), bf16),
-                pltpu.SemaphoreType.DMA((ways,)),
+                pltpu.VMEM((paths, heads * HD, columns), bf16),
+                pltpu.VMEM((paths, heads * HD, columns), bf16),
+                pltpu.SemaphoreType.DMA((2, paths)),
             ],
             cost_estimate=pl.CostEstimate(
                 flops=2 * TILE * heads * HD * width,
@@ -559,10 +597,10 @@
                 transcendentals=0,
             ),
             compiler_params=params(50),
-            name="combine",
-        )(meta, where, last[5 * j], last[5 * j + 1], swapped[j], crossed[j], out_weight)
+            name="project",
+        )(where, near[j], far[j], out_weight, weight_mine, weight_theirs)
         total = pieces[0]
-        for k in range(1, ways):
+        for k in range(1, paths):
             piece = lax.ppermute(pieces[k], "tp", [(i, i ^ k) for i in range(ways)])
             total = total + piece.astype(f32)
         shared.append(total)

time: 144 us -> 170 us (1.18)
  waiting for transfers between devices: 32.7 us -> 73.3 us
  starting transfers between devices: 60.3 us -> 44.2 us
  local copies, waits for them, and re-layouts: 4.34 us -> 8.28 us
  other arithmetic: 8.92 us -> 5.64 us
    ppermute x3, waiting for transfers between devices: 0.01 us -> 40.8 us  [shards(): queries.append(lax.ppermute(suffix_query, 'req', beside(k)))]
    ppermute x14 -> x6, starting transfers between devices: 29.8 us -> 9.57 us  [shards(): piece = lax.ppermute(pieces[k], 'tp', [(i, i ^ k) for i in range(ways)])]
    ppermute x6, waiting for transfers between devices: 7.52 us -> 0.68 us  [shards(): moving_down = lax.ppermute(moving_down, 'req', down_pairs)]
    ppermute x0 -> x4, starting transfers between devices: none -> 3.79 us  [the longest x1 2.12 us: shards(): lax.ppermute(outgoing, 'tp', [(i, i ^ FAR) for i in range(ways)])]
    ppermute x0 -> x4, waiting for transfers between devices: none -> 3.11 us  [the longest x2 3.1 us: shards(): far.append(lax.ppermute(attn, 'tp', [(i, i ^ FAR) for i in range(ways)]))]
    dynamic_slice x0 -> x1, local copies, waits for them, and re-layouts: none -> 2.74 us  [shards(): lax.dynamic_slice_in_dim(out_weight, (far_side * FAR + 2 * core) * column...]
    ppermute x2, waiting for transfers between devices: 4.92 us -> 7.49 us  [shards(): crossed.append(lax.ppermute(merged, 'req', beside(2)))]
    ppermute x6, starting transfers between devices: 15.1 us -> 17.5 us  [shards(): moving_down = lax.ppermute(moving_down, 'req', down_pairs)]
  transfers between devices with their start and end apart: 37 -> 33, of which waited for: 14 -> 14; matrix products, arithmetic and copies ran while one was open for 5% -> 4% of each run, Pallas kernels for 23% -> 22%
where the time goes in v1:
time: 170 us
  waiting for transfers between devices  73.3 us (43%)
  starting transfers between devices  44.2 us (26%)
  Pallas kernels  37.3 us (22%)
  local copies, waits for them, and re-layouts  8.28 us (5%)
  other arithmetic  5.64 us (3%)
    ppermute x3, waiting for transfers between devices, shards(): queries.append(lax.ppermute(suffix_query, 'req', beside(k)))  40.8 us
    ppermute x6, starting transfers between devices, shards(): moving_down = lax.ppermute(moving_down, 'req', down_pairs)  17.5 us
    pallas_call x1, Pallas kernels, shards(): pl.pallas_call(make_first(base, len(parts)), out_shape=(shape((every, lin...  13 us
    pallas_call x2, Pallas kernels, shards(): pl.pallas_call(make_middle(base, len(parts)), out_shape=state_shapes, in_...  10 us
    ppermute x6, starting transfers between devices, shards(): piece = lax.ppermute(pieces[k], 'tp', [(i, i ^ k) for i in range(ways)])  9.57 us
    pallas_call x2, Pallas kernels, shards(): pl.pallas_call(project_kernel, out_shape=tuple((shape((TILE, columns), bf...  7.96 us
    all_to_all x1, waiting for transfers between devices, shards(): lax.all_to_all(jnp.broadcast_to(squares[None], (ways, 8, HD)), 'tp', 0, 0)  7.67 us
    ppermute x2, waiting for transfers between devices, shards(): crossed.append(lax.ppermute(merged, 'req', beside(2)))  7.49 us
  transfers between devices with their start and end apart: 33, of which 14 were waited for; matrix products, arithmetic and copies ran while one was open for 4% of the time, Pallas kernels for 22%

profile of v1, /device:TPU:2, one launch (start us, length us, event | category | flops | bytes accessed | tf_op | source)
XLA Modules:
  0.0 169.8 jit_solution(218602357932250979)
XLA Ops:
  0.7 1.0 constant_dynamic-update-slice_fusion.1
  1.8 1.0 constant_dynamic-update-slice_fusion
  2.8 2.0 %collective-permute-start.4 = (bf16[2,512,128]{2,1,0:T(8,128)(2,1)S(1)}, bf16[2,512,128]{2,1,0:T(8,128)(2,1)}, u32[]{:S(2)}, u32[]{:S(2)}) collective-permute-start(bf16[2,512,128]{2,1,0:T(8,128)(2,1)S(1)} %get-tuple-element.76.rest_0_), channel_id=1, source_target_pairs={{0,32},{8,40},{16,48},{24,56},{32,64},{40,72},{48,80},{56,88},{64,... | collective-permute-start | bytes 786440 | tf_op jit(solution)/shard_map/ppermute | solution.py:415
  4.8 4.0 %collective-permute-start.5 = (bf16[2,512,128]{2,1,0:T(8,128)(2,1)S(1)}, bf16[2,512,128]{2,1,0:T(8,128)(2,1)S(1)}, u32[]{:S(2)}, u32[]{:S(2)}) collective-permute-start(bf16[2,512,128]{2,1,0:T(8,128)(2,1)S(1)} %get-tuple-element.76.rest_0_), channel_id=1, source_target_pairs={{0,224},{8,232},{16,240},{24,248},{32,0},{40,8},{48,16},{56,24},{6... | collective-permute-start | bytes 786440 | tf_op jit(solution)/shard_map/ppermute | solution.py:416
  8.9 0.5 collective-permute-start
  9.4 2.7 %constant_dynamic-slice_fusion = bf16[640,1280]{1,0:T(8,128)(2,1)} fusion(bf16[640,5120]{1,0:T(8,128)(2,1)} %weight_in.3, s32[]{:T(128)S(6)} %select_n.87), kind=kLoop, calls=%fused_computation.40 | loop fusion | bytes 3276804 | tf_op jit(solution)/shard_map/dynamic_slice | solution.py:397
  12.1 2.1 %collective-permute-start.21 = (bf16[640,1280]{1,0:T(8,128)(2,1)}, bf16[640,1280]{1,0:T(8,128)(2,1)S(1)}, u32[]{:S(2)}, u32[]{:S(2)}) collective-permute-start(bf16[640,1280]{1,0:T(8,128)(2,1)} %constant_dynamic-slice_fusion), channel_id=1, source_target_pairs={{0,4},{1,5},{2,6},{3,7},{4,0},{5,1},{6,2},{7,3},{8,12},{9,13},{10,... | collective-permute-start | bytes 4915208 | tf_op jit(solution)/shard_map/ppermute | solution.py:400
  14.2 0.1 select_reduce_fusion.1
  14.4 0.2 select_reduce_fusion.3
  14.6 0.2 select_reduce_fusion.2
  14.8 0.2 select_reduce_fusion.5
  15.0 1.5 collective-permute-start.1
  16.5 1.9 %collective-permute-start.7 = (bf16[2,512,128]{2,1,0:T(8,128)(2,1)}, bf16[2,512,128]{2,1,0:T(8,128)(2,1)}, u32[]{:S(2)}, u32[]{:S(2)}) collective-permute-start(bf16[2,512,128]{2,1,0:T(8,128)(2,1)} %collective-permute-done.3.rest_1_), channel_id=1, source_target_pairs={{0,224},{8,232},{16,240},{24,248},{32,0},{40,8},{48,16},{56,24},{6... | collective-permute-start | bytes 786440 | tf_op jit(solution)/shard_map/ppermute | solution.py:416
  18.5 1.3 fusion.4
  19.8 0.2 collective-permute-start.6
  19.9 0.5 copy-done.1
  20.5 39.1 %collective-permute-done.1.q2 = bf16[256,640]{1,0:T(8,128)(2,1)S(1)} collective-permute-done((bf16[256,640]{1,0:T(8,128)(2,1)S(1)}, bf16[256,640]{1,0:T(8,128)(2,1)S(1)}, u32[]{:S(2)}, u32[]{:S(2)}) %collective-permute-start.1) | collective-permute-done | bytes 327712 | tf_op jit(solution)/shard_map/ppermute | solution.py:407
  59.5 3.2 %collective-permute-start.11 = (bf16[2,512,128]{2,1,0:T(8,128)(2,1)}, bf16[2,512,128]{2,1,0:T(8,128)(2,1)S(1)}, u32[]{:S(2)}, u32[]{:S(2)}) collective-permute-start(bf16[2,512,128]{2,1,0:T(8,128)(2,1)} %collective-permute-done.7.rest_5_), channel_id=1, source_target_pairs={{0,224},{8,232},{16,240},{24,248},{32,0},{40,8},{48,16},{56,24},{6... | collective-permute-start | bytes 786440 | tf_op jit(solution)/shard_map/ppermute | solution.py:416
  63.0 0.1 collective-permute-start.22
  63.1 1.7 collective-permute-done.2.q3
  64.7 1.9 %collective-permute-start.9 = (bf16[2,512,128]{2,1,0:T(8,128)(2,1)}, bf16[2,512,128]{2,1,0:T(8,128)(2,1)S(1)}, u32[]{:S(2)}, u32[]{:S(2)}) collective-permute-start(bf16[2,512,128]{2,1,0:T(8,128)(2,1)} %copy-done.1), channel_id=1, source_target_pairs={{0,224},{8,232},{16,240},{24,248},{32,0},{40,8},{48,16},{56,24},{6... | collective-permute-start | bytes 786440 | tf_op jit(solution)/shard_map/ppermute | solution.py:416
  66.8 0.6 collective-permute-done.8.rest_0_
  67.4 3.2 %collective-permute-start.15 = (bf16[2,512,128]{2,1,0:T(8,128)(2,1)S(1)}, bf16[2,512,128]{2,1,0:T(8,128)(2,1)S(1)}, u32[]{:S(2)}, u32[]{:S(2)}) collective-permute-start(bf16[2,512,128]{2,1,0:T(8,128)(2,1)S(1)} %collective-permute-done.11.rest_3_), channel_id=1, source_target_pairs={{0,224},{8,232},{16,240},{24,248},{32,0},{40,8},{48,16},{56,24},{6... | collective-permute-start | bytes 786440 | tf_op jit(solution)/shard_map/ppermute | solution.py:416
  70.7 1.2 pad_maximum_fusion
  71.9 1.5 own.1
  73.4 0.7 collective-permute-done.9.rest_1_
  74.1 3.1 %collective-permute-start.13 = (bf16[2,512,128]{2,1,0:T(8,128)(2,1)S(1)}, bf16[2,512,128]{2,1,0:T(8,128)(2,1)S(1)}, u32[]{:S(2)}, u32[]{:S(2)}) collective-permute-start(bf16[2,512,128]{2,1,0:T(8,128)(2,1)S(1)} %collective-permute-done.9.rest_1_), channel_id=1, source_target_pairs={{0,224},{8,232},{16,240},{24,248},{32,0},{40,8},{48,16},{56,24},{6... | collective-permute-start | bytes 786440 | tf_op jit(solution)/shard_map/ppermute | solution.py:416
  77.3 5.6 %collective-permute-done.12.rest_0_ = bf16[2,512,128]{2,1,0:T(8,128)(2,1)S(1)} collective-permute-done((bf16[2,512,128]{2,1,0:T(8,128)(2,1)S(1)}, bf16[2,512,128]{2,1,0:T(8,128)(2,1)S(1)}, u32[]{:S(2)}, u32[]{:S(2)}) %collective-permute-start.12) | collective-permute-done | bytes 262176 | tf_op jit(solution)/shard_map/ppermute | solution.py:415
  82.9 3.2 %collective-permute-start.17 = (bf16[2,512,128]{2,1,0:T(8,128)(2,1)S(1)}, bf16[2,512,128]{2,1,0:T(8,128)(2,1)S(1)}, u32[]{:S(2)}, u32[]{:S(2)}) collective-permute-start(bf16[2,512,128]{2,1,0:T(8,128)(2,1)S(1)} %collective-permute-done.15.rest_3_), channel_id=1, source_target_pairs={{0,224},{8,232},{16,240},{24,248},{32,0},{40,8},{48,16},{56,24},{6... | collective-permute-start | bytes 786440 | tf_op jit(solution)/shard_map/ppermute | solution.py:422
  86.1 0.9 copy-done.2
  87.1 13.0 %first.1 = (bf16[9,640,128]{2,1,0:T(8,128)(2,1)S(1)}, f32[9,128,640]{2,1,0:T(8,128)S(1)}, f32[9,1,640]{2,1,0:T(1,128)S(1)}, f32[9,1,640]{2,1,0:T(1,128)S(1)}) custom-call(s32[72]{0:T(128)S(1)} %pad_add_fusion.1.meta, bf16[2,640,128]{2,1,0:T(8,128)(2,1)S(1)} %get-tuple-element.36.q_own, f32[2,128,640]{2,1,0:T(8,128)S(1)} %get-tuple-element.37.acc_own, ...), custom_call_target="tpu_custom_call" | custom-call | flops 2013265920 | bytes 8388608 | tf_op jit(solution)/shard_map/first/pallas_call | solution.py:500
  100.1 5.0 %middle.2 = (f32[9,128,640]{2,1,0:T(8,128)S(1)}, f32[9,1,640]{2,1,0:T(1,128)S(1)}, f32[9,1,640]{2,1,0:T(1,128)S(1)}) custom-call(s32[72]{0:T(128)S(1)} %pad_add_fusion.1.meta, bf16[9,640,128]{2,1,0:T(8,128)(2,1)S(1)} %get-tuple-element.40.q_ref, f32[9,128,640]{2,1,0:T(8,128)S(1)} %get-tuple-element.41.acc_in, f32[9,1,640]{2,1,0:T(1,128)S(1)} %get-tuple-element.42.max_in, ...), custom_call_target="tpu_custom_call" | custom-call | flops 1342177280 | bytes 8388608 | tf_op jit(solution)/shard_map/middle/pallas_call | solution.py:513
  105.1 5.0 %middle.3 = (f32[9,128,640]{2,1,0:T(8,128)S(1)}, f32[9,1,640]{2,1,0:T(1,128)S(1)}, f32[9,1,640]{2,1,0:T(1,128)S(1)}) custom-call(s32[72]{0:T(128)S(1)} %pad_add_fusion.1.meta, bf16[9,640,128]{2,1,0:T(8,128)(2,1)S(1)} %get-tuple-element.40.q_ref, f32[9,128,640]{2,1,0:T(8,128)S(1)} %get-tuple-element.44.acc_in, f32[9,1,640]{2,1,0:T(1,128)S(1)} %get-tuple-element.45.max_in, ...), custom_call_target="tpu_custom_call" | custom-call | flops 1342177280 | bytes 8388608 | tf_op jit(solution)/shard_map/middle/pallas_call | solution.py:513
  110.2 3.2 %last.1 = (f32[128,640]{1,0:T(8,128)S(1)}, f32[16,128]{1,0:T(8,128)S(1)}, f32[128,640]{1,0:T(8,128)S(1)}, f32[16,128]{1,0:T(8,128)S(1)}, bf16[2,688,128]{2,1,0:T...) custom-call(s32[72]{0:T(128)S(1)} %pad_add_fusion.1.meta, ...), custom_call_target="tpu_custom_call" | custom-call | flops 671088640 | bytes 8388608 | tf_op jit(solution)/shard_map/last/pallas_call | solution.py:526
  113.4 0.1 collective-permute-start.18
  113.5 0.5 collective-permute-start.26
  114.0 1.2 collective-permute-done.18.swapped
  115.2 0.1 collective-permute-start.19
  115.3 0.3 collective-permute-done.26.swapped
  115.7 1.8 %collective-permute-start.27 = (bf16[688,128]{1,0:T(8,128)(2,1)S(1)}, bf16[688,128]{1,0:T(8,128)(2,1)S(1)}, u32[]{:S(2)}, u32[]{:S(2)}) collective-permute-start(bf16[688,128]{1,0:T(8,128)(2,1)S(1)} %merge.3), channel_id=1, source_target_pairs={{0,16},{8,24},{16,0},{24,8},{32,48},{40,56},{48,32},{56,40},{64,80... | collective-permute-start | bytes 528392 | tf_op jit(solution)/shard_map/ppermute | solution.py:563
  117.5 5.1 %collective-permute-done.19.crossed = bf16[688,128]{1,0:T(8,128)(2,1)S(1)} collective-permute-done((bf16[688,128]{1,0:T(8,128)(2,1)S(1)}, bf16[688,128]{1,0:T(8,128)(2,1)S(1)}, u32[]{:S(2)}, u32[]{:S(2)}) %collective-permute-start.19) | collective-permute-done | bytes 176160 | tf_op jit(solution)/shard_map/ppermute | solution.py:563
  122.6 0.7 combine.2.attn_near
  123.3 0.7 collective-permute-start.20
  124.0 2.4 %collective-permute-done.27.crossed = bf16[688,128]{1,0:T(8,128)(2,1)S(1)} collective-permute-done((bf16[688,128]{1,0:T(8,128)(2,1)S(1)}, bf16[688,128]{1,0:T(8,128)(2,1)S(1)}, u32[]{:S(2)}, u32[]{:S(2)}) %collective-permute-start.27) | collective-permute-done | bytes 176160 | tf_op jit(solution)/shard_map/ppermute | solution.py:563
  126.4 0.7 combine.3.attn_near
  127.1 0.9 collective-permute-start.28
  128.1 3.1 %collective-permute-done.20.attn_far = bf16[128,640]{1,0:T(8,128)(2,1)S(1)} collective-permute-done((bf16[128,640]{1,0:T(8,128)(2,1)S(1)}, bf16[128,640]{1,0:T(8,128)(2,1)S(1)}, u32[]{:S(2)}, u32[]{:S(2)}) %collective-permute-start.20) | collective-permute-done | bytes 163872 | tf_op jit(solution)/shard_map/ppermute | solution.py:577
  131.2 1.2 copy-done.5
  132.4 4.0 %project.2 = (f32[128,640]{1,0:T(8,128)S(1)}, bf16[128,640]{1,0:T(8,128)(2,1)S(1)}, bf16[128,640]{1,0:T(8,128)(2,1)S(1)}, bf16[128,640]{1,0:T(8,128)(2,1)S(1)}) custom-call(s32[2]{0:T(128)S(1)} %pad_add_fusion.where, bf16[128,640]{1,0:T(8,128)(2,1)S(1)} %combine.2.attn_near, bf16[128,640]{1,0:T(8,128)(2,1)S(1)} %collective-permute-done.20.attn_far, ...), custom_call_target="tpu_custom_call" | custom-call | flops 838860800 | bytes 8388608 | tf_op jit(solution)/shard_map/project/pallas_call | solution.py:582
  136.4 1.7 collective-permute-start.23
  138.1 2.6 %collective-permute-start.24 = (bf16[128,640]{1,0:T(8,128)(2,1)S(1)}, bf16[128,640]{1,0:T(8,128)(2,1)S(1)}, u32[]{:S(2)}, u32[]{:S(2)}) collective-permute-start(bf16[128,640]{1,0:T(8,128)(2,1)S(1)} %get-tuple-element.57), channel_id=1, source_target_pairs={{0,2},{1,3},{2,0},{3,1},{4,6},{5,7},{6,4},{7,5},{8,10},{9,11},{10,... | collective-permute-start | bytes 491528 | tf_op jit(solution)/shard_map/ppermute | solution.py:604
  140.7 0.5 collective-permute-start.25
  141.2 4.0 %project.3 = (f32[128,640]{1,0:T(8,128)S(1)}, bf16[128,640]{1,0:T(8,128)(2,1)S(1)}, bf16[128,640]{1,0:T(8,128)(2,1)S(1)}, bf16[128,640]{1,0:T(8,128)(2,1)S(1)}) custom-call(s32[2]{0:T(128)S(1)} %pad_add_fusion.where, bf16[128,640]{1,0:T(8,128)(2,1)S(1)} %combine.3.attn_near, bf16[128,640]{1,0:T(8,128)(2,1)S(1)} %collective-permute-done.28.attn_far, ...), custom_call_target="tpu_custom_call" | custom-call | flops 838860800 | bytes 8388608 | tf_op jit(solution)/shard_map/project/pallas_call | solution.py:582
  145.2 0.5 collective-permute-start.29
  145.6 3.5 %collective-permute-start.30 = (bf16[128,640]{1,0:T(8,128)(2,1)S(1)}, bf16[128,640]{1,0:T(8,128)(2,1)S(1)}, u32[]{:S(2)}, u32[]{:S(2)}) collective-permute-start(bf16[128,640]{1,0:T(8,128)(2,1)S(1)} %get-tuple-element.66), channel_id=1, source_target_pairs={{0,2},{1,3},{2,0},{3,1},{4,6},{5,7},{6,4},{7,5},{8,10},{9,11},{10,... | collective-permute-start | bytes 491528 | tf_op jit(solution)/shard_map/ppermute | solution.py:604
  149.1 0.8 collective-permute-start.31
  150.1 0.5 collective-permute-done.29
  150.6 3.6 %collective-permute-done.30 = bf16[128,640]{1,0:T(8,128)(2,1)S(1)} collective-permute-done((bf16[128,640]{1,0:T(8,128)(2,1)S(1)}, bf16[128,640]{1,0:T(8,128)(2,1)S(1)}, u32[]{:S(2)}, u32[]{:S(2)}) %collective-permute-start.30) | collective-permute-done | bytes 163872 | tf_op jit(solution)/shard_map/ppermute | solution.py:604
  154.2 1.7 %collective-permute-done.31 = bf16[128,640]{1,0:T(8,128)(2,1)S(1)} collective-permute-done((bf16[128,640]{1,0:T(8,128)(2,1)S(1)}, bf16[128,640]{1,0:T(8,128)(2,1)S(1)}, u32[]{:S(2)}, u32[]{:S(2)}) %collective-permute-start.31) | collective-permute-done | bytes 163872 | tf_op jit(solution)/shard_map/ppermute | solution.py:604
  156.0 1.2 fusion
  157.2 0.7 broadcast_in_dim.88
  157.9 3.3 %all-to-all-start = ((f32[8,8,128]{2,1,0:T(8,128)}), f32[8,8,128]{2,1,0:T(8,128)S(1)}, u32[]{:S(2)}, u32[]{:S(2)}) async-start(f32[8,8,128]{2,1,0:T(8,128)} %broadcast_in_dim.88), calls=%async_computation | async-start | bytes 65536 | tf_op jit(solution)/shard_map/all_to_all | solution.py:613
  161.2 7.7 %all-to-all-done = f32[8,8,128]{2,1,0:T(8,128)S(1)} async-done(((f32[8,8,128]{2,1,0:T(8,128)}), f32[8,8,128]{2,1,0:T(8,128)S(1)}, u32[]{:S(2)}, u32[]{:S(2)}) %all-to-all-start) | async-done | bytes 32800 | tf_op jit(solution)/shard_map/all_to_all | solution.py:613
  168.9 0.9 fusion.2
  (70 shorter events, 1.0 us)
Async XLA Ops:
  0.7 13.6 %copy-start.13 = (s32[32]{0:T(128)S(1)}, s32[32]{0:T(128)}, u32[]{:S(2)}) copy-start(s32[32]{0:T(128)} %param.24) | copy-start | bytes 388
  0.7 13.7 %copy-start.11 = (s32[16]{0:T(128)S(1)}, s32[16]{0:T(128)}, u32[]{:S(2)}) copy-start(s32[16]{0:T(128)} %constant.122.clone) | copy-start | bytes 196
  0.7 13.7 %copy-start.12 = (s32[16]{0:T(128)S(1)}, s32[16]{0:T(128)}, u32[]{:S(2)}) copy-start(s32[16]{0:T(128)} %constant.123.clone) | copy-start | bytes 196
  0.7 13.9 %copy-start.8 = (s32[32]{0:T(128)S(1)}, s32[32]{0:T(128)}, u32[]{:S(2)}) copy-start(s32[32]{0:T(128)} %param.22) | copy-start | bytes 388
  0.7 13.9 %copy-start.9 = (s32[32]{0:T(128)S(1)}, s32[32]{0:T(128)}, u32[]{:S(2)}) copy-start(s32[32]{0:T(128)} %param.23) | copy-start | bytes 388
  0.7 13.9 %copy-start.10 = (s32[32,1]{0,1:T(1,128)S(1)}, s32[32,1]{0,1:T(1,128)}, u32[]{:S(2)}) copy-start(s32[32,1]{0,1:T(1,128)} %param.25) | copy-start | bytes 388
  0.7 14.3 %copy-start = (bf16[256,640]{1,0:T(8,128)(2,1)S(1)}, bf16[256,640]{1,0:T(8,128)(2,1)}, u32[]{:S(2)}) copy-start(bf16[256,640]{1,0:T(8,128)(2,1)} %q_in.1) | copy-start | bytes 983044
  2.8 69.2 %copy-start.3 = (bf16[256,128]{1,0:T(8,128)(2,1)S(1)}, bf16[256,128]{1,0:T(8,128)(2,1)}, u32[]{:S(2)}) copy-start(bf16[256,128]{1,0:T(8,128)(2,1)} %k_in.1) | copy-start | bytes 196612
  2.8 69.2 %copy-start.4 = (bf16[256,128]{1,0:T(8,128)(2,1)S(1)}, bf16[256,128]{1,0:T(8,128)(2,1)}, u32[]{:S(2)}) copy-start(bf16[256,128]{1,0:T(8,128)(2,1)} %v_in.1) | copy-start | bytes 196612
  2.8 13.7 %collective-permute-start.4 = (bf16[2,512,128]{2,1,0:T(8,128)(2,1)S(1)}, bf16[2,512,128]{2,1,0:T(8,128)(2,1)}, u32[]{:S(2)}, u32[]{:S(2)}) collective-permute-start(bf16[2,512,128]{2,1,0:T(8,128)(2,1)S(1)} %get-tuple-element.76.rest_0_), channel_id=1, source_target_pairs={{0,32},{8,40},{16,48},{24,56},{32,64},{40,72},{48,80},{56,88},{64,... | collective-permute-start | bytes 786440 | tf_op jit(solution)/shard_map/ppermute | solution.py:415
  4.8 14.9 %collective-permute-start.5 = (bf16[2,512,128]{2,1,0:T(8,128)(2,1)S(1)}, bf16[2,512,128]{2,1,0:T(8,128)(2,1)S(1)}, u32[]{:S(2)}, u32[]{:S(2)}) collective-permute-start(bf16[2,512,128]{2,1,0:T(8,128)(2,1)S(1)} %get-tuple-element.76.rest_0_), channel_id=1, source_target_pairs={{0,224},{8,232},{16,240},{24,248},{32,0},{40,8},{48,16},{56,24},{6... | collective-permute-start | bytes 786440 | tf_op jit(solution)/shard_map/ppermute | solution.py:416
  8.9 6.1 %collective-permute-start.3 = (bf16[2,512,128]{2,1,0:T(8,128)(2,1)S(1)}, bf16[2,512,128]{2,1,0:T(8,128)(2,1)}, u32[]{:S(2)}, u32[]{:S(2)}) collective-permute-start(bf16[2,512,128]{2,1,0:T(8,128)(2,1)S(1)} %get-tuple-element.75), channel_id=1, source_target_pairs={{0,8},{8,0},{16,24},{24,16},{32,40},{40,32},{48,56},{56,48},{64,72... | collective-permute-start | bytes 786440 | tf_op jit(solution)/shard_map/ppermute | solution.py:404
  8.9 10.9 %collective-permute-start = (bf16[256,640]{1,0:T(8,128)(2,1)}, bf16[256,640]{1,0:T(8,128)(2,1)S(1)}, u32[]{:S(2)}, u32[]{:S(2)}) collective-permute-start(bf16[256,640]{1,0:T(8,128)(2,1)} %q_in.1), channel_id=1, source_target_pairs={{0,8},{8,0},{16,24},{24,16},{32,40},{40,32},{48,56},{56,48},{64,72... | collective-permute-start | bytes 983048 | tf_op jit(solution)/shard_map/ppermute | solution.py:407
  12.1 50.8 %collective-permute-start.21 = (bf16[640,1280]{1,0:T(8,128)(2,1)}, bf16[640,1280]{1,0:T(8,128)(2,1)S(1)}, u32[]{:S(2)}, u32[]{:S(2)}) collective-permute-start(bf16[640,1280]{1,0:T(8,128)(2,1)} %constant_dynamic-slice_fusion), channel_id=1, source_target_pairs={{0,4},{1,5},{2,6},{3,7},{4,0},{5,1},{6,2},{7,3},{8,12},{9,13},{10,... | collective-permute-start | bytes 4915208 | tf_op jit(solution)/shard_map/ppermute | solution.py:400
  15.0 44.5 %collective-permute-start.1 = (bf16[256,640]{1,0:T(8,128)(2,1)S(1)}, bf16[256,640]{1,0:T(8,128)(2,1)S(1)}, u32[]{:S(2)}, u32[]{:S(2)}) collective-permute-start(bf16[256,640]{1,0:T(8,128)(2,1)S(1)} %copy-done), channel_id=1, source_target_pairs={{0,16},{8,24},{16,0},{24,8},{32,48},{40,56},{48,32},{56,40},{64,80... | collective-permute-start | bytes 983048 | tf_op jit(solution)/shard_map/ppermute | solution.py:407
  16.5 43.0 %collective-permute-start.7 = (bf16[2,512,128]{2,1,0:T(8,128)(2,1)}, bf16[2,512,128]{2,1,0:T(8,128)(2,1)}, u32[]{:S(2)}, u32[]{:S(2)}) collective-permute-start(bf16[2,512,128]{2,1,0:T(8,128)(2,1)} %collective-permute-done.3.rest_1_), channel_id=1, source_target_pairs={{0,224},{8,232},{16,240},{24,248},{32,0},{40,8},{48,16},{56,24},{6... | collective-permute-start | bytes 786440 | tf_op jit(solution)/shard_map/ppermute | solution.py:416
  19.7 0.7 copy-start.1
  19.7 45.0 %collective-permute-start.2 = (bf16[256,640]{1,0:T(8,128)(2,1)S(1)}, bf16[256,640]{1,0:T(8,128)(2,1)}, u32[]{:S(2)}, u32[]{:S(2)}) collective-permute-start(bf16[256,640]{1,0:T(8,128)(2,1)S(1)} %copy-done), channel_id=1, source_target_pairs={{0,24},{8,16},{16,8},{24,0},{32,56},{40,48},{48,40},{56,32},{64,88... | collective-permute-start | bytes 983048 | tf_op jit(solution)/shard_map/ppermute | solution.py:407
  19.8 46.9 %collective-permute-start.6 = (bf16[2,512,128]{2,1,0:T(8,128)(2,1)}, bf16[2,512,128]{2,1,0:T(8,128)(2,1)}, u32[]{:S(2)}, u32[]{:S(2)}) collective-permute-start(bf16[2,512,128]{2,1,0:T(8,128)(2,1)} %collective-permute-done.3.rest_1_), channel_id=1, source_target_pairs={{0,32},{8,40},{16,48},{24,56},{32,64},{40,72},{48,80},{56,88},{64,... | collective-permute-start | bytes 786440 | tf_op jit(solution)/shard_map/ppermute | solution.py:415
  59.5 7.8 %collective-permute-start.8 = (bf16[2,512,128]{2,1,0:T(8,128)(2,1)}, bf16[2,512,128]{2,1,0:T(8,128)(2,1)S(1)}, u32[]{:S(2)}, u32[]{:S(2)}) collective-permute-start(bf16[2,512,128]{2,1,0:T(8,128)(2,1)} %collective-permute-done.4.rest_2_), channel_id=1, source_target_pairs={{0,32},{8,40},{16,48},{24,56},{32,64},{40,72},{48,80},{56,88},{64,... | collective-permute-start | bytes 786440 | tf_op jit(solution)/shard_map/ppermute | solution.py:415
  59.5 7.8 %collective-permute-start.11 = (bf16[2,512,128]{2,1,0:T(8,128)(2,1)}, bf16[2,512,128]{2,1,0:T(8,128)(2,1)S(1)}, u32[]{:S(2)}, u32[]{:S(2)}) collective-permute-start(bf16[2,512,128]{2,1,0:T(8,128)(2,1)} %collective-permute-done.7.rest_5_), channel_id=1, source_target_pairs={{0,224},{8,232},{16,240},{24,248},{32,0},{40,8},{48,16},{56,24},{6... | collective-permute-start | bytes 786440 | tf_op jit(solution)/shard_map/ppermute | solution.py:416
  63.0 68.2 %collective-permute-start.22 = (bf16[640,1280]{1,0:T(8,128)(2,1)S(1)}, bf16[640,1280]{1,0:T(8,128)(2,1)S(1)}, u32[]{:S(2)}, u32[]{:S(2)}) collective-permute-start(bf16[640,1280]{1,0:T(8,128)(2,1)S(1)} %collective-permute-done.21.mine_in), channel_id=1, source_target_pairs={{0,8},{8,0},{16,24},{24,16},{32,40},{40,32},{48,56},{56,48},{64,72... | collective-permute-start | bytes 4915208 | tf_op jit(solution)/shard_map/ppermute | solution.py:578
  64.7 9.4 %collective-permute-start.9 = (bf16[2,512,128]{2,1,0:T(8,128)(2,1)}, bf16[2,512,128]{2,1,0:T(8,128)(2,1)S(1)}, u32[]{:S(2)}, u32[]{:S(2)}) collective-permute-start(bf16[2,512,128]{2,1,0:T(8,128)(2,1)} %copy-done.1), channel_id=1, source_target_pairs={{0,224},{8,232},{16,240},{24,248},{32,0},{40,8},{48,16},{56,24},{6... | collective-permute-start | bytes 786440 | tf_op jit(solution)/shard_map/ppermute | solution.py:416
  66.7 10.6 %collective-permute-start.10 = (bf16[2,512,128]{2,1,0:T(8,128)(2,1)}, bf16[2,512,128]{2,1,0:T(8,128)(2,1)S(1)}, u32[]{:S(2)}, u32[]{:S(2)}) collective-permute-start(bf16[2,512,128]{2,1,0:T(8,128)(2,1)} %collective-permute-done.6.rest_4_), channel_id=1, source_target_pairs={{0,32},{8,40},{16,48},{24,56},{32,64},{40,72},{48,80},{56,88},{64,... | collective-permute-start | bytes 786440 | tf_op jit(solution)/shard_map/ppermute | solution.py:415
  67.4 15.5 %collective-permute-start.12 = (bf16[2,512,128]{2,1,0:T(8,128)(2,1)S(1)}, bf16[2,512,128]{2,1,0:T(8,128)(2,1)S(1)}, u32[]{:S(2)}, u32[]{:S(2)}) collective-permute-start(bf16[2,512,128]{2,1,0:T(8,128)(2,1)S(1)} %collective-permute-done.8.rest_0_), channel_id=1, source_target_pairs={{0,32},{8,40},{16,48},{24,56},{32,64},{40,72},{48,80},{56,88},{64,... | collective-permute-start | bytes 786440 | tf_op jit(solution)/shard_map/ppermute | solution.py:415
  67.4 15.5 %collective-permute-start.15 = (bf16[2,512,128]{2,1,0:T(8,128)(2,1)S(1)}, bf16[2,512,128]{2,1,0:T(8,128)(2,1)S(1)}, u32[]{:S(2)}, u32[]{:S(2)}) collective-permute-start(bf16[2,512,128]{2,1,0:T(8,128)(2,1)S(1)} %collective-permute-done.11.rest_3_), channel_id=1, source_target_pairs={{0,224},{8,232},{16,240},{24,248},{32,0},{40,8},{48,16},{56,24},{6... | collective-permute-start | bytes 786440 | tf_op jit(solution)/shard_map/ppermute | solution.py:416
  74.1 31.0 %collective-permute-start.13 = (bf16[2,512,128]{2,1,0:T(8,128)(2,1)S(1)}, bf16[2,512,128]{2,1,0:T(8,128)(2,1)S(1)}, u32[]{:S(2)}, u32[]{:S(2)}) collective-permute-start(bf16[2,512,128]{2,1,0:T(8,128)(2,1)S(1)} %collective-permute-done.9.rest_1_), channel_id=1, source_target_pairs={{0,224},{8,232},{16,240},{24,248},{32,0},{40,8},{48,16},{56,24},{6... | collective-permute-start | bytes 786440 | tf_op jit(solution)/shard_map/ppermute | solution.py:416
  77.3 27.9 %collective-permute-start.14 = (bf16[2,512,128]{2,1,0:T(8,128)(2,1)S(1)}, bf16[2,512,128]{2,1,0:T(8,128)(2,1)S(1)}, u32[]{:S(2)}, u32[]{:S(2)}) collective-permute-start(bf16[2,512,128]{2,1,0:T(8,128)(2,1)S(1)} %collective-permute-done.10.rest_2_), channel_id=1, source_target_pairs={{0,32},{8,40},{16,48},{24,56},{32,64},{40,72},{48,80},{56,88},{64,... | collective-permute-start | bytes 786440 | tf_op jit(solution)/shard_map/ppermute | solution.py:415
  82.9 27.3 %collective-permute-start.16 = (bf16[2,512,128]{2,1,0:T(8,128)(2,1)S(1)}, bf16[2,512,128]{2,1,0:T(8,128)(2,1)S(1)}, u32[]{:S(2)}, u32[]{:S(2)}) collective-permute-start(bf16[2,512,128]{2,1,0:T(8,128)(2,1)S(1)} %collective-permute-done.12.rest_0_), channel_id=1, source_target_pairs={{0,32},{8,40},{16,48},{24,56},{32,64},{40,72},{48,80},{56,88},{64,... | collective-permute-start | bytes 786440 | tf_op jit(solution)/shard_map/ppermute | solution.py:420
  82.9 27.3 %collective-permute-start.17 = (bf16[2,512,128]{2,1,0:T(8,128)(2,1)S(1)}, bf16[2,512,128]{2,1,0:T(8,128)(2,1)S(1)}, u32[]{:S(2)}, u32[]{:S(2)}) collective-permute-start(bf16[2,512,128]{2,1,0:T(8,128)(2,1)S(1)} %collective-permute-done.15.rest_3_), channel_id=1, source_target_pairs={{0,224},{8,232},{16,240},{24,248},{32,0},{40,8},{48,16},{56,24},{6... | collective-permute-start | bytes 786440 | tf_op jit(solution)/shard_map/ppermute | solution.py:422
  86.1 0.9 copy-start.2
  113.4 1.8 %collective-permute-start.18 = (bf16[2,688,128]{2,1,0:T(8,128)(2,1)S(1)}, bf16[2,688,128]{2,1,0:T(8,128)(2,1)S(1)}, u32[]{:S(2)}, u32[]{:S(2)}) collective-permute-start(bf16[2,688,128]{2,1,0:T(8,128)(2,1)S(1)} %get-tuple-element.52), channel_id=1, source_target_pairs={{0,8},{8,0},{16,24},{24,16},{32,40},{40,32},{48,56},{56,48},{64,72... | collective-permute-start | bytes 1056776 | tf_op jit(solution)/shard_map/ppermute | solution.py:551
  113.5 2.2 %collective-permute-start.26 = (bf16[2,688,128]{2,1,0:T(8,128)(2,1)S(1)}, bf16[2,688,128]{2,1,0:T(8,128)(2,1)S(1)}, u32[]{:S(2)}, u32[]{:S(2)}) collective-permute-start(bf16[2,688,128]{2,1,0:T(8,128)(2,1)S(1)} %get-tuple-element.61), channel_id=1, source_target_pairs={{0,8},{8,0},{16,24},{24,16},{32,40},{40,32},{48,56},{56,48},{64,72... | collective-permute-start | bytes 1056776 | tf_op jit(solution)/shard_map/ppermute | solution.py:551
  115.2 7.4 %collective-permute-start.19 = (bf16[688,128]{1,0:T(8,128)(2,1)S(1)}, bf16[688,128]{1,0:T(8,128)(2,1)S(1)}, u32[]{:S(2)}, u32[]{:S(2)}) collective-permute-start(bf16[688,128]{1,0:T(8,128)(2,1)S(1)} %merge.2), channel_id=1, source_target_pairs={{0,16},{8,24},{16,0},{24,8},{32,48},{40,56},{48,32},{56,40},{64,80... | collective-permute-start | bytes 528392 | tf_op jit(solution)/shard_map/ppermute | solution.py:563
  115.7 10.7 %collective-permute-start.27 = (bf16[688,128]{1,0:T(8,128)(2,1)S(1)}, bf16[688,128]{1,0:T(8,128)(2,1)S(1)}, u32[]{:S(2)}, u32[]{:S(2)}) collective-permute-start(bf16[688,128]{1,0:T(8,128)(2,1)S(1)} %merge.3), channel_id=1, source_target_pairs={{0,16},{8,24},{16,0},{24,8},{32,48},{40,56},{48,32},{56,40},{64,80... | collective-permute-start | bytes 528392 | tf_op jit(solution)/shard_map/ppermute | solution.py:563
  123.3 7.8 %collective-permute-start.20 = (bf16[128,640]{1,0:T(8,128)(2,1)S(1)}, bf16[128,640]{1,0:T(8,128)(2,1)S(1)}, u32[]{:S(2)}, u32[]{:S(2)}) collective-permute-start(bf16[128,640]{1,0:T(8,128)(2,1)S(1)} %combine.2.attn_near), channel_id=1, source_target_pairs={{0,4},{1,5},{2,6},{3,7},{4,0},{5,1},{6,2},{7,3},{8,12},{9,13},{10,... | collective-permute-start | bytes 491528 | tf_op jit(solution)/shard_map/ppermute | solution.py:577
  127.1 14.1 %collective-permute-start.28 = (bf16[128,640]{1,0:T(8,128)(2,1)S(1)}, bf16[128,640]{1,0:T(8,128)(2,1)S(1)}, u32[]{:S(2)}, u32[]{:S(2)}) collective-permute-start(bf16[128,640]{1,0:T(8,128)(2,1)S(1)} %combine.3.attn_near), channel_id=1, source_target_pairs={{0,4},{1,5},{2,6},{3,7},{4,0},{5,1},{6,2},{7,3},{8,12},{9,13},{10,... | collective-permute-start | bytes 491528 | tf_op jit(solution)/shard_map/ppermute | solution.py:577
  131.2 1.2 copy-start.5
  136.4 12.8 %collective-permute-start.23 = (bf16[128,640]{1,0:T(8,128)(2,1)S(1)}, bf16[128,640]{1,0:T(8,128)(2,1)S(1)}, u32[]{:S(2)}, u32[]{:S(2)}) collective-permute-start(bf16[128,640]{1,0:T(8,128)(2,1)S(1)} %get-tuple-element.56), channel_id=1, source_target_pairs={{0,1},{1,0},{2,3},{3,2},{4,5},{5,4},{6,7},{7,6},{8,9},{9,8},{10,11... | collective-permute-start | bytes 491528 | tf_op jit(solution)/shard_map/ppermute | solution.py:604
  138.1 11.9 %collective-permute-start.24 = (bf16[128,640]{1,0:T(8,128)(2,1)S(1)}, bf16[128,640]{1,0:T(8,128)(2,1)S(1)}, u32[]{:S(2)}, u32[]{:S(2)}) collective-permute-start(bf16[128,640]{1,0:T(8,128)(2,1)S(1)} %get-tuple-element.57), channel_id=1, source_target_pairs={{0,2},{1,3},{2,0},{3,1},{4,6},{5,7},{6,4},{7,5},{8,10},{9,11},{10,... | collective-permute-start | bytes 491528 | tf_op jit(solution)/shard_map/ppermute | solution.py:604
  140.7 9.3 %collective-permute-start.25 = (bf16[128,640]{1,0:T(8,128)(2,1)S(1)}, bf16[128,640]{1,0:T(8,128)(2,1)S(1)}, u32[]{:S(2)}, u32[]{:S(2)}) collective-permute-start(bf16[128,640]{1,0:T(8,128)(2,1)S(1)} %get-tuple-element.58), channel_id=1, source_target_pairs={{0,3},{1,2},{2,1},{3,0},{4,7},{5,6},{6,5},{7,4},{8,11},{9,10},{10,... | collective-permute-start | bytes 491528 | tf_op jit(solution)/shard_map/ppermute | solution.py:604
  145.2 16.1 %copy-start.7 = (bf16[640]{0:T(1024)(128)(2,1)S(1)}, bf16[640]{0:T(1024)(128)(2,1)}, u32[]{:S(2)}) copy-start(bf16[640]{0:T(1024)(128)(2,1)} %param.21) | copy-start | bytes 3844
  145.2 5.4 %collective-permute-start.29 = (bf16[128,640]{1,0:T(8,128)(2,1)S(1)}, bf16[128,640]{1,0:T(8,128)(2,1)S(1)}, u32[]{:S(2)}, u32[]{:S(2)}) collective-permute-start(bf16[128,640]{1,0:T(8,128)(2,1)S(1)} %get-tuple-element.65), channel_id=1, source_target_pairs={{0,1},{1,0},{2,3},{3,2},{4,5},{5,4},{6,7},{7,6},{8,9},{9,8},{10,11... | collective-permute-start | bytes 491528 | tf_op jit(solution)/shard_map/ppermute | solution.py:604
  145.6 8.6 %collective-permute-start.30 = (bf16[128,640]{1,0:T(8,128)(2,1)S(1)}, bf16[128,640]{1,0:T(8,128)(2,1)S(1)}, u32[]{:S(2)}, u32[]{:S(2)}) collective-permute-start(bf16[128,640]{1,0:T(8,128)(2,1)S(1)} %get-tuple-element.66), channel_id=1, source_target_pairs={{0,2},{1,3},{2,0},{3,1},{4,6},{5,7},{6,4},{7,5},{8,10},{9,11},{10,... | collective-permute-start | bytes 491528 | tf_op jit(solution)/shard_map/ppermute | solution.py:604
  149.1 6.8 %collective-permute-start.31 = (bf16[128,640]{1,0:T(8,128)(2,1)S(1)}, bf16[128,640]{1,0:T(8,128)(2,1)S(1)}, u32[]{:S(2)}, u32[]{:S(2)}) collective-permute-start(bf16[128,640]{1,0:T(8,128)(2,1)S(1)} %get-tuple-element.67), channel_id=1, source_target_pairs={{0,3},{1,2},{2,1},{3,0},{4,7},{5,6},{6,5},{7,4},{8,11},{9,10},{10,... | collective-permute-start | bytes 491528 | tf_op jit(solution)/shard_map/ppermute | solution.py:604
  157.2 12.6 %copy-start.6 = (bf16[256,640]{1,0:T(8,128)(2,1)}, bf16[256,640]{1,0:T(8,128)(2,1)S(1)}, u32[]{:S(2)}) copy-start(bf16[256,640]{1,0:T(8,128)(2,1)S(1)} %get-tuple-element.74) | copy-start | bytes 983044
  157.9 11.0 %all-to-all-start = ((f32[8,8,128]{2,1,0:T(8,128)}), f32[8,8,128]{2,1,0:T(8,128)S(1)}, u32[]{:S(2)}, u32[]{:S(2)}) async-start(f32[8,8,128]{2,1,0:T(8,128)} %broadcast_in_dim.88), calls=%async_computation | async-start | bytes 65536 | tf_op jit(solution)/shard_map/all_to_all | solution.py:613

commit v2 on v1

--- a/solution.py
+++ b/solution.py
@@ -16,6 +16,7 @@
 LOG2E = 1.4426950408889634
 PATHS = (2, 3, 1, 0)
 FAR = 4
+LIMIT = 50
 
 
 SMEM = pltpu.SMEM
@@ -26,7 +27,7 @@
     return pl.BlockSpec(memory_space=space)
 
 
-def params(limit=26):
+def params(limit=18):
     return pltpu.CompilerParams(vmem_limit_bytes=limit * 1024 * 1024)
 
 
@@ -313,23 +314,36 @@
     return kernel
 
 
-def project_kernel(where, attn_near, attn_far, weight_in, mine_in, theirs_in, *rest):
+def near_kernel(where, attn_near, weight_in, *rest):
     paths = len(PATHS)
     outs = rest[:paths]
-    near_ref, far_ref, sems = rest[paths:]
+    near_ref, sems = rest[paths:]
     columns = near_ref.shape[2]
+    copies = {}
+    for k in PATHS:
+        at = pl.multiple_of((where[0] ^ k) * columns, HD)
+        copies[k] = pltpu.make_async_copy(
+            weight_in.at[:, pl.ds(at, columns)], near_ref.at[k], sems.at[k]
+        )
+        copies[k].start()
+    for k in PATHS:
+        copies[k].wait()
+        outs[k][...] = jnp.dot(attn_near[...], near_ref[k], preferred_element_type=jnp.float32)
+
+
+def far_kernel(where, attn_far, mine_in, theirs_in, *rest):
+    paths = len(PATHS)
+    sums = rest[:paths]
+    outs = rest[paths : 2 * paths]
+    far_ref, sems = rest[2 * paths :]
+    columns = far_ref.shape[2]
     tensor, core = where[0], where[1]
-
-    def copy_near(k):
-        at = pl.multiple_of((tensor ^ k) * columns, HD)
-        return pltpu.make_async_copy(weight_in.at[:, pl.ds(at, columns)], near_ref.at[k], sems.at[0, k])
 
     def copy_far(k, source):
         at = pl.multiple_of(((tensor ^ k) % 2) * columns, HD)
-        return pltpu.make_async_copy(source.at[:, pl.ds(at, columns)], far_ref.at[k], sems.at[1, k])
+        return pltpu.make_async_copy(source.at[:, pl.ds(at, columns)], far_ref.at[k], sems.at[k])
 
     for k in PATHS:
-        copy_near(k).start()
         same = ((tensor ^ k) % FAR) // 2 == core
 
         @pl.when(same)
@@ -341,10 +355,10 @@
             copy_far(k, theirs_in).start()
 
     for k in PATHS:
-        copy_near(k).wait()
         copy_far(k, mine_in).wait()
-        total = jnp.dot(attn_near[...], near_ref[k], preferred_element_type=jnp.float32)
-        total = total + jnp.dot(attn_far[...], far_ref[k], preferred_element_type=jnp.float32)
+        total = sums[k][...] + jnp.dot(
+            attn_far[...], far_ref[k], preferred_element_type=jnp.float32
+        )
         outs[k][...] = total.astype(outs[k].dtype)
 
 
@@ -398,10 +412,16 @@
         out_weight, (far_side * FAR + 2 * core) * columns, 2 * columns, 1
     )
     weight_mine = lax.ppermute(outgoing, "tp", [(i, i ^ FAR) for i in range(ways)])
-    both = jnp.concatenate([prefix_key, prefix_value], axis=0)
-    mine = lax.dynamic_slice_in_dim(both, core * part, part, 1)
-    theirs = lax.dynamic_slice_in_dim(both, (1 - core) * part, part, 1)
-    lanes = [mine, lax.ppermute(theirs, "req", beside(1))]
+
+    def half(which):
+        cut = [
+            lax.dynamic_slice_in_dim(x, which * part, part, 1) for x in (prefix_key, prefix_value)
+        ]
+        return jnp.concatenate(cut, axis=0)
+
+    theirs = half(1 - core)
+    swapped_half = lax.ppermute(theirs, "req", beside(1))
+    lanes = [half(core), swapped_half]
     queries = []
     for k in range(1, PLANE):
         queries.append(lax.ppermute(suffix_query, "req", beside(k)))
@@ -578,27 +598,42 @@
     weight_theirs = lax.ppermute(weight_mine, "req", beside(1))
     shared = []
     paths = len(PATHS)
+    estimate = pl.CostEstimate(
+        flops=TILE * heads * HD * width, bytes_accessed=4 << 20, transcendentals=0
+    )
+    begun = []
+    for j in range(tiles_each):
+        begun.append(
+            pl.pallas_call(
+                near_kernel,
+                out_shape=(shape((TILE, columns), f32),) * paths,
+                in_specs=[full(SMEM), full(), full(pl.ANY)],
+                out_specs=(full(),) * paths,
+                scratch_shapes=[
+                    pltpu.VMEM((paths, heads * HD, columns), bf16),
+                    pltpu.SemaphoreType.DMA((paths,)),
+                ],
+                cost_estimate=estimate,
+                compiler_params=params(LIMIT),
+                name="near",
+            )(where, near[j], out_weight)
+        )
     for j in range(tiles_each):
         pieces = pl.pallas_call(
-            project_kernel,
+            far_kernel,
             out_shape=tuple(
                 shape((TILE, columns), bf16 if k else f32) for k in range(paths)
             ),
-            in_specs=[full(SMEM), full(), full()] + [full(pl.ANY)] * 3,
+            in_specs=[full(SMEM), full()] + [full(pl.ANY)] * 2 + [full()] * paths,
             out_specs=(full(),) * paths,
             scratch_shapes=[
                 pltpu.VMEM((paths, heads * HD, columns), bf16),
-                pltpu.VMEM((paths, heads * HD, columns), bf16),
-                pltpu.SemaphoreType.DMA((2, paths)),
+                pltpu.SemaphoreType.DMA((paths,)),
             ],
-            cost_estimate=pl.CostEstimate(
-                flops=2 * TILE * heads * HD * width,
-                bytes_accessed=8 << 20,
-                transcendentals=0,
-            ),
-            compiler_params=params(50),
+            cost_estimate=estimate,
+            compiler_params=params(16),
             name="project",
-        )(where, near[j], far[j], out_weight, weight_mine, weight_theirs)
+        )(where, far[j], weight_mine, weight_theirs, *begun[j])
         total = pieces[0]
         for k in range(1, paths):
             piece = lax.ppermute(pieces[k], "tp", [(i, i ^ k) for i in range(ways)])

time: 170 us -> 175 us (1.029)
  waiting for transfers between devices: 73.3 us -> 68 us
  Pallas kernels: 37.3 us -> 41.9 us
  local copies, waits for them, and re-layouts: 8.28 us -> 12.4 us
    unnamed x29 -> x40, local copies, waits for them, and re-layouts: 3.75 us -> 7.76 us
    pallas_call x2 -> x4, Pallas kernels: 7.96 us -> 11.4 us  [the longest x2 6.03 us: shards(): pl.pallas_call(near_kernel, out_shape=(shape((TILE, columns), f32),) * pa...]
    ppermute x2, waiting for transfers between devices: 3.1 us -> 0.08 us  [shards(): far.append(lax.ppermute(attn, 'tp', [(i, i ^ FAR) for i in range(ways)]))]
    ppermute x6, starting transfers between devices: 17.5 us -> 15.4 us  [shards(): moving_down = lax.ppermute(moving_down, 'req', down_pairs)]
  transfers between devices with their start and end apart: 33 -> 33, of which waited for: 14 -> 12; matrix products, arithmetic and copies ran while one was open for 4% -> 4% of each run, Pallas kernels for 22% -> 24%
where the time goes in v2:
time: 175 us; the launch traced here: 174 us
  waiting for transfers between devices  68 us (39%)
  starting transfers between devices  44 us (25%)
  Pallas kernels  41.9 us (24%)
  local copies, waits for them, and re-layouts  12.4 us (7%)
  other arithmetic  6.76 us (4%)
    ppermute x3, waiting for transfers between devices, shards(): queries.append(lax.ppermute(suffix_query, 'req', beside(k)))  40 us
    ppermute x6, starting transfers between devices, shards(): moving_down = lax.ppermute(moving_down, 'req', down_pairs)  15.4 us
    pallas_call x1, Pallas kernels, shards(): pl.pallas_call(make_first(base, len(parts)), out_shape=(shape((every, lin...  13.1 us
    pallas_call x2, Pallas kernels, shards(): pl.pallas_call(make_middle(base, len(parts)), out_shape=state_shapes, in_...  10.6 us
    ppermute x6, starting transfers between devices, shards(): piece = lax.ppermute(pieces[k], 'tp', [(i, i ^ k) for i in range(ways)])  9.48 us
    unnamed x40, local copies, waits for them, and re-layouts  7.76 us
    all_to_all x1, waiting for transfers between devices, shards(): lax.all_to_all(jnp.broadcast_to(squares[None], (ways, 8, HD)), 'tp', 0, 0)  7.75 us
    ppermute x2, waiting for transfers between devices, shards(): crossed.append(lax.ppermute(merged, 'req', beside(2)))  7.4 us
  transfers between devices with their start and end apart: 33, of which 12 were waited for; matrix products, arithmetic and copies ran while one was open for 4% of the time, Pallas kernels for 24%

profile of v2, /device:TPU:2, one launch (start us, length us, event | category | flops | bytes accessed | tf_op | source)
XLA Modules:
  0.0 174.2 jit_solution(13853352576328955482)
XLA Ops:
  0.7 1.2 constant_dynamic-slice_fusion.1
  1.9 2.0 %collective-permute-start.4 = (bf16[2,512,128]{2,1,0:T(8,128)(2,1)S(1)}, bf16[2,512,128]{2,1,0:T(8,128)(2,1)}, u32[]{:S(2)}, u32[]{:S(2)}) collective-permute-start(bf16[2,512,128]{2,1,0:T(8,128)(2,1)S(1)} %pad_maximum_fusion.rest_0_), channel_id=1, source_target_pairs={{0,32},{8,40},{16,48},{24,56},{32,64},{40,72},{48,80},{56,88},{64,... | collective-permute-start | bytes 786440 | tf_op jit(solution)/shard_map/ppermute | solution.py:435
  3.9 4.0 %collective-permute-start.5 = (bf16[2,512,128]{2,1,0:T(8,128)(2,1)S(1)}, bf16[2,512,128]{2,1,0:T(8,128)(2,1)S(1)}, u32[]{:S(2)}, u32[]{:S(2)}) collective-permute-start(bf16[2,512,128]{2,1,0:T(8,128)(2,1)S(1)} %pad_maximum_fusion.rest_0_), channel_id=1, source_target_pairs={{0,224},{8,232},{16,240},{24,248},{32,0},{40,8},{48,16},{56,24},{6... | collective-permute-start | bytes 786440 | tf_op jit(solution)/shard_map/ppermute | solution.py:436
  8.1 0.5 collective-permute-start
  8.6 2.7 %constant_dynamic-slice_fusion = bf16[640,1280]{1,0:T(8,128)(2,1)} fusion(bf16[640,5120]{1,0:T(8,128)(2,1)} %weight_in.3, s32[]{:T(128)S(6)} %select_n.89), kind=kLoop, calls=%fused_computation.32 | loop fusion | bytes 3276804 | tf_op jit(solution)/shard_map/dynamic_slice | solution.py:411
  11.3 2.1 %collective-permute-start.21 = (bf16[640,1280]{1,0:T(8,128)(2,1)}, bf16[640,1280]{1,0:T(8,128)(2,1)S(1)}, u32[]{:S(2)}, u32[]{:S(2)}) collective-permute-start(bf16[640,1280]{1,0:T(8,128)(2,1)} %constant_dynamic-slice_fusion), channel_id=1, source_target_pairs={{0,4},{1,5},{2,6},{3,7},{4,0},{5,1},{6,2},{7,3},{8,12},{9,13},{10,... | collective-permute-start | bytes 4915208 | tf_op jit(solution)/shard_map/ppermute | solution.py:414
  13.6 0.2 select_reduce_fusion.3
  14.0 0.2 select_reduce_fusion.5
  14.2 1.5 collective-permute-start.1
  15.7 1.9 %collective-permute-start.7 = (bf16[2,512,128]{2,1,0:T(8,128)(2,1)}, bf16[2,512,128]{2,1,0:T(8,128)(2,1)}, u32[]{:S(2)}, u32[]{:S(2)}) collective-permute-start(bf16[2,512,128]{2,1,0:T(8,128)(2,1)} %collective-permute-done.3.rest_1_), channel_id=1, source_target_pairs={{0,224},{8,232},{16,240},{24,248},{32,0},{40,8},{48,16},{56,24},{6... | collective-permute-start | bytes 786440 | tf_op jit(solution)/shard_map/ppermute | solution.py:436
  17.7 1.3 fusion.4
  19.0 0.7 copy-done.4
  19.8 38.9 %collective-permute-done.1.q2 = bf16[256,640]{1,0:T(8,128)(2,1)S(1)} collective-permute-done((bf16[256,640]{1,0:T(8,128)(2,1)}, bf16[256,640]{1,0:T(8,128)(2,1)S(1)}, u32[]{:S(2)}, u32[]{:S(2)}) %collective-permute-start.1) | collective-permute-done | bytes 327712 | tf_op jit(solution)/shard_map/ppermute | solution.py:427
  58.8 0.7 copy-done.6
  59.5 3.2 %collective-permute-start.11 = (bf16[2,512,128]{2,1,0:T(8,128)(2,1)}, bf16[2,512,128]{2,1,0:T(8,128)(2,1)}, u32[]{:S(2)}, u32[]{:S(2)}) collective-permute-start(bf16[2,512,128]{2,1,0:T(8,128)(2,1)} %collective-permute-done.7.rest_5_), channel_id=1, source_target_pairs={{0,224},{8,232},{16,240},{24,248},{32,0},{40,8},{48,16},{56,24},{6... | collective-permute-start | bytes 786440 | tf_op jit(solution)/shard_map/ppermute | solution.py:436
  63.0 1.1 collective-permute-done.2.q3
  64.1 1.9 %collective-permute-start.9 = (bf16[2,512,128]{2,1,0:T(8,128)(2,1)}, bf16[2,512,128]{2,1,0:T(8,128)(2,1)S(1)}, u32[]{:S(2)}, u32[]{:S(2)}) collective-permute-start(bf16[2,512,128]{2,1,0:T(8,128)(2,1)} %copy-done.8), channel_id=1, source_target_pairs={{0,224},{8,232},{16,240},{24,248},{32,0},{40,8},{48,16},{56,24},{6... | collective-permute-start | bytes 786440 | tf_op jit(solution)/shard_map/ppermute | solution.py:436
  66.2 1.3 collective-permute-done.8.rest_0_
  67.5 3.2 %collective-permute-start.15 = (bf16[2,512,128]{2,1,0:T(8,128)(2,1)}, bf16[2,512,128]{2,1,0:T(8,128)(2,1)S(1)}, u32[]{:S(2)}, u32[]{:S(2)}) collective-permute-start(bf16[2,512,128]{2,1,0:T(8,128)(2,1)} %collective-permute-done.11.rest_3_), channel_id=1, source_target_pairs={{0,224},{8,232},{16,240},{24,248},{32,0},{40,8},{48,16},{56,24},{6... | collective-permute-start | bytes 786440 | tf_op jit(solution)/shard_map/ppermute | solution.py:436
  70.8 1.2 pad_maximum_fusion.2
  72.1 0.8 copy-done.10
  72.9 0.8 copy-done.11
  73.7 1.9 %own.1 = (bf16[2,640,128]{2,1,0:T(8,128)(2,1)S(1)}, bf16[256,128]{1,0:T(8,128)(2,1)}, f32[2,128,640]{2,1,0:T(8,128)S(1)}, f32[2,1,640]{2,1,0:T(1,128)S(1)}, f32[2,1,640]{2,1,0:T(1,128)S(1)}) custom-call(s32[72]{0:T(128)S(1)} %pad_add_fusion.1.meta, bf16[256,640]{1,0:T(8,128)(2,1)} %q_in.1, bf16[256,128]{1,0:T(8,128)(2,1)S(1)} %copy-done.10, ...), custom_call_target="tpu_custom_call" | custom-call | flops 335544320 | bytes 3145728 | tf_op jit(solution)/shard_map/own/pallas_call | solution.py:482
  75.7 1.0 collective-permute-start.13
  76.7 1.1 collective-permute-start.14
  77.8 4.5 %collective-permute-done.12.rest_0_ = bf16[2,512,128]{2,1,0:T(8,128)(2,1)S(1)} collective-permute-done((bf16[2,512,128]{2,1,0:T(8,128)(2,1)S(1)}, bf16[2,512,128]{2,1,0:T(8,128)(2,1)S(1)}, u32[]{:S(2)}, u32[]{:S(2)}) %collective-permute-start.12) | collective-permute-done | bytes 262176 | tf_op jit(solution)/shard_map/ppermute | solution.py:435
  82.3 3.2 %collective-permute-start.17 = (bf16[2,512,128]{2,1,0:T(8,128)(2,1)S(1)}, bf16[2,512,128]{2,1,0:T(8,128)(2,1)S(1)}, u32[]{:S(2)}, u32[]{:S(2)}) collective-permute-start(bf16[2,512,128]{2,1,0:T(8,128)(2,1)S(1)} %collective-permute-done.15.rest_3_), channel_id=1, source_target_pairs={{0,224},{8,232},{16,240},{24,248},{32,0},{40,8},{48,16},{56,24},{6... | collective-permute-start | bytes 786440 | tf_op jit(solution)/shard_map/ppermute | solution.py:442
  85.5 0.9 copy-done.3
  86.5 1.0 copy-done.5
  87.5 1.0 copy-done.7
  88.4 0.9 copy-done.9
  89.4 13.1 %first.1 = (bf16[9,640,128]{2,1,0:T(8,128)(2,1)S(1)}, f32[9,128,640]{2,1,0:T(8,128)S(1)}, f32[9,1,640]{2,1,0:T(1,128)S(1)}, f32[9,1,640]{2,1,0:T(1,128)S(1)}) custom-call(s32[72]{0:T(128)S(1)} %pad_add_fusion.1.meta, bf16[2,640,128]{2,1,0:T(8,128)(2,1)S(1)} %get-tuple-element.44.q_own, f32[2,128,640]{2,1,0:T(8,128)S(1)} %get-tuple-element.45.acc_own, ...), custom_call_target="tpu_custom_call" | custom-call | flops 2013265920 | bytes 8388608 | tf_op jit(solution)/shard_map/first/pallas_call | solution.py:520
  102.5 5.6 %middle.2 = (f32[9,128,640]{2,1,0:T(8,128)S(1)}, f32[9,1,640]{2,1,0:T(1,128)S(1)}, f32[9,1,640]{2,1,0:T(1,128)S(1)}) custom-call(s32[72]{0:T(128)S(1)} %pad_add_fusion.1.meta, bf16[9,640,128]{2,1,0:T(8,128)(2,1)S(1)} %get-tuple-element.48.q_ref, f32[9,128,640]{2,1,0:T(8,128)S(1)} %get-tuple-element.49.acc_in, f32[9,1,640]{2,1,0:T(1,128)S(1)} %get-tuple-element.50.max_in, ...), custom_call_target="tpu_custom_call" | custom-call | flops 1342177280 | bytes 8388608 | tf_op jit(solution)/shard_map/middle/pallas_call | solution.py:533
  108.1 5.0 %middle.3 = (f32[9,128,640]{2,1,0:T(8,128)S(1)}, f32[9,1,640]{2,1,0:T(1,128)S(1)}, f32[9,1,640]{2,1,0:T(1,128)S(1)}) custom-call(s32[72]{0:T(128)S(1)} %pad_add_fusion.1.meta, bf16[9,640,128]{2,1,0:T(8,128)(2,1)S(1)} %get-tuple-element.48.q_ref, f32[9,128,640]{2,1,0:T(8,128)S(1)} %get-tuple-element.52.acc_in, f32[9,1,640]{2,1,0:T(1,128)S(1)} %get-tuple-element.53.max_in, ...), custom_call_target="tpu_custom_call" | custom-call | flops 1342177280 | bytes 8388608 | tf_op jit(solution)/shard_map/middle/pallas_call | solution.py:533
  113.2 3.2 %last.1 = (f32[128,640]{1,0:T(8,128)S(1)}, f32[16,128]{1,0:T(8,128)S(1)}, f32[128,640]{1,0:T(8,128)S(1)}, f32[16,128]{1,0:T(8,128)S(1)}, bf16[2,688,128]{2,1,0:T...) custom-call(s32[72]{0:T(128)S(1)} %pad_add_fusion.1.meta, ...), custom_call_target="tpu_custom_call" | custom-call | flops 671088640 | bytes 8388608 | tf_op jit(solution)/shard_map/last/pallas_call | solution.py:546
  116.4 0.5 collective-permute-start.26
  116.9 1.2 collective-permute-done.18.swapped
  118.3 0.3 collective-permute-done.26.swapped
  118.7 1.8 %collective-permute-start.27 = (bf16[688,128]{1,0:T(8,128)(2,1)S(1)}, bf16[688,128]{1,0:T(8,128)(2,1)S(1)}, u32[]{:S(2)}, u32[]{:S(2)}) collective-permute-start(bf16[688,128]{1,0:T(8,128)(2,1)S(1)} %merge.3), channel_id=1, source_target_pairs={{0,16},{8,24},{16,0},{24,8},{32,48},{40,56},{48,32},{56,40},{64,80... | collective-permute-start | bytes 528392 | tf_op jit(solution)/shard_map/ppermute | solution.py:583
  120.5 5.1 %collective-permute-done.19.crossed = bf16[688,128]{1,0:T(8,128)(2,1)S(1)} collective-permute-done((bf16[688,128]{1,0:T(8,128)(2,1)S(1)}, bf16[688,128]{1,0:T(8,128)(2,1)S(1)}, u32[]{:S(2)}, u32[]{:S(2)}) %collective-permute-start.19) | collective-permute-done | bytes 176160 | tf_op jit(solution)/shard_map/ppermute | solution.py:583
  125.6 0.7 combine.2.attn_near
  126.3 0.7 collective-permute-start.20
  127.1 2.3 %collective-permute-done.27.crossed = bf16[688,128]{1,0:T(8,128)(2,1)S(1)} collective-permute-done((bf16[688,128]{1,0:T(8,128)(2,1)S(1)}, bf16[688,128]{1,0:T(8,128)(2,1)S(1)}, u32[]{:S(2)}, u32[]{:S(2)}) %collective-permute-start.27) | collective-permute-done | bytes 176160 | tf_op jit(solution)/shard_map/ppermute | solution.py:583
  129.4 0.7 combine.3.attn_near
  130.1 1.0 collective-permute-start.28
  131.1 3.0 %near.2 = (f32[128,640]{1,0:T(8,128)S(1)}, f32[128,640]{1,0:T(8,128)S(1)}, f32[128,640]{1,0:T(8,128)S(1)}, f32[128,640]{1,0:T(8,128)S(1)}) custom-call(s32[2]{0:T(128)S(1)} %pad_add_fusion.where, bf16[128,640]{1,0:T(8,128)(2,1)S(1)} %combine.2.attn_near, bf16[640,5120]{1,0:T(8,128)(2,1)} %weight_in.3), custom_call_target="tpu_custom_call" | custom-call | flops 419430400 | bytes 4194304 | tf_op jit(solution)/shard_map/near/pallas_call | solution.py:607
  134.2 2.7 %project.2 = (f32[128,640]{1,0:T(8,128)S(1)}, bf16[128,640]{1,0:T(8,128)(2,1)}, bf16[128,640]{1,0:T(8,128)(2,1)}, bf16[128,640]{1,0:T(8,128)(2,1)}) custom-call(s32[2]{0:T(128)S(1)} %pad_add_fusion.where, bf16[128,640]{1,0:T(8,128)(2,1)S(1)} %collective-permute-done.20.attn_far, bf16[640,1280]{1,0:T(8,128)(2,1)S(1)} %collective-permute-done.21.mine_in, ...), custom_call_target="tpu_custom_call" | custom-call | flops 419430400 | bytes 4194304 | tf_op jit(solution)/shard_map/project/pallas_call | solution.py:622
  136.9 0.7 copy-done
  137.6 1.6 collective-permute-start.23
  139.2 2.9 %collective-permute-start.24 = (bf16[128,640]{1,0:T(8,128)(2,1)}, bf16[128,640]{1,0:T(8,128)(2,1)}, u32[]{:S(2)}, u32[]{:S(2)}) collective-permute-start(bf16[128,640]{1,0:T(8,128)(2,1)} %get-tuple-element.69), channel_id=1, source_target_pairs={{0,2},{1,3},{2,0},{3,1},{4,6},{5,7},{6,4},{7,5},{8,10},{9,11},{10,... | collective-permute-start | bytes 491528 | tf_op jit(solution)/shard_map/ppermute | solution.py:639
  142.1 0.2 collective-permute-start.25
  142.3 3.0 %near.3 = (f32[128,640]{1,0:T(8,128)S(1)}, f32[128,640]{1,0:T(8,128)S(1)}, f32[128,640]{1,0:T(8,128)S(1)}, f32[128,640]{1,0:T(8,128)S(1)}) custom-call(s32[2]{0:T(128)S(1)} %pad_add_fusion.where, bf16[128,640]{1,0:T(8,128)(2,1)S(1)} %combine.3.attn_near, bf16[640,5120]{1,0:T(8,128)(2,1)} %weight_in.3), custom_call_target="tpu_custom_call" | custom-call | flops 419430400 | bytes 4194304 | tf_op jit(solution)/shard_map/near/pallas_call | solution.py:607
  145.4 2.7 %project.3 = (f32[128,640]{1,0:T(8,128)S(1)}, bf16[128,640]{1,0:T(8,128)(2,1)S(1)}, bf16[128,640]{1,0:T(8,128)(2,1)S(1)}, bf16[128,640]{1,0:T(8,128)(2,1)S(1)}) custom-call(s32[2]{0:T(128)S(1)} %pad_add_fusion.where, bf16[128,640]{1,0:T(8,128)(2,1)} %collective-permute-done.28.attn_far, bf16[640,1280]{1,0:T(8,128)(2,1)S(1)} %collective-permute-done.21.mine_in, ...), custom_call_target="tpu_custom_call" | custom-call | flops 419430400 | bytes 4194304 | tf_op jit(solution)/shard_map/project/pallas_call | solution.py:622
  148.1 0.4 collective-permute-start.29
  148.5 4.1 %collective-permute-start.30 = (bf16[128,640]{1,0:T(8,128)(2,1)S(1)}, bf16[128,640]{1,0:T(8,128)(2,1)S(1)}, u32[]{:S(2)}, u32[]{:S(2)}) collective-permute-start(bf16[128,640]{1,0:T(8,128)(2,1)S(1)} %get-tuple-element.82), channel_id=1, source_target_pairs={{0,2},{1,3},{2,0},{3,1},{4,6},{5,7},{6,4},{7,5},{8,10},{9,11},{10,... | collective-permute-start | bytes 491528 | tf_op jit(solution)/shard_map/ppermute | solution.py:639
  152.6 0.2 collective-permute-start.31
  152.9 1.1 convert_add_fusion.1
  154.0 3.7 %collective-permute-done.30 = bf16[128,640]{1,0:T(8,128)(2,1)S(1)} collective-permute-done((bf16[128,640]{1,0:T(8,128)(2,1)S(1)}, bf16[128,640]{1,0:T(8,128)(2,1)S(1)}, u32[]{:S(2)}, u32[]{:S(2)}) %collective-permute-start.30) | collective-permute-done | bytes 163872 | tf_op jit(solution)/shard_map/ppermute | solution.py:639
  157.7 1.7 collective-permute-done.31
  159.5 1.2 fusion
  160.7 0.7 broadcast_in_dim.88
  161.4 4.1 %all-to-all-start = ((f32[8,8,128]{2,1,0:T(8,128)}), f32[8,8,128]{2,1,0:T(8,128)S(1)}, u32[]{:S(2)}, u32[]{:S(2)}) async-start(f32[8,8,128]{2,1,0:T(8,128)} %broadcast_in_dim.88), calls=%async_computation | async-start | bytes 65536 | tf_op jit(solution)/shard_map/all_to_all | solution.py:648
  165.5 7.7 %all-to-all-done = f32[8,8,128]{2,1,0:T(8,128)S(1)} async-done(((f32[8,8,128]{2,1,0:T(8,128)}), f32[8,8,128]{2,1,0:T(8,128)S(1)}, u32[]{:S(2)}, u32[]{:S(2)}) %all-to-all-start) | async-done | bytes 32800 | tf_op jit(solution)/shard_map/all_to_all | solution.py:648
  173.3 0.9 fusion.2
  (84 shorter events, 1.7 us)
Async XLA Ops:
  0.7 12.8 %copy-start.19 = (s32[32]{0:T(128)S(1)}, s32[32]{0:T(128)}, u32[]{:S(2)}) copy-start(s32[32]{0:T(128)} %param.24) | copy-start | bytes 388
  0.7 12.9 %copy-start.17 = (s32[16]{0:T(128)S(1)}, s32[16]{0:T(128)}, u32[]{:S(2)}) copy-start(s32[16]{0:T(128)} %constant.122.clone) | copy-start | bytes 196
  0.7 12.9 %copy-start.18 = (s32[16]{0:T(128)S(1)}, s32[16]{0:T(128)}, u32[]{:S(2)}) copy-start(s32[16]{0:T(128)} %constant.123.clone) | copy-start | bytes 196
  0.7 13.1 %copy-start.14 = (s32[32]{0:T(128)S(1)}, s32[32]{0:T(128)}, u32[]{:S(2)}) copy-start(s32[32]{0:T(128)} %param.22) | copy-start | bytes 388
  0.7 13.1 %copy-start.15 = (s32[32]{0:T(128)S(1)}, s32[32]{0:T(128)}, u32[]{:S(2)}) copy-start(s32[32]{0:T(128)} %param.23) | copy-start | bytes 388
  0.7 13.1 %copy-start.16 = (s32[32,1]{0,1:T(1,128)S(1)}, s32[32,1]{0,1:T(1,128)}, u32[]{:S(2)}) copy-start(s32[32,1]{0,1:T(1,128)} %param.25) | copy-start | bytes 388
  1.9 61.0 %copy-start.2 = (bf16[2,512,128]{2,1,0:T(8,128)(2,1)}, bf16[2,512,128]{2,1,0:T(8,128)(2,1)S(1)}, u32[]{:S(2)}) copy-start(bf16[2,512,128]{2,1,0:T(8,128)(2,1)S(1)} %pad_maximum_fusion.rest_0_) | copy-start | bytes 786436
  1.9 13.8 %collective-permute-start.4 = (bf16[2,512,128]{2,1,0:T(8,128)(2,1)S(1)}, bf16[2,512,128]{2,1,0:T(8,128)(2,1)}, u32[]{:S(2)}, u32[]{:S(2)}) collective-permute-start(bf16[2,512,128]{2,1,0:T(8,128)(2,1)S(1)} %pad_maximum_fusion.rest_0_), channel_id=1, source_target_pairs={{0,32},{8,40},{16,48},{24,56},{32,64},{40,72},{48,80},{56,88},{64,... | collective-permute-start | bytes 786440 | tf_op jit(solution)/shard_map/ppermute | solution.py:435
  3.9 15.0 %collective-permute-start.5 = (bf16[2,512,128]{2,1,0:T(8,128)(2,1)S(1)}, bf16[2,512,128]{2,1,0:T(8,128)(2,1)S(1)}, u32[]{:S(2)}, u32[]{:S(2)}) collective-permute-start(bf16[2,512,128]{2,1,0:T(8,128)(2,1)S(1)} %pad_maximum_fusion.rest_0_), channel_id=1, source_target_pairs={{0,224},{8,232},{16,240},{24,248},{32,0},{40,8},{48,16},{56,24},{6... | collective-permute-start | bytes 786440 | tf_op jit(solution)/shard_map/ppermute | solution.py:436
  8.0 6.2 %collective-permute-start.3 = (bf16[2,512,128]{2,1,0:T(8,128)(2,1)S(1)}, bf16[2,512,128]{2,1,0:T(8,128)(2,1)}, u32[]{:S(2)}, u32[]{:S(2)}) collective-permute-start(bf16[2,512,128]{2,1,0:T(8,128)(2,1)S(1)} %pad_maximum_fusion.1), channel_id=1, source_target_pairs={{0,8},{8,0},{16,24},{24,16},{32,40},{40,32},{48,56},{56,48},{64,72... | collective-permute-start | bytes 786440 | tf_op jit(solution)/shard_map/ppermute | solution.py:423
  8.1 10.9 %collective-permute-start = (bf16[256,640]{1,0:T(8,128)(2,1)}, bf16[256,640]{1,0:T(8,128)(2,1)S(1)}, u32[]{:S(2)}, u32[]{:S(2)}) collective-permute-start(bf16[256,640]{1,0:T(8,128)(2,1)} %q_in.1), channel_id=1, source_target_pairs={{0,8},{8,0},{16,24},{24,16},{32,40},{40,32},{48,56},{56,48},{64,72... | collective-permute-start | bytes 983048 | tf_op jit(solution)/shard_map/ppermute | solution.py:427
  11.3 51.6 %collective-permute-start.21 = (bf16[640,1280]{1,0:T(8,128)(2,1)}, bf16[640,1280]{1,0:T(8,128)(2,1)S(1)}, u32[]{:S(2)}, u32[]{:S(2)}) collective-permute-start(bf16[640,1280]{1,0:T(8,128)(2,1)} %constant_dynamic-slice_fusion), channel_id=1, source_target_pairs={{0,4},{1,5},{2,6},{3,7},{4,0},{5,1},{6,2},{7,3},{8,12},{9,13},{10,... | collective-permute-start | bytes 4915208 | tf_op jit(solution)/shard_map/ppermute | solution.py:414
  14.2 44.6 %collective-permute-start.1 = (bf16[256,640]{1,0:T(8,128)(2,1)}, bf16[256,640]{1,0:T(8,128)(2,1)S(1)}, u32[]{:S(2)}, u32[]{:S(2)}) collective-permute-start(bf16[256,640]{1,0:T(8,128)(2,1)} %q_in.1), channel_id=1, source_target_pairs={{0,16},{8,24},{16,0},{24,8},{32,48},{40,56},{48,32},{56,40},{64,80... | collective-permute-start | bytes 983048 | tf_op jit(solution)/shard_map/ppermute | solution.py:427
  15.7 43.8 %collective-permute-start.7 = (bf16[2,512,128]{2,1,0:T(8,128)(2,1)}, bf16[2,512,128]{2,1,0:T(8,128)(2,1)}, u32[]{:S(2)}, u32[]{:S(2)}) collective-permute-start(bf16[2,512,128]{2,1,0:T(8,128)(2,1)} %collective-permute-done.3.rest_1_), channel_id=1, source_target_pairs={{0,224},{8,232},{16,240},{24,248},{32,0},{40,8},{48,16},{56,24},{6... | collective-permute-start | bytes 786440 | tf_op jit(solution)/shard_map/ppermute | solution.py:436
  19.0 43.9 %copy-start.8 = (bf16[2,512,128]{2,1,0:T(8,128)(2,1)}, bf16[2,512,128]{2,1,0:T(8,128)(2,1)S(1)}, u32[]{:S(2)}) copy-start(bf16[2,512,128]{2,1,0:T(8,128)(2,1)S(1)} %collective-permute-done.5.rest_3_) | copy-start | bytes 786436
  19.0 45.2 %collective-permute-start.2 = (bf16[256,640]{1,0:T(8,128)(2,1)}, bf16[256,640]{1,0:T(8,128)(2,1)}, u32[]{:S(2)}, u32[]{:S(2)}) collective-permute-start(bf16[256,640]{1,0:T(8,128)(2,1)} %q_in.1), channel_id=1, source_target_pairs={{0,24},{8,16},{16,8},{24,0},{32,56},{40,48},{48,40},{56,32},{64,88... | collective-permute-start | bytes 983048 | tf_op jit(solution)/shard_map/ppermute | solution.py:427
  19.0 0.8 copy-start.4
  19.7 46.4 %collective-permute-start.6 = (bf16[2,512,128]{2,1,0:T(8,128)(2,1)}, bf16[2,512,128]{2,1,0:T(8,128)(2,1)}, u32[]{:S(2)}, u32[]{:S(2)}) collective-permute-start(bf16[2,512,128]{2,1,0:T(8,128)(2,1)} %collective-permute-done.3.rest_1_), channel_id=1, source_target_pairs={{0,32},{8,40},{16,48},{24,56},{32,64},{40,72},{48,80},{56,88},{64,... | collective-permute-start | bytes 786440 | tf_op jit(solution)/shard_map/ppermute | solution.py:435
  58.8 0.7 copy-start.6
  59.5 8.0 %collective-permute-start.8 = (bf16[2,512,128]{2,1,0:T(8,128)(2,1)}, bf16[2,512,128]{2,1,0:T(8,128)(2,1)S(1)}, u32[]{:S(2)}, u32[]{:S(2)}) collective-permute-start(bf16[2,512,128]{2,1,0:T(8,128)(2,1)} %collective-permute-done.4.rest_2_), channel_id=1, source_target_pairs={{0,32},{8,40},{16,48},{24,56},{32,64},{40,72},{48,80},{56,88},{64,... | collective-permute-start | bytes 786440 | tf_op jit(solution)/shard_map/ppermute | solution.py:435
  59.5 8.0 %collective-permute-start.11 = (bf16[2,512,128]{2,1,0:T(8,128)(2,1)}, bf16[2,512,128]{2,1,0:T(8,128)(2,1)}, u32[]{:S(2)}, u32[]{:S(2)}) collective-permute-start(bf16[2,512,128]{2,1,0:T(8,128)(2,1)} %collective-permute-done.7.rest_5_), channel_id=1, source_target_pairs={{0,224},{8,232},{16,240},{24,248},{32,0},{40,8},{48,16},{56,24},{6... | collective-permute-start | bytes 786440 | tf_op jit(solution)/shard_map/ppermute | solution.py:436
  62.9 71.2 %collective-permute-start.22 = (bf16[640,1280]{1,0:T(8,128)(2,1)S(1)}, bf16[640,1280]{1,0:T(8,128)(2,1)S(1)}, u32[]{:S(2)}, u32[]{:S(2)}) collective-permute-start(bf16[640,1280]{1,0:T(8,128)(2,1)S(1)} %collective-permute-done.21.mine_in), channel_id=1, source_target_pairs={{0,8},{8,0},{16,24},{24,16},{32,40},{40,32},{48,56},{56,48},{64,72... | collective-permute-start | bytes 4915208 | tf_op jit(solution)/shard_map/ppermute | solution.py:598
  64.1 11.5 %collective-permute-start.9 = (bf16[2,512,128]{2,1,0:T(8,128)(2,1)}, bf16[2,512,128]{2,1,0:T(8,128)(2,1)S(1)}, u32[]{:S(2)}, u32[]{:S(2)}) collective-permute-start(bf16[2,512,128]{2,1,0:T(8,128)(2,1)} %copy-done.8), channel_id=1, source_target_pairs={{0,224},{8,232},{16,240},{24,248},{32,0},{40,8},{48,16},{56,24},{6... | collective-permute-start | bytes 786440 | tf_op jit(solution)/shard_map/ppermute | solution.py:436
  66.1 10.6 %collective-permute-start.10 = (bf16[2,512,128]{2,1,0:T(8,128)(2,1)}, bf16[2,512,128]{2,1,0:T(8,128)(2,1)S(1)}, u32[]{:S(2)}, u32[]{:S(2)}) collective-permute-start(bf16[2,512,128]{2,1,0:T(8,128)(2,1)} %collective-permute-done.6.rest_4_), channel_id=1, source_target_pairs={{0,32},{8,40},{16,48},{24,56},{32,64},{40,72},{48,80},{56,88},{64,... | collective-permute-start | bytes 786440 | tf_op jit(solution)/shard_map/ppermute | solution.py:435
  67.5 14.8 %collective-permute-start.12 = (bf16[2,512,128]{2,1,0:T(8,128)(2,1)S(1)}, bf16[2,512,128]{2,1,0:T(8,128)(2,1)S(1)}, u32[]{:S(2)}, u32[]{:S(2)}) collective-permute-start(bf16[2,512,128]{2,1,0:T(8,128)(2,1)S(1)} %collective-permute-done.8.rest_0_), channel_id=1, source_target_pairs={{0,32},{8,40},{16,48},{24,56},{32,64},{40,72},{48,80},{56,88},{64,... | collective-permute-start | bytes 786440 | tf_op jit(solution)/shard_map/ppermute | solution.py:435
  67.5 14.8 %collective-permute-start.15 = (bf16[2,512,128]{2,1,0:T(8,128)(2,1)}, bf16[2,512,128]{2,1,0:T(8,128)(2,1)S(1)}, u32[]{:S(2)}, u32[]{:S(2)}) collective-permute-start(bf16[2,512,128]{2,1,0:T(8,128)(2,1)} %collective-permute-done.11.rest_3_), channel_id=1, source_target_pairs={{0,224},{8,232},{16,240},{24,248},{32,0},{40,8},{48,16},{56,24},{6... | collective-permute-start | bytes 786440 | tf_op jit(solution)/shard_map/ppermute | solution.py:436
  72.0 0.8 copy-start.10
  72.9 0.8 copy-start.11
  75.7 32.4 %collective-permute-start.13 = (bf16[2,512,128]{2,1,0:T(8,128)(2,1)S(1)}, bf16[2,512,128]{2,1,0:T(8,128)(2,1)S(1)}, u32[]{:S(2)}, u32[]{:S(2)}) collective-permute-start(bf16[2,512,128]{2,1,0:T(8,128)(2,1)S(1)} %collective-permute-done.9.rest_1_), channel_id=1, source_target_pairs={{0,224},{8,232},{16,240},{24,248},{32,0},{40,8},{48,16},{56,24},{6... | collective-permute-start | bytes 786440 | tf_op jit(solution)/shard_map/ppermute | solution.py:436
  76.7 31.4 %collective-permute-start.14 = (bf16[2,512,128]{2,1,0:T(8,128)(2,1)S(1)}, bf16[2,512,128]{2,1,0:T(8,128)(2,1)S(1)}, u32[]{:S(2)}, u32[]{:S(2)}) collective-permute-start(bf16[2,512,128]{2,1,0:T(8,128)(2,1)S(1)} %collective-permute-done.10.rest_2_), channel_id=1, source_target_pairs={{0,32},{8,40},{16,48},{24,56},{32,64},{40,72},{48,80},{56,88},{64,... | collective-permute-start | bytes 786440 | tf_op jit(solution)/shard_map/ppermute | solution.py:435
  82.3 30.8 %collective-permute-start.16 = (bf16[2,512,128]{2,1,0:T(8,128)(2,1)S(1)}, bf16[2,512,128]{2,1,0:T(8,128)(2,1)S(1)}, u32[]{:S(2)}, u32[]{:S(2)}) collective-permute-start(bf16[2,512,128]{2,1,0:T(8,128)(2,1)S(1)} %collective-permute-done.12.rest_0_), channel_id=1, source_target_pairs={{0,32},{8,40},{16,48},{24,56},{32,64},{40,72},{48,80},{56,88},{64,... | collective-permute-start | bytes 786440 | tf_op jit(solution)/shard_map/ppermute | solution.py:440
  82.3 30.9 %collective-permute-start.17 = (bf16[2,512,128]{2,1,0:T(8,128)(2,1)S(1)}, bf16[2,512,128]{2,1,0:T(8,128)(2,1)S(1)}, u32[]{:S(2)}, u32[]{:S(2)}) collective-permute-start(bf16[2,512,128]{2,1,0:T(8,128)(2,1)S(1)} %collective-permute-done.15.rest_3_), channel_id=1, source_target_pairs={{0,224},{8,232},{16,240},{24,248},{32,0},{40,8},{48,16},{56,24},{6... | collective-permute-start | bytes 786440 | tf_op jit(solution)/shard_map/ppermute | solution.py:442
  85.5 0.9 copy-start.3
  86.5 1.0 copy-start.5
  87.5 1.0 copy-start.7
  88.4 0.9 copy-start.9
  116.3 1.8 %collective-permute-start.18 = (bf16[2,688,128]{2,1,0:T(8,128)(2,1)S(1)}, bf16[2,688,128]{2,1,0:T(8,128)(2,1)S(1)}, u32[]{:S(2)}, u32[]{:S(2)}) collective-permute-start(bf16[2,688,128]{2,1,0:T(8,128)(2,1)S(1)} %get-tuple-element.60), channel_id=1, source_target_pairs={{0,8},{8,0},{16,24},{24,16},{32,40},{40,32},{48,56},{56,48},{64,72... | collective-permute-start | bytes 1056776 | tf_op jit(solution)/shard_map/ppermute | solution.py:571
  116.4 2.2 %collective-permute-start.26 = (bf16[2,688,128]{2,1,0:T(8,128)(2,1)S(1)}, bf16[2,688,128]{2,1,0:T(8,128)(2,1)S(1)}, u32[]{:S(2)}, u32[]{:S(2)}) collective-permute-start(bf16[2,688,128]{2,1,0:T(8,128)(2,1)S(1)} %get-tuple-element.73), channel_id=1, source_target_pairs={{0,8},{8,0},{16,24},{24,16},{32,40},{40,32},{48,56},{56,48},{64,72... | collective-permute-start | bytes 1056776 | tf_op jit(solution)/shard_map/ppermute | solution.py:571
  118.2 7.4 %collective-permute-start.19 = (bf16[688,128]{1,0:T(8,128)(2,1)S(1)}, bf16[688,128]{1,0:T(8,128)(2,1)S(1)}, u32[]{:S(2)}, u32[]{:S(2)}) collective-permute-start(bf16[688,128]{1,0:T(8,128)(2,1)S(1)} %merge.2), channel_id=1, source_target_pairs={{0,16},{8,24},{16,0},{24,8},{32,48},{40,56},{48,32},{56,40},{64,80... | collective-permute-start | bytes 528392 | tf_op jit(solution)/shard_map/ppermute | solution.py:583
  118.7 10.7 %collective-permute-start.27 = (bf16[688,128]{1,0:T(8,128)(2,1)S(1)}, bf16[688,128]{1,0:T(8,128)(2,1)S(1)}, u32[]{:S(2)}, u32[]{:S(2)}) collective-permute-start(bf16[688,128]{1,0:T(8,128)(2,1)S(1)} %merge.3), channel_id=1, source_target_pairs={{0,16},{8,24},{16,0},{24,8},{32,48},{40,56},{48,32},{56,40},{64,80... | collective-permute-start | bytes 528392 | tf_op jit(solution)/shard_map/ppermute | solution.py:583
  126.3 7.8 %collective-permute-start.20 = (bf16[128,640]{1,0:T(8,128)(2,1)S(1)}, bf16[128,640]{1,0:T(8,128)(2,1)S(1)}, u32[]{:S(2)}, u32[]{:S(2)}) collective-permute-start(bf16[128,640]{1,0:T(8,128)(2,1)S(1)} %combine.2.attn_near), channel_id=1, source_target_pairs={{0,4},{1,5},{2,6},{3,7},{4,0},{5,1},{6,2},{7,3},{8,12},{9,13},{10,... | collective-permute-start | bytes 491528 | tf_op jit(solution)/shard_map/ppermute | solution.py:597
  130.1 15.3 %collective-permute-start.28 = (bf16[128,640]{1,0:T(8,128)(2,1)S(1)}, bf16[128,640]{1,0:T(8,128)(2,1)}, u32[]{:S(2)}, u32[]{:S(2)}) collective-permute-start(bf16[128,640]{1,0:T(8,128)(2,1)S(1)} %combine.3.attn_near), channel_id=1, source_target_pairs={{0,4},{1,5},{2,6},{3,7},{4,0},{5,1},{6,2},{7,3},{8,12},{9,13},{10,... | collective-permute-start | bytes 491528 | tf_op jit(solution)/shard_map/ppermute | solution.py:597
  136.9 0.7 copy-start
  137.6 15.0 %collective-permute-start.23 = (bf16[128,640]{1,0:T(8,128)(2,1)}, bf16[128,640]{1,0:T(8,128)(2,1)}, u32[]{:S(2)}, u32[]{:S(2)}) collective-permute-start(bf16[128,640]{1,0:T(8,128)(2,1)} %get-tuple-element.68), channel_id=1, source_target_pairs={{0,1},{1,0},{2,3},{3,2},{4,5},{5,4},{6,7},{7,6},{8,9},{9,8},{10,11... | collective-permute-start | bytes 491528 | tf_op jit(solution)/shard_map/ppermute | solution.py:639
  139.2 13.7 %collective-permute-start.24 = (bf16[128,640]{1,0:T(8,128)(2,1)}, bf16[128,640]{1,0:T(8,128)(2,1)}, u32[]{:S(2)}, u32[]{:S(2)}) collective-permute-start(bf16[128,640]{1,0:T(8,128)(2,1)} %get-tuple-element.69), channel_id=1, source_target_pairs={{0,2},{1,3},{2,0},{3,1},{4,6},{5,7},{6,4},{7,5},{8,10},{9,11},{10,... | collective-permute-start | bytes 491528 | tf_op jit(solution)/shard_map/ppermute | solution.py:639
  142.1 10.8 %collective-permute-start.25 = (bf16[128,640]{1,0:T(8,128)(2,1)}, bf16[128,640]{1,0:T(8,128)(2,1)}, u32[]{:S(2)}, u32[]{:S(2)}) collective-permute-start(bf16[128,640]{1,0:T(8,128)(2,1)} %get-tuple-element.70), channel_id=1, source_target_pairs={{0,3},{1,2},{2,1},{3,0},{4,7},{5,6},{6,5},{7,4},{8,11},{9,10},{10,... | collective-permute-start | bytes 491528 | tf_op jit(solution)/shard_map/ppermute | solution.py:639
  145.4 7.5 %copy-start.1 = (f32[128,640]{1,0:T(8,128)S(1)}, f32[128,640]{1,0:T(8,128)}, u32[]{:S(2)}) copy-start(f32[128,640]{1,0:T(8,128)} %copy-done) | copy-start | bytes 983044
  148.1 17.4 %copy-start.13 = (bf16[640]{0:T(1024)(128)(2,1)S(1)}, bf16[640]{0:T(1024)(128)(2,1)}, u32[]{:S(2)}) copy-start(bf16[640]{0:T(1024)(128)(2,1)} %param.21) | copy-start | bytes 3844
  148.1 6.0 %collective-permute-start.29 = (bf16[128,640]{1,0:T(8,128)(2,1)S(1)}, bf16[128,640]{1,0:T(8,128)(2,1)S(1)}, u32[]{:S(2)}, u32[]{:S(2)}) collective-permute-start(bf16[128,640]{1,0:T(8,128)(2,1)S(1)} %get-tuple-element.81), channel_id=1, source_target_pairs={{0,1},{1,0},{2,3},{3,2},{4,5},{5,4},{6,7},{7,6},{8,9},{9,8},{10,11... | collective-permute-start | bytes 491528 | tf_op jit(solution)/shard_map/ppermute | solution.py:639
  148.5 9.2 %collective-permute-start.30 = (bf16[128,640]{1,0:T(8,128)(2,1)S(1)}, bf16[128,640]{1,0:T(8,128)(2,1)S(1)}, u32[]{:S(2)}, u32[]{:S(2)}) collective-permute-start(bf16[128,640]{1,0:T(8,128)(2,1)S(1)} %get-tuple-element.82), channel_id=1, source_target_pairs={{0,2},{1,3},{2,0},{3,1},{4,6},{5,7},{6,4},{7,5},{8,10},{9,11},{10,... | collective-permute-start | bytes 491528 | tf_op jit(solution)/shard_map/ppermute | solution.py:639
  152.6 6.8 %collective-permute-start.31 = (bf16[128,640]{1,0:T(8,128)(2,1)S(1)}, bf16[128,640]{1,0:T(8,128)(2,1)S(1)}, u32[]{:S(2)}, u32[]{:S(2)}) collective-permute-start(bf16[128,640]{1,0:T(8,128)(2,1)S(1)} %get-tuple-element.83), channel_id=1, source_target_pairs={{0,3},{1,2},{2,1},{3,0},{4,7},{5,6},{6,5},{7,4},{8,11},{9,10},{10,... | collective-permute-start | bytes 491528 | tf_op jit(solution)/shard_map/ppermute | solution.py:639
  160.7 13.5 %copy-start.12 = (bf16[256,640]{1,0:T(8,128)(2,1)}, bf16[256,640]{1,0:T(8,128)(2,1)S(1)}, u32[]{:S(2)}) copy-start(bf16[256,640]{1,0:T(8,128)(2,1)S(1)} %get-tuple-element.90) | copy-start | bytes 983044
  161.4 11.9 %all-to-all-start = ((f32[8,8,128]{2,1,0:T(8,128)}), f32[8,8,128]{2,1,0:T(8,128)S(1)}, u32[]{:S(2)}, u32[]{:S(2)}) async-start(f32[8,8,128]{2,1,0:T(8,128)} %broadcast_in_dim.88), calls=%async_computation | async-start | bytes 65536 | tf_op jit(solution)/shard_map/all_to_all | solution.py:648

commit v3 on v1

--- a/solution.py
+++ b/solution.py
@@ -398,10 +398,15 @@
         out_weight, (far_side * FAR + 2 * core) * columns, 2 * columns, 1
     )
     weight_mine = lax.ppermute(outgoing, "tp", [(i, i ^ FAR) for i in range(ways)])
-    both = jnp.concatenate([prefix_key, prefix_value], axis=0)
-    mine = lax.dynamic_slice_in_dim(both, core * part, part, 1)
-    theirs = lax.dynamic_slice_in_dim(both, (1 - core) * part, part, 1)
-    lanes = [mine, lax.ppermute(theirs, "req", beside(1))]
+
+    def half(which):
+        cut = [
+            lax.dynamic_slice_in_dim(x, which * part, part, 1) for x in (prefix_key, prefix_value)
+        ]
+        return jnp.concatenate(cut, axis=0)
+
+    theirs = half(1 - core)
+    lanes = [half(core), lax.ppermute(theirs, "req", beside(1))]
     queries = []
     for k in range(1, PLANE):
         queries.append(lax.ppermute(suffix_query, "req", beside(k)))
@@ -596,7 +601,7 @@
                 bytes_accessed=8 << 20,
                 transcendentals=0,
             ),
-            compiler_params=params(50),
+            compiler_params=params(47),
             name="project",
         )(where, near[j], far[j], out_weight, weight_mine, weight_theirs)
         total = pieces[0]

time: 170 us -> 174 us (1.024)
  local copies, waits for them, and re-layouts: 8.28 us -> 12.4 us
  waiting for transfers between devices: 73.3 us -> 71 us
    unnamed x29 -> x40, local copies, waits for them, and re-layouts: 3.75 us -> 7.77 us
    ppermute x6, starting transfers between devices: 17.5 us -> 15.4 us  [shards(): moving_down = lax.ppermute(moving_down, 'req', down_pairs)]
  transfers between devices with their start and end apart: 33 -> 33, of which waited for: 14 -> 12; matrix products, arithmetic and copies ran while one was open for 4% -> 4% of each run, Pallas kernels for 22% -> 22%
where the time goes in v3:
time: 174 us; the launch traced here: 173 us
  waiting for transfers between devices  71 us (41%)
  starting transfers between devices  43.1 us (25%)
  Pallas kernels  38.7 us (22%)
  local copies, waits for them, and re-layouts  12.4 us (7%)
  other arithmetic  6.78 us (4%)
    ppermute x3, waiting for transfers between devices, shards(): queries.append(lax.ppermute(suffix_query, 'req', beside(k)))  40 us
    ppermute x6, starting transfers between devices, shards(): moving_down = lax.ppermute(moving_down, 'req', down_pairs)  15.4 us
    pallas_call x1, Pallas kernels, shards(): pl.pallas_call(make_first(base, len(parts)), out_shape=(shape((every, lin...  13.1 us
    pallas_call x2, Pallas kernels, shards(): pl.pallas_call(make_middle(base, len(parts)), out_shape=state_shapes, in_...  10.6 us
    ppermute x6, starting transfers between devices, shards(): piece = lax.ppermute(pieces[k], 'tp', [(i, i ^ k) for i in range(ways)])  9.48 us
    pallas_call x2, Pallas kernels, shards(): pl.pallas_call(project_kernel, out_shape=tuple((shape((TILE, columns), bf...  8.31 us
    unnamed x40, local copies, waits for them, and re-layouts  7.77 us
    all_to_all x1, waiting for transfers between devices, shards(): lax.all_to_all(jnp.broadcast_to(squares[None], (ways, 8, HD)), 'tp', 0, 0)  7.67 us
  transfers between devices with their start and end apart: 33, of which 12 were waited for; matrix products, arithmetic and copies ran while one was open for 4% of the time, Pallas kernels for 22%

profile of v3, /device:TPU:2, one launch (start us, length us, event | category | flops | bytes accessed | tf_op | source)
XLA Modules:
  0.0 173.2 jit_solution(3544018021722427044)
XLA Ops:
  0.7 1.2 constant_dynamic-slice_fusion.1
  1.9 2.0 %collective-permute-start.4 = (bf16[2,512,128]{2,1,0:T(8,128)(2,1)S(1)}, bf16[2,512,128]{2,1,0:T(8,128)(2,1)}, u32[]{:S(2)}, u32[]{:S(2)}) collective-permute-start(bf16[2,512,128]{2,1,0:T(8,128)(2,1)S(1)} %pad_maximum_fusion.rest_0_), channel_id=1, source_target_pairs={{0,32},{8,40},{16,48},{24,56},{32,64},{40,72},{48,80},{56,88},{64,... | collective-permute-start | bytes 786440 | tf_op jit(solution)/shard_map/ppermute | solution.py:420
  3.9 4.0 %collective-permute-start.5 = (bf16[2,512,128]{2,1,0:T(8,128)(2,1)S(1)}, bf16[2,512,128]{2,1,0:T(8,128)(2,1)S(1)}, u32[]{:S(2)}, u32[]{:S(2)}) collective-permute-start(bf16[2,512,128]{2,1,0:T(8,128)(2,1)S(1)} %pad_maximum_fusion.rest_0_), channel_id=1, source_target_pairs={{0,224},{8,232},{16,240},{24,248},{32,0},{40,8},{48,16},{56,24},{6... | collective-permute-start | bytes 786440 | tf_op jit(solution)/shard_map/ppermute | solution.py:421
  8.1 0.5 collective-permute-start
  8.6 2.7 %constant_dynamic-slice_fusion = bf16[640,1280]{1,0:T(8,128)(2,1)} fusion(bf16[640,5120]{1,0:T(8,128)(2,1)} %weight_in.3, s32[]{:T(128)S(6)} %select_n.89), kind=kLoop, calls=%fused_computation.32 | loop fusion | bytes 3276804 | tf_op jit(solution)/shard_map/dynamic_slice | solution.py:397
  11.3 2.1 %collective-permute-start.21 = (bf16[640,1280]{1,0:T(8,128)(2,1)}, bf16[640,1280]{1,0:T(8,128)(2,1)S(1)}, u32[]{:S(2)}, u32[]{:S(2)}) collective-permute-start(bf16[640,1280]{1,0:T(8,128)(2,1)} %constant_dynamic-slice_fusion), channel_id=1, source_target_pairs={{0,4},{1,5},{2,6},{3,7},{4,0},{5,1},{6,2},{7,3},{8,12},{9,13},{10,... | collective-permute-start | bytes 4915208 | tf_op jit(solution)/shard_map/ppermute | solution.py:400
  13.6 0.2 select_reduce_fusion.3
  13.8 0.2 select_reduce_fusion.2
  14.0 0.2 select_reduce_fusion.5
  14.2 1.5 collective-permute-start.1
  15.7 1.9 %collective-permute-start.7 = (bf16[2,512,128]{2,1,0:T(8,128)(2,1)}, bf16[2,512,128]{2,1,0:T(8,128)(2,1)}, u32[]{:S(2)}, u32[]{:S(2)}) collective-permute-start(bf16[2,512,128]{2,1,0:T(8,128)(2,1)} %collective-permute-done.3.rest_1_), channel_id=1, source_target_pairs={{0,224},{8,232},{16,240},{24,248},{32,0},{40,8},{48,16},{56,24},{6... | collective-permute-start | bytes 786440 | tf_op jit(solution)/shard_map/ppermute | solution.py:421
  17.7 1.3 fusion.4
  19.0 0.7 copy-done.4
  19.8 38.9 %collective-permute-done.1.q2 = bf16[256,640]{1,0:T(8,128)(2,1)S(1)} collective-permute-done((bf16[256,640]{1,0:T(8,128)(2,1)}, bf16[256,640]{1,0:T(8,128)(2,1)S(1)}, u32[]{:S(2)}, u32[]{:S(2)}) %collective-permute-start.1) | collective-permute-done | bytes 327712 | tf_op jit(solution)/shard_map/ppermute | solution.py:412
  58.8 0.7 copy-done.6
  59.5 3.2 %collective-permute-start.11 = (bf16[2,512,128]{2,1,0:T(8,128)(2,1)}, bf16[2,512,128]{2,1,0:T(8,128)(2,1)}, u32[]{:S(2)}, u32[]{:S(2)}) collective-permute-start(bf16[2,512,128]{2,1,0:T(8,128)(2,1)} %collective-permute-done.7.rest_5_), channel_id=1, source_target_pairs={{0,224},{8,232},{16,240},{24,248},{32,0},{40,8},{48,16},{56,24},{6... | collective-permute-start | bytes 786440 | tf_op jit(solution)/shard_map/ppermute | solution.py:421
  63.0 1.1 collective-permute-done.2.q3
  64.1 1.9 %collective-permute-start.9 = (bf16[2,512,128]{2,1,0:T(8,128)(2,1)}, bf16[2,512,128]{2,1,0:T(8,128)(2,1)S(1)}, u32[]{:S(2)}, u32[]{:S(2)}) collective-permute-start(bf16[2,512,128]{2,1,0:T(8,128)(2,1)} %copy-done.8), channel_id=1, source_target_pairs={{0,224},{8,232},{16,240},{24,248},{32,0},{40,8},{48,16},{56,24},{6... | collective-permute-start | bytes 786440 | tf_op jit(solution)/shard_map/ppermute | solution.py:421
  66.2 1.3 collective-permute-done.8.rest_0_
  67.5 3.2 %collective-permute-start.15 = (bf16[2,512,128]{2,1,0:T(8,128)(2,1)}, bf16[2,512,128]{2,1,0:T(8,128)(2,1)S(1)}, u32[]{:S(2)}, u32[]{:S(2)}) collective-permute-start(bf16[2,512,128]{2,1,0:T(8,128)(2,1)} %collective-permute-done.11.rest_3_), channel_id=1, source_target_pairs={{0,224},{8,232},{16,240},{24,248},{32,0},{40,8},{48,16},{56,24},{6... | collective-permute-start | bytes 786440 | tf_op jit(solution)/shard_map/ppermute | solution.py:421
  70.8 1.2 pad_maximum_fusion.2
  72.0 0.8 copy-done.10
  72.9 0.8 copy-done.11
  73.7 1.9 %own.1 = (bf16[2,640,128]{2,1,0:T(8,128)(2,1)S(1)}, bf16[256,128]{1,0:T(8,128)(2,1)}, f32[2,128,640]{2,1,0:T(8,128)S(1)}, f32[2,1,640]{2,1,0:T(1,128)S(1)}, f32[2,1,640]{2,1,0:T(1,128)S(1)}) custom-call(s32[72]{0:T(128)S(1)} %pad_add_fusion.1.meta, bf16[256,640]{1,0:T(8,128)(2,1)} %q_in.1, bf16[256,128]{1,0:T(8,128)(2,1)S(1)} %copy-done.10, ...), custom_call_target="tpu_custom_call" | custom-call | flops 335544320 | bytes 3145728 | tf_op jit(solution)/shard_map/own/pallas_call | solution.py:467
  75.7 1.0 collective-permute-start.13
  76.7 1.1 collective-permute-start.14
  77.8 4.5 %collective-permute-done.12.rest_0_ = bf16[2,512,128]{2,1,0:T(8,128)(2,1)S(1)} collective-permute-done((bf16[2,512,128]{2,1,0:T(8,128)(2,1)S(1)}, bf16[2,512,128]{2,1,0:T(8,128)(2,1)S(1)}, u32[]{:S(2)}, u32[]{:S(2)}) %collective-permute-start.12) | collective-permute-done | bytes 262176 | tf_op jit(solution)/shard_map/ppermute | solution.py:420
  82.3 3.2 %collective-permute-start.17 = (bf16[2,512,128]{2,1,0:T(8,128)(2,1)S(1)}, bf16[2,512,128]{2,1,0:T(8,128)(2,1)S(1)}, u32[]{:S(2)}, u32[]{:S(2)}) collective-permute-start(bf16[2,512,128]{2,1,0:T(8,128)(2,1)S(1)} %collective-permute-done.15.rest_3_), channel_id=1, source_target_pairs={{0,224},{8,232},{16,240},{24,248},{32,0},{40,8},{48,16},{56,24},{6... | collective-permute-start | bytes 786440 | tf_op jit(solution)/shard_map/ppermute | solution.py:427
  85.5 0.9 copy-done.3
  86.5 1.0 copy-done.5
  87.5 1.0 copy-done.7
  88.4 0.9 copy-done.9
  89.4 13.1 %first.1 = (bf16[9,640,128]{2,1,0:T(8,128)(2,1)S(1)}, f32[9,128,640]{2,1,0:T(8,128)S(1)}, f32[9,1,640]{2,1,0:T(1,128)S(1)}, f32[9,1,640]{2,1,0:T(1,128)S(1)}) custom-call(s32[72]{0:T(128)S(1)} %pad_add_fusion.1.meta, bf16[2,640,128]{2,1,0:T(8,128)(2,1)S(1)} %get-tuple-element.36.q_own, f32[2,128,640]{2,1,0:T(8,128)S(1)} %get-tuple-element.37.acc_own, ...), custom_call_target="tpu_custom_call" | custom-call | flops 2013265920 | bytes 8388608 | tf_op jit(solution)/shard_map/first/pallas_call | solution.py:505
  102.5 5.6 %middle.2 = (f32[9,128,640]{2,1,0:T(8,128)S(1)}, f32[9,1,640]{2,1,0:T(1,128)S(1)}, f32[9,1,640]{2,1,0:T(1,128)S(1)}) custom-call(s32[72]{0:T(128)S(1)} %pad_add_fusion.1.meta, bf16[9,640,128]{2,1,0:T(8,128)(2,1)S(1)} %get-tuple-element.40.q_ref, f32[9,128,640]{2,1,0:T(8,128)S(1)} %get-tuple-element.41.acc_in, f32[9,1,640]{2,1,0:T(1,128)S(1)} %get-tuple-element.42.max_in, ...), custom_call_target="tpu_custom_call" | custom-call | flops 1342177280 | bytes 8388608 | tf_op jit(solution)/shard_map/middle/pallas_call | solution.py:518
  108.1 5.0 %middle.3 = (f32[9,128,640]{2,1,0:T(8,128)S(1)}, f32[9,1,640]{2,1,0:T(1,128)S(1)}, f32[9,1,640]{2,1,0:T(1,128)S(1)}) custom-call(s32[72]{0:T(128)S(1)} %pad_add_fusion.1.meta, bf16[9,640,128]{2,1,0:T(8,128)(2,1)S(1)} %get-tuple-element.40.q_ref, f32[9,128,640]{2,1,0:T(8,128)S(1)} %get-tuple-element.44.acc_in, f32[9,1,640]{2,1,0:T(1,128)S(1)} %get-tuple-element.45.max_in, ...), custom_call_target="tpu_custom_call" | custom-call | flops 1342177280 | bytes 8388608 | tf_op jit(solution)/shard_map/middle/pallas_call | solution.py:518
  113.2 3.2 %last.1 = (f32[128,640]{1,0:T(8,128)S(1)}, f32[16,128]{1,0:T(8,128)S(1)}, f32[128,640]{1,0:T(8,128)S(1)}, f32[16,128]{1,0:T(8,128)S(1)}, bf16[2,688,128]{2,1,0:T...) custom-call(s32[72]{0:T(128)S(1)} %pad_add_fusion.1.meta, ...), custom_call_target="tpu_custom_call" | custom-call | flops 671088640 | bytes 8388608 | tf_op jit(solution)/shard_map/last/pallas_call | solution.py:531
  116.4 0.5 collective-permute-start.26
  116.9 1.2 collective-permute-done.18.swapped
  118.3 0.3 collective-permute-done.26.swapped
  118.7 1.8 %collective-permute-start.27 = (bf16[688,128]{1,0:T(8,128)(2,1)S(1)}, bf16[688,128]{1,0:T(8,128)(2,1)S(1)}, u32[]{:S(2)}, u32[]{:S(2)}) collective-permute-start(bf16[688,128]{1,0:T(8,128)(2,1)S(1)} %merge.3), channel_id=1, source_target_pairs={{0,16},{8,24},{16,0},{24,8},{32,48},{40,56},{48,32},{56,40},{64,80... | collective-permute-start | bytes 528392 | tf_op jit(solution)/shard_map/ppermute | solution.py:568
  120.4 5.1 %collective-permute-done.19.crossed = bf16[688,128]{1,0:T(8,128)(2,1)S(1)} collective-permute-done((bf16[688,128]{1,0:T(8,128)(2,1)S(1)}, bf16[688,128]{1,0:T(8,128)(2,1)S(1)}, u32[]{:S(2)}, u32[]{:S(2)}) %collective-permute-start.19) | collective-permute-done | bytes 176160 | tf_op jit(solution)/shard_map/ppermute | solution.py:568
  125.6 0.7 combine.2.attn_near
  126.3 0.7 collective-permute-start.20
  127.0 2.3 %collective-permute-done.27.crossed = bf16[688,128]{1,0:T(8,128)(2,1)S(1)} collective-permute-done((bf16[688,128]{1,0:T(8,128)(2,1)S(1)}, bf16[688,128]{1,0:T(8,128)(2,1)S(1)}, u32[]{:S(2)}, u32[]{:S(2)}) %collective-permute-start.27) | collective-permute-done | bytes 176160 | tf_op jit(solution)/shard_map/ppermute | solution.py:568
  129.4 0.7 combine.3.attn_near
  130.1 0.9 collective-permute-start.28
  131.1 3.1 %collective-permute-done.20.attn_far = bf16[128,640]{1,0:T(8,128)(2,1)S(1)} collective-permute-done((bf16[128,640]{1,0:T(8,128)(2,1)S(1)}, bf16[128,640]{1,0:T(8,128)(2,1)S(1)}, u32[]{:S(2)}, u32[]{:S(2)}) %collective-permute-start.20) | collective-permute-done | bytes 163872 | tf_op jit(solution)/shard_map/ppermute | solution.py:582
  134.2 4.2 %project.2 = (f32[128,640]{1,0:T(8,128)S(1)}, bf16[128,640]{1,0:T(8,128)(2,1)}, bf16[128,640]{1,0:T(8,128)(2,1)}, bf16[128,640]{1,0:T(8,128)(2,1)}) custom-call(s32[2]{0:T(128)S(1)} %pad_add_fusion.where, bf16[128,640]{1,0:T(8,128)(2,1)S(1)} %combine.2.attn_near, bf16[128,640]{1,0:T(8,128)(2,1)S(1)} %collective-permute-done.20.attn_far, ...), custom_call_target="tpu_custom_call" | custom-call | flops 838860800 | bytes 8388608 | tf_op jit(solution)/shard_map/project/pallas_call | solution.py:587
  138.4 0.7 copy-done
  139.1 1.6 collective-permute-start.23
  140.7 2.9 %collective-permute-start.24 = (bf16[128,640]{1,0:T(8,128)(2,1)}, bf16[128,640]{1,0:T(8,128)(2,1)}, u32[]{:S(2)}, u32[]{:S(2)}) collective-permute-start(bf16[128,640]{1,0:T(8,128)(2,1)} %get-tuple-element.57), channel_id=1, source_target_pairs={{0,2},{1,3},{2,0},{3,1},{4,6},{5,7},{6,4},{7,5},{8,10},{9,11},{10,... | collective-permute-start | bytes 491528 | tf_op jit(solution)/shard_map/ppermute | solution.py:609
  143.6 0.2 collective-permute-start.25
  143.8 4.1 %project.3 = (f32[128,640]{1,0:T(8,128)S(1)}, bf16[128,640]{1,0:T(8,128)(2,1)S(1)}, bf16[128,640]{1,0:T(8,128)(2,1)S(1)}, bf16[128,640]{1,0:T(8,128)(2,1)S(1)}) custom-call(s32[2]{0:T(128)S(1)} %pad_add_fusion.where, bf16[128,640]{1,0:T(8,128)(2,1)S(1)} %combine.3.attn_near, bf16[128,640]{1,0:T(8,128)(2,1)} %collective-permute-done.28.attn_far, ...), custom_call_target="tpu_custom_call" | custom-call | flops 838860800 | bytes 8388608 | tf_op jit(solution)/shard_map/project/pallas_call | solution.py:587
  147.9 0.4 collective-permute-start.29
  148.4 4.1 %collective-permute-start.30 = (bf16[128,640]{1,0:T(8,128)(2,1)S(1)}, bf16[128,640]{1,0:T(8,128)(2,1)S(1)}, u32[]{:S(2)}, u32[]{:S(2)}) collective-permute-start(bf16[128,640]{1,0:T(8,128)(2,1)S(1)} %get-tuple-element.66), channel_id=1, source_target_pairs={{0,2},{1,3},{2,0},{3,1},{4,6},{5,7},{6,4},{7,5},{8,10},{9,11},{10,... | collective-permute-start | bytes 491528 | tf_op jit(solution)/shard_map/ppermute | solution.py:609
  152.5 0.2 collective-permute-start.31
  152.7 1.1 convert_add_fusion.1
  153.9 3.7 %collective-permute-done.30 = bf16[128,640]{1,0:T(8,128)(2,1)S(1)} collective-permute-done((bf16[128,640]{1,0:T(8,128)(2,1)S(1)}, bf16[128,640]{1,0:T(8,128)(2,1)S(1)}, u32[]{:S(2)}, u32[]{:S(2)}) %collective-permute-start.30) | collective-permute-done | bytes 163872 | tf_op jit(solution)/shard_map/ppermute | solution.py:609
  157.6 1.7 collective-permute-done.31
  159.4 1.2 fusion
  160.5 0.7 broadcast_in_dim.88
  161.2 3.3 %all-to-all-start = ((f32[8,8,128]{2,1,0:T(8,128)}), f32[8,8,128]{2,1,0:T(8,128)S(1)}, u32[]{:S(2)}, u32[]{:S(2)}) async-start(f32[8,8,128]{2,1,0:T(8,128)} %broadcast_in_dim.88), calls=%async_computation | async-start | bytes 65536 | tf_op jit(solution)/shard_map/all_to_all | solution.py:618
  164.6 7.7 %all-to-all-done = f32[8,8,128]{2,1,0:T(8,128)S(1)} async-done(((f32[8,8,128]{2,1,0:T(8,128)}), f32[8,8,128]{2,1,0:T(8,128)S(1)}, u32[]{:S(2)}, u32[]{:S(2)}) %all-to-all-start) | async-done | bytes 32800 | tf_op jit(solution)/shard_map/all_to_all | solution.py:618
  172.3 0.9 fusion.2
  (82 shorter events, 1.5 us)
Async XLA Ops:
  0.7 12.8 %copy-start.19 = (s32[32]{0:T(128)S(1)}, s32[32]{0:T(128)}, u32[]{:S(2)}) copy-start(s32[32]{0:T(128)} %param.24) | copy-start | bytes 388
  0.7 12.9 %copy-start.17 = (s32[16]{0:T(128)S(1)}, s32[16]{0:T(128)}, u32[]{:S(2)}) copy-start(s32[16]{0:T(128)} %constant.122.clone) | copy-start | bytes 196
  0.7 12.9 %copy-start.18 = (s32[16]{0:T(128)S(1)}, s32[16]{0:T(128)}, u32[]{:S(2)}) copy-start(s32[16]{0:T(128)} %constant.123.clone) | copy-start | bytes 196
  0.7 13.1 %copy-start.14 = (s32[32]{0:T(128)S(1)}, s32[32]{0:T(128)}, u32[]{:S(2)}) copy-start(s32[32]{0:T(128)} %param.22) | copy-start | bytes 388
  0.7 13.1 %copy-start.15 = (s32[32]{0:T(128)S(1)}, s32[32]{0:T(128)}, u32[]{:S(2)}) copy-start(s32[32]{0:T(128)} %param.23) | copy-start | bytes 388
  0.7 13.1 %copy-start.16 = (s32[32,1]{0,1:T(1,128)S(1)}, s32[32,1]{0,1:T(1,128)}, u32[]{:S(2)}) copy-start(s32[32,1]{0,1:T(1,128)} %param.25) | copy-start | bytes 388
  1.9 61.0 %copy-start.2 = (bf16[2,512,128]{2,1,0:T(8,128)(2,1)}, bf16[2,512,128]{2,1,0:T(8,128)(2,1)S(1)}, u32[]{:S(2)}) copy-start(bf16[2,512,128]{2,1,0:T(8,128)(2,1)S(1)} %pad_maximum_fusion.rest_0_) | copy-start | bytes 786436
  1.9 13.8 %collective-permute-start.4 = (bf16[2,512,128]{2,1,0:T(8,128)(2,1)S(1)}, bf16[2,512,128]{2,1,0:T(8,128)(2,1)}, u32[]{:S(2)}, u32[]{:S(2)}) collective-permute-start(bf16[2,512,128]{2,1,0:T(8,128)(2,1)S(1)} %pad_maximum_fusion.rest_0_), channel_id=1, source_target_pairs={{0,32},{8,40},{16,48},{24,56},{32,64},{40,72},{48,80},{56,88},{64,... | collective-permute-start | bytes 786440 | tf_op jit(solution)/shard_map/ppermute | solution.py:420
  3.9 15.0 %collective-permute-start.5 = (bf16[2,512,128]{2,1,0:T(8,128)(2,1)S(1)}, bf16[2,512,128]{2,1,0:T(8,128)(2,1)S(1)}, u32[]{:S(2)}, u32[]{:S(2)}) collective-permute-start(bf16[2,512,128]{2,1,0:T(8,128)(2,1)S(1)} %pad_maximum_fusion.rest_0_), channel_id=1, source_target_pairs={{0,224},{8,232},{16,240},{24,248},{32,0},{40,8},{48,16},{56,24},{6... | collective-permute-start | bytes 786440 | tf_op jit(solution)/shard_map/ppermute | solution.py:421
  8.0 6.2 %collective-permute-start.3 = (bf16[2,512,128]{2,1,0:T(8,128)(2,1)S(1)}, bf16[2,512,128]{2,1,0:T(8,128)(2,1)}, u32[]{:S(2)}, u32[]{:S(2)}) collective-permute-start(bf16[2,512,128]{2,1,0:T(8,128)(2,1)S(1)} %pad_maximum_fusion.1), channel_id=1, source_target_pairs={{0,8},{8,0},{16,24},{24,16},{32,40},{40,32},{48,56},{56,48},{64,72... | collective-permute-start | bytes 786440 | tf_op jit(solution)/shard_map/ppermute | solution.py:409
  8.1 10.9 %collective-permute-start = (bf16[256,640]{1,0:T(8,128)(2,1)}, bf16[256,640]{1,0:T(8,128)(2,1)S(1)}, u32[]{:S(2)}, u32[]{:S(2)}) collective-permute-start(bf16[256,640]{1,0:T(8,128)(2,1)} %q_in.1), channel_id=1, source_target_pairs={{0,8},{8,0},{16,24},{24,16},{32,40},{40,32},{48,56},{56,48},{64,72... | collective-permute-start | bytes 983048 | tf_op jit(solution)/shard_map/ppermute | solution.py:412
  11.3 51.6 %collective-permute-start.21 = (bf16[640,1280]{1,0:T(8,128)(2,1)}, bf16[640,1280]{1,0:T(8,128)(2,1)S(1)}, u32[]{:S(2)}, u32[]{:S(2)}) collective-permute-start(bf16[640,1280]{1,0:T(8,128)(2,1)} %constant_dynamic-slice_fusion), channel_id=1, source_target_pairs={{0,4},{1,5},{2,6},{3,7},{4,0},{5,1},{6,2},{7,3},{8,12},{9,13},{10,... | collective-permute-start | bytes 4915208 | tf_op jit(solution)/shard_map/ppermute | solution.py:400
  14.2 44.6 %collective-permute-start.1 = (bf16[256,640]{1,0:T(8,128)(2,1)}, bf16[256,640]{1,0:T(8,128)(2,1)S(1)}, u32[]{:S(2)}, u32[]{:S(2)}) collective-permute-start(bf16[256,640]{1,0:T(8,128)(2,1)} %q_in.1), channel_id=1, source_target_pairs={{0,16},{8,24},{16,0},{24,8},{32,48},{40,56},{48,32},{56,40},{64,80... | collective-permute-start | bytes 983048 | tf_op jit(solution)/shard_map/ppermute | solution.py:412
  15.7 43.8 %collective-permute-start.7 = (bf16[2,512,128]{2,1,0:T(8,128)(2,1)}, bf16[2,512,128]{2,1,0:T(8,128)(2,1)}, u32[]{:S(2)}, u32[]{:S(2)}) collective-permute-start(bf16[2,512,128]{2,1,0:T(8,128)(2,1)} %collective-permute-done.3.rest_1_), channel_id=1, source_target_pairs={{0,224},{8,232},{16,240},{24,248},{32,0},{40,8},{48,16},{56,24},{6... | collective-permute-start | bytes 786440 | tf_op jit(solution)/shard_map/ppermute | solution.py:421
  19.0 43.9 %copy-start.8 = (bf16[2,512,128]{2,1,0:T(8,128)(2,1)}, bf16[2,512,128]{2,1,0:T(8,128)(2,1)S(1)}, u32[]{:S(2)}) copy-start(bf16[2,512,128]{2,1,0:T(8,128)(2,1)S(1)} %collective-permute-done.5.rest_3_) | copy-start | bytes 786436
  19.0 45.2 %collective-permute-start.2 = (bf16[256,640]{1,0:T(8,128)(2,1)}, bf16[256,640]{1,0:T(8,128)(2,1)}, u32[]{:S(2)}, u32[]{:S(2)}) collective-permute-start(bf16[256,640]{1,0:T(8,128)(2,1)} %q_in.1), channel_id=1, source_target_pairs={{0,24},{8,16},{16,8},{24,0},{32,56},{40,48},{48,40},{56,32},{64,88... | collective-permute-start | bytes 983048 | tf_op jit(solution)/shard_map/ppermute | solution.py:412
  19.0 0.8 copy-start.4
  19.7 46.3 %collective-permute-start.6 = (bf16[2,512,128]{2,1,0:T(8,128)(2,1)}, bf16[2,512,128]{2,1,0:T(8,128)(2,1)}, u32[]{:S(2)}, u32[]{:S(2)}) collective-permute-start(bf16[2,512,128]{2,1,0:T(8,128)(2,1)} %collective-permute-done.3.rest_1_), channel_id=1, source_target_pairs={{0,32},{8,40},{16,48},{24,56},{32,64},{40,72},{48,80},{56,88},{64,... | collective-permute-start | bytes 786440 | tf_op jit(solution)/shard_map/ppermute | solution.py:420
  58.7 0.7 copy-start.6
  59.5 8.0 %collective-permute-start.8 = (bf16[2,512,128]{2,1,0:T(8,128)(2,1)}, bf16[2,512,128]{2,1,0:T(8,128)(2,1)S(1)}, u32[]{:S(2)}, u32[]{:S(2)}) collective-permute-start(bf16[2,512,128]{2,1,0:T(8,128)(2,1)} %collective-permute-done.4.rest_2_), channel_id=1, source_target_pairs={{0,32},{8,40},{16,48},{24,56},{32,64},{40,72},{48,80},{56,88},{64,... | collective-permute-start | bytes 786440 | tf_op jit(solution)/shard_map/ppermute | solution.py:420
  59.5 8.0 %collective-permute-start.11 = (bf16[2,512,128]{2,1,0:T(8,128)(2,1)}, bf16[2,512,128]{2,1,0:T(8,128)(2,1)}, u32[]{:S(2)}, u32[]{:S(2)}) collective-permute-start(bf16[2,512,128]{2,1,0:T(8,128)(2,1)} %collective-permute-done.7.rest_5_), channel_id=1, source_target_pairs={{0,224},{8,232},{16,240},{24,248},{32,0},{40,8},{48,16},{56,24},{6... | collective-permute-start | bytes 786440 | tf_op jit(solution)/shard_map/ppermute | solution.py:421
  62.9 71.3 %collective-permute-start.22 = (bf16[640,1280]{1,0:T(8,128)(2,1)S(1)}, bf16[640,1280]{1,0:T(8,128)(2,1)S(1)}, u32[]{:S(2)}, u32[]{:S(2)}) collective-permute-start(bf16[640,1280]{1,0:T(8,128)(2,1)S(1)} %collective-permute-done.21.mine_in), channel_id=1, source_target_pairs={{0,8},{8,0},{16,24},{24,16},{32,40},{40,32},{48,56},{56,48},{64,72... | collective-permute-start | bytes 4915208 | tf_op jit(solution)/shard_map/ppermute | solution.py:583
  64.1 11.5 %collective-permute-start.9 = (bf16[2,512,128]{2,1,0:T(8,128)(2,1)}, bf16[2,512,128]{2,1,0:T(8,128)(2,1)S(1)}, u32[]{:S(2)}, u32[]{:S(2)}) collective-permute-start(bf16[2,512,128]{2,1,0:T(8,128)(2,1)} %copy-done.8), channel_id=1, source_target_pairs={{0,224},{8,232},{16,240},{24,248},{32,0},{40,8},{48,16},{56,24},{6... | collective-permute-start | bytes 786440 | tf_op jit(solution)/shard_map/ppermute | solution.py:421
  66.1 10.6 %collective-permute-start.10 = (bf16[2,512,128]{2,1,0:T(8,128)(2,1)}, bf16[2,512,128]{2,1,0:T(8,128)(2,1)S(1)}, u32[]{:S(2)}, u32[]{:S(2)}) collective-permute-start(bf16[2,512,128]{2,1,0:T(8,128)(2,1)} %collective-permute-done.6.rest_4_), channel_id=1, source_target_pairs={{0,32},{8,40},{16,48},{24,56},{32,64},{40,72},{48,80},{56,88},{64,... | collective-permute-start | bytes 786440 | tf_op jit(solution)/shard_map/ppermute | solution.py:420
  67.5 14.8 %collective-permute-start.12 = (bf16[2,512,128]{2,1,0:T(8,128)(2,1)S(1)}, bf16[2,512,128]{2,1,0:T(8,128)(2,1)S(1)}, u32[]{:S(2)}, u32[]{:S(2)}) collective-permute-start(bf16[2,512,128]{2,1,0:T(8,128)(2,1)S(1)} %collective-permute-done.8.rest_0_), channel_id=1, source_target_pairs={{0,32},{8,40},{16,48},{24,56},{32,64},{40,72},{48,80},{56,88},{64,... | collective-permute-start | bytes 786440 | tf_op jit(solution)/shard_map/ppermute | solution.py:420
  67.5 14.8 %collective-permute-start.15 = (bf16[2,512,128]{2,1,0:T(8,128)(2,1)}, bf16[2,512,128]{2,1,0:T(8,128)(2,1)S(1)}, u32[]{:S(2)}, u32[]{:S(2)}) collective-permute-start(bf16[2,512,128]{2,1,0:T(8,128)(2,1)} %collective-permute-done.11.rest_3_), channel_id=1, source_target_pairs={{0,224},{8,232},{16,240},{24,248},{32,0},{40,8},{48,16},{56,24},{6... | collective-permute-start | bytes 786440 | tf_op jit(solution)/shard_map/ppermute | solution.py:421
  72.0 0.8 copy-start.10
  72.9 0.8 copy-start.11
  75.7 32.4 %collective-permute-start.13 = (bf16[2,512,128]{2,1,0:T(8,128)(2,1)S(1)}, bf16[2,512,128]{2,1,0:T(8,128)(2,1)S(1)}, u32[]{:S(2)}, u32[]{:S(2)}) collective-permute-start(bf16[2,512,128]{2,1,0:T(8,128)(2,1)S(1)} %collective-permute-done.9.rest_1_), channel_id=1, source_target_pairs={{0,224},{8,232},{16,240},{24,248},{32,0},{40,8},{48,16},{56,24},{6... | collective-permute-start | bytes 786440 | tf_op jit(solution)/shard_map/ppermute | solution.py:421
  76.7 31.4 %collective-permute-start.14 = (bf16[2,512,128]{2,1,0:T(8,128)(2,1)S(1)}, bf16[2,512,128]{2,1,0:T(8,128)(2,1)S(1)}, u32[]{:S(2)}, u32[]{:S(2)}) collective-permute-start(bf16[2,512,128]{2,1,0:T(8,128)(2,1)S(1)} %collective-permute-done.10.rest_2_), channel_id=1, source_target_pairs={{0,32},{8,40},{16,48},{24,56},{32,64},{40,72},{48,80},{56,88},{64,... | collective-permute-start | bytes 786440 | tf_op jit(solution)/shard_map/ppermute | solution.py:420
  82.3 30.8 %collective-permute-start.16 = (bf16[2,512,128]{2,1,0:T(8,128)(2,1)S(1)}, bf16[2,512,128]{2,1,0:T(8,128)(2,1)S(1)}, u32[]{:S(2)}, u32[]{:S(2)}) collective-permute-start(bf16[2,512,128]{2,1,0:T(8,128)(2,1)S(1)} %collective-permute-done.12.rest_0_), channel_id=1, source_target_pairs={{0,32},{8,40},{16,48},{24,56},{32,64},{40,72},{48,80},{56,88},{64,... | collective-permute-start | bytes 786440 | tf_op jit(solution)/shard_map/ppermute | solution.py:425
  82.3 30.9 %collective-permute-start.17 = (bf16[2,512,128]{2,1,0:T(8,128)(2,1)S(1)}, bf16[2,512,128]{2,1,0:T(8,128)(2,1)S(1)}, u32[]{:S(2)}, u32[]{:S(2)}) collective-permute-start(bf16[2,512,128]{2,1,0:T(8,128)(2,1)S(1)} %collective-permute-done.15.rest_3_), channel_id=1, source_target_pairs={{0,224},{8,232},{16,240},{24,248},{32,0},{40,8},{48,16},{56,24},{6... | collective-permute-start | bytes 786440 | tf_op jit(solution)/shard_map/ppermute | solution.py:427
  85.5 0.9 copy-start.3
  86.5 1.0 copy-start.5
  87.5 1.0 copy-start.7
  88.4 0.9 copy-start.9
  116.3 1.8 %collective-permute-start.18 = (bf16[2,688,128]{2,1,0:T(8,128)(2,1)S(1)}, bf16[2,688,128]{2,1,0:T(8,128)(2,1)S(1)}, u32[]{:S(2)}, u32[]{:S(2)}) collective-permute-start(bf16[2,688,128]{2,1,0:T(8,128)(2,1)S(1)} %get-tuple-element.52), channel_id=1, source_target_pairs={{0,8},{8,0},{16,24},{24,16},{32,40},{40,32},{48,56},{56,48},{64,72... | collective-permute-start | bytes 1056776 | tf_op jit(solution)/shard_map/ppermute | solution.py:556
  116.4 2.2 %collective-permute-start.26 = (bf16[2,688,128]{2,1,0:T(8,128)(2,1)S(1)}, bf16[2,688,128]{2,1,0:T(8,128)(2,1)S(1)}, u32[]{:S(2)}, u32[]{:S(2)}) collective-permute-start(bf16[2,688,128]{2,1,0:T(8,128)(2,1)S(1)} %get-tuple-element.61), channel_id=1, source_target_pairs={{0,8},{8,0},{16,24},{24,16},{32,40},{40,32},{48,56},{56,48},{64,72... | collective-permute-start | bytes 1056776 | tf_op jit(solution)/shard_map/ppermute | solution.py:556
  118.2 7.4 %collective-permute-start.19 = (bf16[688,128]{1,0:T(8,128)(2,1)S(1)}, bf16[688,128]{1,0:T(8,128)(2,1)S(1)}, u32[]{:S(2)}, u32[]{:S(2)}) collective-permute-start(bf16[688,128]{1,0:T(8,128)(2,1)S(1)} %merge.2), channel_id=1, source_target_pairs={{0,16},{8,24},{16,0},{24,8},{32,48},{40,56},{48,32},{56,40},{64,80... | collective-permute-start | bytes 528392 | tf_op jit(solution)/shard_map/ppermute | solution.py:568
  118.7 10.7 %collective-permute-start.27 = (bf16[688,128]{1,0:T(8,128)(2,1)S(1)}, bf16[688,128]{1,0:T(8,128)(2,1)S(1)}, u32[]{:S(2)}, u32[]{:S(2)}) collective-permute-start(bf16[688,128]{1,0:T(8,128)(2,1)S(1)} %merge.3), channel_id=1, source_target_pairs={{0,16},{8,24},{16,0},{24,8},{32,48},{40,56},{48,32},{56,40},{64,80... | collective-permute-start | bytes 528392 | tf_op jit(solution)/shard_map/ppermute | solution.py:568
  126.3 7.8 %collective-permute-start.20 = (bf16[128,640]{1,0:T(8,128)(2,1)S(1)}, bf16[128,640]{1,0:T(8,128)(2,1)S(1)}, u32[]{:S(2)}, u32[]{:S(2)}) collective-permute-start(bf16[128,640]{1,0:T(8,128)(2,1)S(1)} %combine.2.attn_near), channel_id=1, source_target_pairs={{0,4},{1,5},{2,6},{3,7},{4,0},{5,1},{6,2},{7,3},{8,12},{9,13},{10,... | collective-permute-start | bytes 491528 | tf_op jit(solution)/shard_map/ppermute | solution.py:582
  130.1 13.7 %collective-permute-start.28 = (bf16[128,640]{1,0:T(8,128)(2,1)S(1)}, bf16[128,640]{1,0:T(8,128)(2,1)}, u32[]{:S(2)}, u32[]{:S(2)}) collective-permute-start(bf16[128,640]{1,0:T(8,128)(2,1)S(1)} %combine.3.attn_near), channel_id=1, source_target_pairs={{0,4},{1,5},{2,6},{3,7},{4,0},{5,1},{6,2},{7,3},{8,12},{9,13},{10,... | collective-permute-start | bytes 491528 | tf_op jit(solution)/shard_map/ppermute | solution.py:582
  138.4 0.7 copy-start
  139.1 13.4 %collective-permute-start.23 = (bf16[128,640]{1,0:T(8,128)(2,1)}, bf16[128,640]{1,0:T(8,128)(2,1)}, u32[]{:S(2)}, u32[]{:S(2)}) collective-permute-start(bf16[128,640]{1,0:T(8,128)(2,1)} %get-tuple-element.56), channel_id=1, source_target_pairs={{0,1},{1,0},{2,3},{3,2},{4,5},{5,4},{6,7},{7,6},{8,9},{9,8},{10,11... | collective-permute-start | bytes 491528 | tf_op jit(solution)/shard_map/ppermute | solution.py:609
  140.7 12.1 %collective-permute-start.24 = (bf16[128,640]{1,0:T(8,128)(2,1)}, bf16[128,640]{1,0:T(8,128)(2,1)}, u32[]{:S(2)}, u32[]{:S(2)}) collective-permute-start(bf16[128,640]{1,0:T(8,128)(2,1)} %get-tuple-element.57), channel_id=1, source_target_pairs={{0,2},{1,3},{2,0},{3,1},{4,6},{5,7},{6,4},{7,5},{8,10},{9,11},{10,... | collective-permute-start | bytes 491528 | tf_op jit(solution)/shard_map/ppermute | solution.py:609
  143.6 9.2 %collective-permute-start.25 = (bf16[128,640]{1,0:T(8,128)(2,1)}, bf16[128,640]{1,0:T(8,128)(2,1)}, u32[]{:S(2)}, u32[]{:S(2)}) collective-permute-start(bf16[128,640]{1,0:T(8,128)(2,1)} %get-tuple-element.58), channel_id=1, source_target_pairs={{0,3},{1,2},{2,1},{3,0},{4,7},{5,6},{6,5},{7,4},{8,11},{9,10},{10,... | collective-permute-start | bytes 491528 | tf_op jit(solution)/shard_map/ppermute | solution.py:609
  143.8 8.9 %copy-start.1 = (f32[128,640]{1,0:T(8,128)S(1)}, f32[128,640]{1,0:T(8,128)}, u32[]{:S(2)}) copy-start(f32[128,640]{1,0:T(8,128)} %copy-done) | copy-start | bytes 983044
  147.9 16.6 %copy-start.13 = (bf16[640]{0:T(1024)(128)(2,1)S(1)}, bf16[640]{0:T(1024)(128)(2,1)}, u32[]{:S(2)}) copy-start(bf16[640]{0:T(1024)(128)(2,1)} %param.21) | copy-start | bytes 3844
  147.9 6.0 %collective-permute-start.29 = (bf16[128,640]{1,0:T(8,128)(2,1)S(1)}, bf16[128,640]{1,0:T(8,128)(2,1)S(1)}, u32[]{:S(2)}, u32[]{:S(2)}) collective-permute-start(bf16[128,640]{1,0:T(8,128)(2,1)S(1)} %get-tuple-element.65), channel_id=1, source_target_pairs={{0,1},{1,0},{2,3},{3,2},{4,5},{5,4},{6,7},{7,6},{8,9},{9,8},{10,11... | collective-permute-start | bytes 491528 | tf_op jit(solution)/shard_map/ppermute | solution.py:609
  148.4 9.2 %collective-permute-start.30 = (bf16[128,640]{1,0:T(8,128)(2,1)S(1)}, bf16[128,640]{1,0:T(8,128)(2,1)S(1)}, u32[]{:S(2)}, u32[]{:S(2)}) collective-permute-start(bf16[128,640]{1,0:T(8,128)(2,1)S(1)} %get-tuple-element.66), channel_id=1, source_target_pairs={{0,2},{1,3},{2,0},{3,1},{4,6},{5,7},{6,4},{7,5},{8,10},{9,11},{10,... | collective-permute-start | bytes 491528 | tf_op jit(solution)/shard_map/ppermute | solution.py:609
  152.5 6.8 %collective-permute-start.31 = (bf16[128,640]{1,0:T(8,128)(2,1)S(1)}, bf16[128,640]{1,0:T(8,128)(2,1)S(1)}, u32[]{:S(2)}, u32[]{:S(2)}) collective-permute-start(bf16[128,640]{1,0:T(8,128)(2,1)S(1)} %get-tuple-element.67), channel_id=1, source_target_pairs={{0,3},{1,2},{2,1},{3,0},{4,7},{5,6},{6,5},{7,4},{8,11},{9,10},{10,... | collective-permute-start | bytes 491528 | tf_op jit(solution)/shard_map/ppermute | solution.py:609
  160.5 12.6 %copy-start.12 = (bf16[256,640]{1,0:T(8,128)(2,1)}, bf16[256,640]{1,0:T(8,128)(2,1)S(1)}, u32[]{:S(2)}) copy-start(bf16[256,640]{1,0:T(8,128)(2,1)S(1)} %get-tuple-element.74) | copy-start | bytes 983044
  161.2 11.0 %all-to-all-start = ((f32[8,8,128]{2,1,0:T(8,128)}), f32[8,8,128]{2,1,0:T(8,128)S(1)}, u32[]{:S(2)}, u32[]{:S(2)}) async-start(f32[8,8,128]{2,1,0:T(8,128)} %broadcast_in_dim.88), calls=%async_computation | async-start | bytes 65536 | tf_op jit(solution)/shard_map/all_to_all | solution.py:618

commit v4 on v1

--- a/solution.py
+++ b/solution.py
@@ -610,8 +610,11 @@
     widened = hidden.astype(f32)
     squares = jnp.sum(widened * widened, axis=1).reshape(slots // HD, HD)
     squares = jnp.pad(squares, ((0, 8 - slots // HD), (0, 0)))
-    spread = lax.all_to_all(jnp.broadcast_to(squares[None], (ways, 8, HD)), "tp", 0, 0)
-    row_squares = jnp.sum(spread, axis=0)[: slots // HD].reshape(slots)
+    spread = squares
+    for k in (2, 3, 1):
+        spread = spread + lax.ppermute(squares, "tp", [(i, i ^ k) for i in range(ways)])
+    spread = spread + lax.ppermute(spread, "tp", [(i, i ^ FAR) for i in range(ways)])
+    row_squares = spread[: slots // HD].reshape(slots)
     scale_rows = lax.rsqrt(row_squares / width + EPSILON)
     normed = (widened * scale_rows[:, None] * norm_gain.astype(f32)[None, :]).astype(bf16)
     return (hidden, normed, cache_key)

time: 170 us -> 170 us (level)
    all_to_all x1 -> x0, waiting for transfers between devices: 7.67 us -> none  [shards(): lax.all_to_all(jnp.broadcast_to(squares[None], (ways, 8, HD)), 'tp', 0, 0)]
    ppermute x0 -> x4, waiting for transfers between devices: none -> 7.4 us  [the longest x1 4.84 us: shards(): lax.ppermute(spread, 'tp', [(i, i ^ FAR) for i in range(ways)])]
    ppermute x0 -> x4, starting transfers between devices: none -> 3.84 us  [the longest x3 3.58 us: shards(): lax.ppermute(squares, 'tp', [(i, i ^ k) for i in range(ways)])]
    all_to_all x1 -> x0, starting transfers between devices: 3.34 us -> none  [shards(): lax.all_to_all(jnp.broadcast_to(squares[None], (ways, 8, HD)), 'tp', 0, 0)]
  transfers between devices with their start and end apart: 33 -> 36, of which waited for: 14 -> 16; matrix products, arithmetic and copies ran while one was open for 4% -> 4% of each run, Pallas kernels for 22% -> 22%
where the time goes in v4:
time: 170 us; the launch traced here: 169 us
  waiting for transfers between devices  73 us (43%)
  starting transfers between devices  44.7 us (26%)
  Pallas kernels  37.3 us (22%)
  local copies, waits for them, and re-layouts  7.61 us (4%)
  other arithmetic  5.64 us (3%)
    ppermute x3, waiting for transfers between devices, shards(): queries.append(lax.ppermute(suffix_query, 'req', beside(k)))  40.7 us
    ppermute x6, starting transfers between devices, shards(): moving_down = lax.ppermute(moving_down, 'req', down_pairs)  17.5 us
    pallas_call x1, Pallas kernels, shards(): pl.pallas_call(make_first(base, len(parts)), out_shape=(shape((every, lin...  13 us
    pallas_call x2, Pallas kernels, shards(): pl.pallas_call(make_middle(base, len(parts)), out_shape=state_shapes, in_...  10 us
    ppermute x6, starting transfers between devices, shards(): piece = lax.ppermute(pieces[k], 'tp', [(i, i ^ k) for i in range(ways)])  9.57 us
    pallas_call x2, Pallas kernels, shards(): pl.pallas_call(project_kernel, out_shape=tuple((shape((TILE, columns), bf...  7.95 us
    ppermute x2, waiting for transfers between devices, shards(): crossed.append(lax.ppermute(merged, 'req', beside(2)))  7.48 us
    ppermute x6, waiting for transfers between devices, shards(): moving_up = lax.ppermute(moving_up, 'req', up_pairs)  6.23 us
  transfers between devices with their start and end apart: 36, of which 16 were waited for; matrix products, arithmetic and copies ran while one was open for 4% of the time, Pallas kernels for 22%

profile of v4, /device:TPU:2, one launch (start us, length us, event | category | flops | bytes accessed | tf_op | source)
XLA Modules:
  0.0 169.3 jit_solution(11291788510699716609)
XLA Ops:
  0.7 1.0 constant_dynamic-update-slice_fusion.1
  1.8 1.0 constant_dynamic-update-slice_fusion
  2.8 2.0 %collective-permute-start.4 = (bf16[2,512,128]{2,1,0:T(8,128)(2,1)S(1)}, bf16[2,512,128]{2,1,0:T(8,128)(2,1)}, u32[]{:S(2)}, u32[]{:S(2)}) collective-permute-start(bf16[2,512,128]{2,1,0:T(8,128)(2,1)S(1)} %get-tuple-element.76.rest_0_), channel_id=1, source_target_pairs={{0,32},{8,40},{16,48},{24,56},{32,64},{40,72},{48,80},{56,88},{64,... | collective-permute-start | bytes 786440 | tf_op jit(solution)/shard_map/ppermute | solution.py:415
  4.8 4.0 %collective-permute-start.5 = (bf16[2,512,128]{2,1,0:T(8,128)(2,1)S(1)}, bf16[2,512,128]{2,1,0:T(8,128)(2,1)S(1)}, u32[]{:S(2)}, u32[]{:S(2)}) collective-permute-start(bf16[2,512,128]{2,1,0:T(8,128)(2,1)S(1)} %get-tuple-element.76.rest_0_), channel_id=1, source_target_pairs={{0,224},{8,232},{16,240},{24,248},{32,0},{40,8},{48,16},{56,24},{6... | collective-permute-start | bytes 786440 | tf_op jit(solution)/shard_map/ppermute | solution.py:416
  8.9 0.5 collective-permute-start
  9.4 2.7 %constant_dynamic-slice_fusion = bf16[640,1280]{1,0:T(8,128)(2,1)} fusion(bf16[640,5120]{1,0:T(8,128)(2,1)} %weight_in.3, s32[]{:T(128)S(6)} %select_n.87), kind=kLoop, calls=%fused_computation.41 | loop fusion | bytes 3276804 | tf_op jit(solution)/shard_map/dynamic_slice | solution.py:397
  12.1 2.1 %collective-permute-start.21 = (bf16[640,1280]{1,0:T(8,128)(2,1)}, bf16[640,1280]{1,0:T(8,128)(2,1)S(1)}, u32[]{:S(2)}, u32[]{:S(2)}) collective-permute-start(bf16[640,1280]{1,0:T(8,128)(2,1)} %constant_dynamic-slice_fusion), channel_id=1, source_target_pairs={{0,4},{1,5},{2,6},{3,7},{4,0},{5,1},{6,2},{7,3},{8,12},{9,13},{10,... | collective-permute-start | bytes 4915208 | tf_op jit(solution)/shard_map/ppermute | solution.py:400
  14.4 0.2 select_reduce_fusion.3
  14.6 0.2 select_reduce_fusion.2
  14.8 0.2 select_reduce_fusion.5
  15.0 1.5 collective-permute-start.1
  16.5 1.9 %collective-permute-start.7 = (bf16[2,512,128]{2,1,0:T(8,128)(2,1)}, bf16[2,512,128]{2,1,0:T(8,128)(2,1)}, u32[]{:S(2)}, u32[]{:S(2)}) collective-permute-start(bf16[2,512,128]{2,1,0:T(8,128)(2,1)} %collective-permute-done.3.rest_1_), channel_id=1, source_target_pairs={{0,224},{8,232},{16,240},{24,248},{32,0},{40,8},{48,16},{56,24},{6... | collective-permute-start | bytes 786440 | tf_op jit(solution)/shard_map/ppermute | solution.py:416
  18.5 1.3 fusion.4
  19.8 0.2 collective-permute-start.6
  19.9 0.5 copy-done.1
  20.5 39.1 %collective-permute-done.1.q2 = bf16[256,640]{1,0:T(8,128)(2,1)S(1)} collective-permute-done((bf16[256,640]{1,0:T(8,128)(2,1)S(1)}, bf16[256,640]{1,0:T(8,128)(2,1)S(1)}, u32[]{:S(2)}, u32[]{:S(2)}) %collective-permute-start.1) | collective-permute-done | bytes 327712 | tf_op jit(solution)/shard_map/ppermute | solution.py:407
  59.5 3.2 %collective-permute-start.11 = (bf16[2,512,128]{2,1,0:T(8,128)(2,1)}, bf16[2,512,128]{2,1,0:T(8,128)(2,1)S(1)}, u32[]{:S(2)}, u32[]{:S(2)}) collective-permute-start(bf16[2,512,128]{2,1,0:T(8,128)(2,1)} %collective-permute-done.7.rest_5_), channel_id=1, source_target_pairs={{0,224},{8,232},{16,240},{24,248},{32,0},{40,8},{48,16},{56,24},{6... | collective-permute-start | bytes 786440 | tf_op jit(solution)/shard_map/ppermute | solution.py:416
  63.1 1.7 collective-permute-done.2.q3
  64.7 1.9 %collective-permute-start.9 = (bf16[2,512,128]{2,1,0:T(8,128)(2,1)}, bf16[2,512,128]{2,1,0:T(8,128)(2,1)S(1)}, u32[]{:S(2)}, u32[]{:S(2)}) collective-permute-start(bf16[2,512,128]{2,1,0:T(8,128)(2,1)} %copy-done.1), channel_id=1, source_target_pairs={{0,224},{8,232},{16,240},{24,248},{32,0},{40,8},{48,16},{56,24},{6... | collective-permute-start | bytes 786440 | tf_op jit(solution)/shard_map/ppermute | solution.py:416
  66.8 0.6 collective-permute-done.8.rest_0_
  67.4 3.2 %collective-permute-start.15 = (bf16[2,512,128]{2,1,0:T(8,128)(2,1)S(1)}, bf16[2,512,128]{2,1,0:T(8,128)(2,1)S(1)}, u32[]{:S(2)}, u32[]{:S(2)}) collective-permute-start(bf16[2,512,128]{2,1,0:T(8,128)(2,1)S(1)} %collective-permute-done.11.rest_3_), channel_id=1, source_target_pairs={{0,224},{8,232},{16,240},{24,248},{32,0},{40,8},{48,16},{56,24},{6... | collective-permute-start | bytes 786440 | tf_op jit(solution)/shard_map/ppermute | solution.py:416
  70.7 1.2 pad_maximum_fusion
  71.9 1.5 own.1
  73.4 0.7 collective-permute-done.9.rest_1_
  74.1 3.1 %collective-permute-start.13 = (bf16[2,512,128]{2,1,0:T(8,128)(2,1)S(1)}, bf16[2,512,128]{2,1,0:T(8,128)(2,1)S(1)}, u32[]{:S(2)}, u32[]{:S(2)}) collective-permute-start(bf16[2,512,128]{2,1,0:T(8,128)(2,1)S(1)} %collective-permute-done.9.rest_1_), channel_id=1, source_target_pairs={{0,224},{8,232},{16,240},{24,248},{32,0},{40,8},{48,16},{56,24},{6... | collective-permute-start | bytes 786440 | tf_op jit(solution)/shard_map/ppermute | solution.py:416
  77.3 5.6 %collective-permute-done.12.rest_0_ = bf16[2,512,128]{2,1,0:T(8,128)(2,1)S(1)} collective-permute-done((bf16[2,512,128]{2,1,0:T(8,128)(2,1)S(1)}, bf16[2,512,128]{2,1,0:T(8,128)(2,1)S(1)}, u32[]{:S(2)}, u32[]{:S(2)}) %collective-permute-start.12) | collective-permute-done | bytes 262176 | tf_op jit(solution)/shard_map/ppermute | solution.py:415
  82.9 3.2 %collective-permute-start.17 = (bf16[2,512,128]{2,1,0:T(8,128)(2,1)S(1)}, bf16[2,512,128]{2,1,0:T(8,128)(2,1)S(1)}, u32[]{:S(2)}, u32[]{:S(2)}) collective-permute-start(bf16[2,512,128]{2,1,0:T(8,128)(2,1)S(1)} %collective-permute-done.15.rest_3_), channel_id=1, source_target_pairs={{0,224},{8,232},{16,240},{24,248},{32,0},{40,8},{48,16},{56,24},{6... | collective-permute-start | bytes 786440 | tf_op jit(solution)/shard_map/ppermute | solution.py:422
  86.1 0.9 copy-done.2
  87.1 13.0 %first.1 = (bf16[9,640,128]{2,1,0:T(8,128)(2,1)S(1)}, f32[9,128,640]{2,1,0:T(8,128)S(1)}, f32[9,1,640]{2,1,0:T(1,128)S(1)}, f32[9,1,640]{2,1,0:T(1,128)S(1)}) custom-call(s32[72]{0:T(128)S(1)} %pad_add_fusion.1.meta, bf16[2,640,128]{2,1,0:T(8,128)(2,1)S(1)} %get-tuple-element.36.q_own, f32[2,128,640]{2,1,0:T(8,128)S(1)} %get-tuple-element.37.acc_own, ...), custom_call_target="tpu_custom_call" | custom-call | flops 2013265920 | bytes 8388608 | tf_op jit(solution)/shard_map/first/pallas_call | solution.py:500
  100.1 5.0 %middle.2 = (f32[9,128,640]{2,1,0:T(8,128)S(1)}, f32[9,1,640]{2,1,0:T(1,128)S(1)}, f32[9,1,640]{2,1,0:T(1,128)S(1)}) custom-call(s32[72]{0:T(128)S(1)} %pad_add_fusion.1.meta, bf16[9,640,128]{2,1,0:T(8,128)(2,1)S(1)} %get-tuple-element.40.q_ref, f32[9,128,640]{2,1,0:T(8,128)S(1)} %get-tuple-element.41.acc_in, f32[9,1,640]{2,1,0:T(1,128)S(1)} %get-tuple-element.42.max_in, ...), custom_call_target="tpu_custom_call" | custom-call | flops 1342177280 | bytes 8388608 | tf_op jit(solution)/shard_map/middle/pallas_call | solution.py:513
  105.1 5.0 %middle.3 = (f32[9,128,640]{2,1,0:T(8,128)S(1)}, f32[9,1,640]{2,1,0:T(1,128)S(1)}, f32[9,1,640]{2,1,0:T(1,128)S(1)}) custom-call(s32[72]{0:T(128)S(1)} %pad_add_fusion.1.meta, bf16[9,640,128]{2,1,0:T(8,128)(2,1)S(1)} %get-tuple-element.40.q_ref, f32[9,128,640]{2,1,0:T(8,128)S(1)} %get-tuple-element.44.acc_in, f32[9,1,640]{2,1,0:T(1,128)S(1)} %get-tuple-element.45.max_in, ...), custom_call_target="tpu_custom_call" | custom-call | flops 1342177280 | bytes 8388608 | tf_op jit(solution)/shard_map/middle/pallas_call | solution.py:513
  110.2 3.2 %last.1 = (f32[128,640]{1,0:T(8,128)S(1)}, f32[16,128]{1,0:T(8,128)S(1)}, f32[128,640]{1,0:T(8,128)S(1)}, f32[16,128]{1,0:T(8,128)S(1)}, bf16[2,688,128]{2,1,0:T...) custom-call(s32[72]{0:T(128)S(1)} %pad_add_fusion.1.meta, ...), custom_call_target="tpu_custom_call" | custom-call | flops 671088640 | bytes 8388608 | tf_op jit(solution)/shard_map/last/pallas_call | solution.py:526
  113.4 0.5 collective-permute-start.26
  113.9 1.2 collective-permute-done.18.swapped
  115.3 0.3 collective-permute-done.26.swapped
  115.7 1.8 %collective-permute-start.27 = (bf16[688,128]{1,0:T(8,128)(2,1)S(1)}, bf16[688,128]{1,0:T(8,128)(2,1)S(1)}, u32[]{:S(2)}, u32[]{:S(2)}) collective-permute-start(bf16[688,128]{1,0:T(8,128)(2,1)S(1)} %merge.3), channel_id=1, source_target_pairs={{0,16},{8,24},{16,0},{24,8},{32,48},{40,56},{48,32},{56,40},{64,80... | collective-permute-start | bytes 528392 | tf_op jit(solution)/shard_map/ppermute | solution.py:563
  117.5 5.1 %collective-permute-done.19.crossed = bf16[688,128]{1,0:T(8,128)(2,1)S(1)} collective-permute-done((bf16[688,128]{1,0:T(8,128)(2,1)S(1)}, bf16[688,128]{1,0:T(8,128)(2,1)S(1)}, u32[]{:S(2)}, u32[]{:S(2)}) %collective-permute-start.19) | collective-permute-done | bytes 176160 | tf_op jit(solution)/shard_map/ppermute | solution.py:563
  122.6 0.7 combine.2.attn_near
  123.3 0.7 collective-permute-start.20
  124.0 2.3 %collective-permute-done.27.crossed = bf16[688,128]{1,0:T(8,128)(2,1)S(1)} collective-permute-done((bf16[688,128]{1,0:T(8,128)(2,1)S(1)}, bf16[688,128]{1,0:T(8,128)(2,1)S(1)}, u32[]{:S(2)}, u32[]{:S(2)}) %collective-permute-start.27) | collective-permute-done | bytes 176160 | tf_op jit(solution)/shard_map/ppermute | solution.py:563
  126.4 0.7 combine.3.attn_near
  127.1 0.9 collective-permute-start.28
  128.1 3.1 %collective-permute-done.20.attn_far = bf16[128,640]{1,0:T(8,128)(2,1)S(1)} collective-permute-done((bf16[128,640]{1,0:T(8,128)(2,1)S(1)}, bf16[128,640]{1,0:T(8,128)(2,1)S(1)}, u32[]{:S(2)}, u32[]{:S(2)}) %collective-permute-start.20) | collective-permute-done | bytes 163872 | tf_op jit(solution)/shard_map/ppermute | solution.py:577
  131.2 1.2 copy-done.5
  132.4 4.0 %project.2 = (f32[128,640]{1,0:T(8,128)S(1)}, bf16[128,640]{1,0:T(8,128)(2,1)S(1)}, bf16[128,640]{1,0:T(8,128)(2,1)S(1)}, bf16[128,640]{1,0:T(8,128)(2,1)S(1)}) custom-call(s32[2]{0:T(128)S(1)} %pad_add_fusion.where, bf16[128,640]{1,0:T(8,128)(2,1)S(1)} %combine.2.attn_near, bf16[128,640]{1,0:T(8,128)(2,1)S(1)} %collective-permute-done.20.attn_far, ...), custom_call_target="tpu_custom_call" | custom-call | flops 838860800 | bytes 8388608 | tf_op jit(solution)/shard_map/project/pallas_call | solution.py:582
  136.4 1.7 collective-permute-start.23
  138.0 2.6 %collective-permute-start.24 = (bf16[128,640]{1,0:T(8,128)(2,1)S(1)}, bf16[128,640]{1,0:T(8,128)(2,1)S(1)}, u32[]{:S(2)}, u32[]{:S(2)}) collective-permute-start(bf16[128,640]{1,0:T(8,128)(2,1)S(1)} %get-tuple-element.57), channel_id=1, source_target_pairs={{0,2},{1,3},{2,0},{3,1},{4,6},{5,7},{6,4},{7,5},{8,10},{9,11},{10,... | collective-permute-start | bytes 491528 | tf_op jit(solution)/shard_map/ppermute | solution.py:604
  140.6 0.5 collective-permute-start.25
  141.2 4.0 %project.3 = (f32[128,640]{1,0:T(8,128)S(1)}, bf16[128,640]{1,0:T(8,128)(2,1)S(1)}, bf16[128,640]{1,0:T(8,128)(2,1)S(1)}, bf16[128,640]{1,0:T(8,128)(2,1)S(1)}) custom-call(s32[2]{0:T(128)S(1)} %pad_add_fusion.where, bf16[128,640]{1,0:T(8,128)(2,1)S(1)} %combine.3.attn_near, bf16[128,640]{1,0:T(8,128)(2,1)S(1)} %collective-permute-done.28.attn_far, ...), custom_call_target="tpu_custom_call" | custom-call | flops 838860800 | bytes 8388608 | tf_op jit(solution)/shard_map/project/pallas_call | solution.py:582
  145.1 0.4 collective-permute-start.29
  145.6 3.5 %collective-permute-start.30 = (bf16[128,640]{1,0:T(8,128)(2,1)S(1)}, bf16[128,640]{1,0:T(8,128)(2,1)S(1)}, u32[]{:S(2)}, u32[]{:S(2)}) collective-permute-start(bf16[128,640]{1,0:T(8,128)(2,1)S(1)} %get-tuple-element.66), channel_id=1, source_target_pairs={{0,2},{1,3},{2,0},{3,1},{4,6},{5,7},{6,4},{7,5},{8,10},{9,11},{10,... | collective-permute-start | bytes 491528 | tf_op jit(solution)/shard_map/ppermute | solution.py:604
  149.1 0.8 collective-permute-start.31
  150.0 0.5 collective-permute-done.29
  150.6 3.7 %collective-permute-done.30 = bf16[128,640]{1,0:T(8,128)(2,1)S(1)} collective-permute-done((bf16[128,640]{1,0:T(8,128)(2,1)S(1)}, bf16[128,640]{1,0:T(8,128)(2,1)S(1)}, u32[]{:S(2)}, u32[]{:S(2)}) %collective-permute-start.30) | collective-permute-done | bytes 163872 | tf_op jit(solution)/shard_map/ppermute | solution.py:604
  154.2 1.7 %collective-permute-done.31 = bf16[128,640]{1,0:T(8,128)(2,1)S(1)} collective-permute-done((bf16[128,640]{1,0:T(8,128)(2,1)S(1)}, bf16[128,640]{1,0:T(8,128)(2,1)S(1)}, u32[]{:S(2)}, u32[]{:S(2)}) %collective-permute-start.31) | collective-permute-done | bytes 163872 | tf_op jit(solution)/shard_map/ppermute | solution.py:604
  156.0 1.2 fusion
  157.2 0.4 collective-permute-start.32
  157.6 2.2 %collective-permute-start.33 = (f32[8,128]{1,0:T(8,128)S(1)}, f32[8,128]{1,0:T(8,128)S(1)}, u32[]{:S(2)}, u32[]{:S(2)}) collective-permute-start(f32[8,128]{1,0:T(8,128)S(1)} %pad.4), channel_id=1, source_target_pairs={{0,3},{1,2},{2,1},{3,0},{4,7},{5,6},{6,5},{7,4},{8,11},{9,10},{10,... | collective-permute-start | bytes 12296 | tf_op jit(solution)/shard_map/ppermute | solution.py:615
  159.7 1.0 collective-permute-start.34
  160.8 1.7 collective-permute-done.32
  162.4 0.9 collective-permute-done.34
  163.3 0.3 collective-permute-start.35
  163.6 4.8 %collective-permute-done.35 = f32[8,128]{1,0:T(8,128)S(1)} collective-permute-done((f32[8,128]{1,0:T(8,128)S(1)}, f32[8,128]{1,0:T(8,128)S(1)}, u32[]{:S(2)}, u32[]{:S(2)}) %collective-permute-start.35) | collective-permute-done | bytes 4128 | tf_op jit(solution)/shard_map/ppermute | solution.py:616
  168.5 0.9 fusion.2
  (76 shorter events, 1.3 us)
Async XLA Ops:
  0.7 13.6 %copy-start.13 = (s32[32]{0:T(128)S(1)}, s32[32]{0:T(128)}, u32[]{:S(2)}) copy-start(s32[32]{0:T(128)} %param.24) | copy-start | bytes 388
  0.7 13.7 %copy-start.11 = (s32[16]{0:T(128)S(1)}, s32[16]{0:T(128)}, u32[]{:S(2)}) copy-start(s32[16]{0:T(128)} %constant.122.clone) | copy-start | bytes 196
  0.7 13.7 %copy-start.12 = (s32[16]{0:T(128)S(1)}, s32[16]{0:T(128)}, u32[]{:S(2)}) copy-start(s32[16]{0:T(128)} %constant.123.clone) | copy-start | bytes 196
  0.7 13.9 %copy-start.8 = (s32[32]{0:T(128)S(1)}, s32[32]{0:T(128)}, u32[]{:S(2)}) copy-start(s32[32]{0:T(128)} %param.22) | copy-start | bytes 388
  0.7 13.9 %copy-start.9 = (s32[32]{0:T(128)S(1)}, s32[32]{0:T(128)}, u32[]{:S(2)}) copy-start(s32[32]{0:T(128)} %param.23) | copy-start | bytes 388
  0.7 13.9 %copy-start.10 = (s32[32,1]{0,1:T(1,128)S(1)}, s32[32,1]{0,1:T(1,128)}, u32[]{:S(2)}) copy-start(s32[32,1]{0,1:T(1,128)} %param.25) | copy-start | bytes 388
  0.7 14.3 %copy-start = (bf16[256,640]{1,0:T(8,128)(2,1)S(1)}, bf16[256,640]{1,0:T(8,128)(2,1)}, u32[]{:S(2)}) copy-start(bf16[256,640]{1,0:T(8,128)(2,1)} %q_in.1) | copy-start | bytes 983044
  2.8 69.2 %copy-start.3 = (bf16[256,128]{1,0:T(8,128)(2,1)S(1)}, bf16[256,128]{1,0:T(8,128)(2,1)}, u32[]{:S(2)}) copy-start(bf16[256,128]{1,0:T(8,128)(2,1)} %k_in.1) | copy-start | bytes 196612
  2.8 69.2 %copy-start.4 = (bf16[256,128]{1,0:T(8,128)(2,1)S(1)}, bf16[256,128]{1,0:T(8,128)(2,1)}, u32[]{:S(2)}) copy-start(bf16[256,128]{1,0:T(8,128)(2,1)} %v_in.1) | copy-start | bytes 196612
  2.8 13.7 %collective-permute-start.4 = (bf16[2,512,128]{2,1,0:T(8,128)(2,1)S(1)}, bf16[2,512,128]{2,1,0:T(8,128)(2,1)}, u32[]{:S(2)}, u32[]{:S(2)}) collective-permute-start(bf16[2,512,128]{2,1,0:T(8,128)(2,1)S(1)} %get-tuple-element.76.rest_0_), channel_id=1, source_target_pairs={{0,32},{8,40},{16,48},{24,56},{32,64},{40,72},{48,80},{56,88},{64,... | collective-permute-start | bytes 786440 | tf_op jit(solution)/shard_map/ppermute | solution.py:415
  4.8 14.9 %collective-permute-start.5 = (bf16[2,512,128]{2,1,0:T(8,128)(2,1)S(1)}, bf16[2,512,128]{2,1,0:T(8,128)(2,1)S(1)}, u32[]{:S(2)}, u32[]{:S(2)}) collective-permute-start(bf16[2,512,128]{2,1,0:T(8,128)(2,1)S(1)} %get-tuple-element.76.rest_0_), channel_id=1, source_target_pairs={{0,224},{8,232},{16,240},{24,248},{32,0},{40,8},{48,16},{56,24},{6... | collective-permute-start | bytes 786440 | tf_op jit(solution)/shard_map/ppermute | solution.py:416
  8.9 6.1 %collective-permute-start.3 = (bf16[2,512,128]{2,1,0:T(8,128)(2,1)S(1)}, bf16[2,512,128]{2,1,0:T(8,128)(2,1)}, u32[]{:S(2)}, u32[]{:S(2)}) collective-permute-start(bf16[2,512,128]{2,1,0:T(8,128)(2,1)S(1)} %get-tuple-element.75), channel_id=1, source_target_pairs={{0,8},{8,0},{16,24},{24,16},{32,40},{40,32},{48,56},{56,48},{64,72... | collective-permute-start | bytes 786440 | tf_op jit(solution)/shard_map/ppermute | solution.py:404
  8.9 10.9 %collective-permute-start = (bf16[256,640]{1,0:T(8,128)(2,1)}, bf16[256,640]{1,0:T(8,128)(2,1)S(1)}, u32[]{:S(2)}, u32[]{:S(2)}) collective-permute-start(bf16[256,640]{1,0:T(8,128)(2,1)} %q_in.1), channel_id=1, source_target_pairs={{0,8},{8,0},{16,24},{24,16},{32,40},{40,32},{48,56},{56,48},{64,72... | collective-permute-start | bytes 983048 | tf_op jit(solution)/shard_map/ppermute | solution.py:407
  12.1 50.8 %collective-permute-start.21 = (bf16[640,1280]{1,0:T(8,128)(2,1)}, bf16[640,1280]{1,0:T(8,128)(2,1)S(1)}, u32[]{:S(2)}, u32[]{:S(2)}) collective-permute-start(bf16[640,1280]{1,0:T(8,128)(2,1)} %constant_dynamic-slice_fusion), channel_id=1, source_target_pairs={{0,4},{1,5},{2,6},{3,7},{4,0},{5,1},{6,2},{7,3},{8,12},{9,13},{10,... | collective-permute-start | bytes 4915208 | tf_op jit(solution)/shard_map/ppermute | solution.py:400
  15.0 44.5 %collective-permute-start.1 = (bf16[256,640]{1,0:T(8,128)(2,1)S(1)}, bf16[256,640]{1,0:T(8,128)(2,1)S(1)}, u32[]{:S(2)}, u32[]{:S(2)}) collective-permute-start(bf16[256,640]{1,0:T(8,128)(2,1)S(1)} %copy-done), channel_id=1, source_target_pairs={{0,16},{8,24},{16,0},{24,8},{32,48},{40,56},{48,32},{56,40},{64,80... | collective-permute-start | bytes 983048 | tf_op jit(solution)/shard_map/ppermute | solution.py:407
  16.5 43.0 %collective-permute-start.7 = (bf16[2,512,128]{2,1,0:T(8,128)(2,1)}, bf16[2,512,128]{2,1,0:T(8,128)(2,1)}, u32[]{:S(2)}, u32[]{:S(2)}) collective-permute-start(bf16[2,512,128]{2,1,0:T(8,128)(2,1)} %collective-permute-done.3.rest_1_), channel_id=1, source_target_pairs={{0,224},{8,232},{16,240},{24,248},{32,0},{40,8},{48,16},{56,24},{6... | collective-permute-start | bytes 786440 | tf_op jit(solution)/shard_map/ppermute | solution.py:416
  19.8 0.7 copy-start.1
  19.8 45.0 %collective-permute-start.2 = (bf16[256,640]{1,0:T(8,128)(2,1)S(1)}, bf16[256,640]{1,0:T(8,128)(2,1)}, u32[]{:S(2)}, u32[]{:S(2)}) collective-permute-start(bf16[256,640]{1,0:T(8,128)(2,1)S(1)} %copy-done), channel_id=1, source_target_pairs={{0,24},{8,16},{16,8},{24,0},{32,56},{40,48},{48,40},{56,32},{64,88... | collective-permute-start | bytes 983048 | tf_op jit(solution)/shard_map/ppermute | solution.py:407
  19.8 46.9 %collective-permute-start.6 = (bf16[2,512,128]{2,1,0:T(8,128)(2,1)}, bf16[2,512,128]{2,1,0:T(8,128)(2,1)}, u32[]{:S(2)}, u32[]{:S(2)}) collective-permute-start(bf16[2,512,128]{2,1,0:T(8,128)(2,1)} %collective-permute-done.3.rest_1_), channel_id=1, source_target_pairs={{0,32},{8,40},{16,48},{24,56},{32,64},{40,72},{48,80},{56,88},{64,... | collective-permute-start | bytes 786440 | tf_op jit(solution)/shard_map/ppermute | solution.py:415
  59.5 7.8 %collective-permute-start.8 = (bf16[2,512,128]{2,1,0:T(8,128)(2,1)}, bf16[2,512,128]{2,1,0:T(8,128)(2,1)S(1)}, u32[]{:S(2)}, u32[]{:S(2)}) collective-permute-start(bf16[2,512,128]{2,1,0:T(8,128)(2,1)} %collective-permute-done.4.rest_2_), channel_id=1, source_target_pairs={{0,32},{8,40},{16,48},{24,56},{32,64},{40,72},{48,80},{56,88},{64,... | collective-permute-start | bytes 786440 | tf_op jit(solution)/shard_map/ppermute | solution.py:415
  59.5 7.8 %collective-permute-start.11 = (bf16[2,512,128]{2,1,0:T(8,128)(2,1)}, bf16[2,512,128]{2,1,0:T(8,128)(2,1)S(1)}, u32[]{:S(2)}, u32[]{:S(2)}) collective-permute-start(bf16[2,512,128]{2,1,0:T(8,128)(2,1)} %collective-permute-done.7.rest_5_), channel_id=1, source_target_pairs={{0,224},{8,232},{16,240},{24,248},{32,0},{40,8},{48,16},{56,24},{6... | collective-permute-start | bytes 786440 | tf_op jit(solution)/shard_map/ppermute | solution.py:416
  63.0 68.2 %collective-permute-start.22 = (bf16[640,1280]{1,0:T(8,128)(2,1)S(1)}, bf16[640,1280]{1,0:T(8,128)(2,1)S(1)}, u32[]{:S(2)}, u32[]{:S(2)}) collective-permute-start(bf16[640,1280]{1,0:T(8,128)(2,1)S(1)} %collective-permute-done.21.mine_in), channel_id=1, source_target_pairs={{0,8},{8,0},{16,24},{24,16},{32,40},{40,32},{48,56},{56,48},{64,72... | collective-permute-start | bytes 4915208 | tf_op jit(solution)/shard_map/ppermute | solution.py:578
  64.7 9.4 %collective-permute-start.9 = (bf16[2,512,128]{2,1,0:T(8,128)(2,1)}, bf16[2,512,128]{2,1,0:T(8,128)(2,1)S(1)}, u32[]{:S(2)}, u32[]{:S(2)}) collective-permute-start(bf16[2,512,128]{2,1,0:T(8,128)(2,1)} %copy-done.1), channel_id=1, source_target_pairs={{0,224},{8,232},{16,240},{24,248},{32,0},{40,8},{48,16},{56,24},{6... | collective-permute-start | bytes 786440 | tf_op jit(solution)/shard_map/ppermute | solution.py:416
  66.7 10.6 %collective-permute-start.10 = (bf16[2,512,128]{2,1,0:T(8,128)(2,1)}, bf16[2,512,128]{2,1,0:T(8,128)(2,1)S(1)}, u32[]{:S(2)}, u32[]{:S(2)}) collective-permute-start(bf16[2,512,128]{2,1,0:T(8,128)(2,1)} %collective-permute-done.6.rest_4_), channel_id=1, source_target_pairs={{0,32},{8,40},{16,48},{24,56},{32,64},{40,72},{48,80},{56,88},{64,... | collective-permute-start | bytes 786440 | tf_op jit(solution)/shard_map/ppermute | solution.py:415
  67.4 15.5 %collective-permute-start.12 = (bf16[2,512,128]{2,1,0:T(8,128)(2,1)S(1)}, bf16[2,512,128]{2,1,0:T(8,128)(2,1)S(1)}, u32[]{:S(2)}, u32[]{:S(2)}) collective-permute-start(bf16[2,512,128]{2,1,0:T(8,128)(2,1)S(1)} %collective-permute-done.8.rest_0_), channel_id=1, source_target_pairs={{0,32},{8,40},{16,48},{24,56},{32,64},{40,72},{48,80},{56,88},{64,... | collective-permute-start | bytes 786440 | tf_op jit(solution)/shard_map/ppermute | solution.py:415
  67.4 15.5 %collective-permute-start.15 = (bf16[2,512,128]{2,1,0:T(8,128)(2,1)S(1)}, bf16[2,512,128]{2,1,0:T(8,128)(2,1)S(1)}, u32[]{:S(2)}, u32[]{:S(2)}) collective-permute-start(bf16[2,512,128]{2,1,0:T(8,128)(2,1)S(1)} %collective-permute-done.11.rest_3_), channel_id=1, source_target_pairs={{0,224},{8,232},{16,240},{24,248},{32,0},{40,8},{48,16},{56,24},{6... | collective-permute-start | bytes 786440 | tf_op jit(solution)/shard_map/ppermute | solution.py:416
  74.1 31.0 %collective-permute-start.13 = (bf16[2,512,128]{2,1,0:T(8,128)(2,1)S(1)}, bf16[2,512,128]{2,1,0:T(8,128)(2,1)S(1)}, u32[]{:S(2)}, u32[]{:S(2)}) collective-permute-start(bf16[2,512,128]{2,1,0:T(8,128)(2,1)S(1)} %collective-permute-done.9.rest_1_), channel_id=1, source_target_pairs={{0,224},{8,232},{16,240},{24,248},{32,0},{40,8},{48,16},{56,24},{6... | collective-permute-start | bytes 786440 | tf_op jit(solution)/shard_map/ppermute | solution.py:416
  77.3 27.8 %collective-permute-start.14 = (bf16[2,512,128]{2,1,0:T(8,128)(2,1)S(1)}, bf16[2,512,128]{2,1,0:T(8,128)(2,1)S(1)}, u32[]{:S(2)}, u32[]{:S(2)}) collective-permute-start(bf16[2,512,128]{2,1,0:T(8,128)(2,1)S(1)} %collective-permute-done.10.rest_2_), channel_id=1, source_target_pairs={{0,32},{8,40},{16,48},{24,56},{32,64},{40,72},{48,80},{56,88},{64,... | collective-permute-start | bytes 786440 | tf_op jit(solution)/shard_map/ppermute | solution.py:415
  82.9 27.3 %collective-permute-start.16 = (bf16[2,512,128]{2,1,0:T(8,128)(2,1)S(1)}, bf16[2,512,128]{2,1,0:T(8,128)(2,1)S(1)}, u32[]{:S(2)}, u32[]{:S(2)}) collective-permute-start(bf16[2,512,128]{2,1,0:T(8,128)(2,1)S(1)} %collective-permute-done.12.rest_0_), channel_id=1, source_target_pairs={{0,32},{8,40},{16,48},{24,56},{32,64},{40,72},{48,80},{56,88},{64,... | collective-permute-start | bytes 786440 | tf_op jit(solution)/shard_map/ppermute | solution.py:420
  82.9 27.3 %collective-permute-start.17 = (bf16[2,512,128]{2,1,0:T(8,128)(2,1)S(1)}, bf16[2,512,128]{2,1,0:T(8,128)(2,1)S(1)}, u32[]{:S(2)}, u32[]{:S(2)}) collective-permute-start(bf16[2,512,128]{2,1,0:T(8,128)(2,1)S(1)} %collective-permute-done.15.rest_3_), channel_id=1, source_target_pairs={{0,224},{8,232},{16,240},{24,248},{32,0},{40,8},{48,16},{56,24},{6... | collective-permute-start | bytes 786440 | tf_op jit(solution)/shard_map/ppermute | solution.py:422
  86.1 0.9 copy-start.2
  113.3 1.8 %collective-permute-start.18 = (bf16[2,688,128]{2,1,0:T(8,128)(2,1)S(1)}, bf16[2,688,128]{2,1,0:T(8,128)(2,1)S(1)}, u32[]{:S(2)}, u32[]{:S(2)}) collective-permute-start(bf16[2,688,128]{2,1,0:T(8,128)(2,1)S(1)} %get-tuple-element.52), channel_id=1, source_target_pairs={{0,8},{8,0},{16,24},{24,16},{32,40},{40,32},{48,56},{56,48},{64,72... | collective-permute-start | bytes 1056776 | tf_op jit(solution)/shard_map/ppermute | solution.py:551
  113.4 2.2 %collective-permute-start.26 = (bf16[2,688,128]{2,1,0:T(8,128)(2,1)S(1)}, bf16[2,688,128]{2,1,0:T(8,128)(2,1)S(1)}, u32[]{:S(2)}, u32[]{:S(2)}) collective-permute-start(bf16[2,688,128]{2,1,0:T(8,128)(2,1)S(1)} %get-tuple-element.61), channel_id=1, source_target_pairs={{0,8},{8,0},{16,24},{24,16},{32,40},{40,32},{48,56},{56,48},{64,72... | collective-permute-start | bytes 1056776 | tf_op jit(solution)/shard_map/ppermute | solution.py:551
  115.2 7.4 %collective-permute-start.19 = (bf16[688,128]{1,0:T(8,128)(2,1)S(1)}, bf16[688,128]{1,0:T(8,128)(2,1)S(1)}, u32[]{:S(2)}, u32[]{:S(2)}) collective-permute-start(bf16[688,128]{1,0:T(8,128)(2,1)S(1)} %merge.2), channel_id=1, source_target_pairs={{0,16},{8,24},{16,0},{24,8},{32,48},{40,56},{48,32},{56,40},{64,80... | collective-permute-start | bytes 528392 | tf_op jit(solution)/shard_map/ppermute | solution.py:563
  115.7 10.7 %collective-permute-start.27 = (bf16[688,128]{1,0:T(8,128)(2,1)S(1)}, bf16[688,128]{1,0:T(8,128)(2,1)S(1)}, u32[]{:S(2)}, u32[]{:S(2)}) collective-permute-start(bf16[688,128]{1,0:T(8,128)(2,1)S(1)} %merge.3), channel_id=1, source_target_pairs={{0,16},{8,24},{16,0},{24,8},{32,48},{40,56},{48,32},{56,40},{64,80... | collective-permute-start | bytes 528392 | tf_op jit(solution)/shard_map/ppermute | solution.py:563
  123.3 7.8 %collective-permute-start.20 = (bf16[128,640]{1,0:T(8,128)(2,1)S(1)}, bf16[128,640]{1,0:T(8,128)(2,1)S(1)}, u32[]{:S(2)}, u32[]{:S(2)}) collective-permute-start(bf16[128,640]{1,0:T(8,128)(2,1)S(1)} %combine.2.attn_near), channel_id=1, source_target_pairs={{0,4},{1,5},{2,6},{3,7},{4,0},{5,1},{6,2},{7,3},{8,12},{9,13},{10,... | collective-permute-start | bytes 491528 | tf_op jit(solution)/shard_map/ppermute | solution.py:577
  127.1 14.1 %collective-permute-start.28 = (bf16[128,640]{1,0:T(8,128)(2,1)S(1)}, bf16[128,640]{1,0:T(8,128)(2,1)S(1)}, u32[]{:S(2)}, u32[]{:S(2)}) collective-permute-start(bf16[128,640]{1,0:T(8,128)(2,1)S(1)} %combine.3.attn_near), channel_id=1, source_target_pairs={{0,4},{1,5},{2,6},{3,7},{4,0},{5,1},{6,2},{7,3},{8,12},{9,13},{10,... | collective-permute-start | bytes 491528 | tf_op jit(solution)/shard_map/ppermute | solution.py:577
  131.2 1.2 copy-start.5
  136.4 12.8 %collective-permute-start.23 = (bf16[128,640]{1,0:T(8,128)(2,1)S(1)}, bf16[128,640]{1,0:T(8,128)(2,1)S(1)}, u32[]{:S(2)}, u32[]{:S(2)}) collective-permute-start(bf16[128,640]{1,0:T(8,128)(2,1)S(1)} %get-tuple-element.56), channel_id=1, source_target_pairs={{0,1},{1,0},{2,3},{3,2},{4,5},{5,4},{6,7},{7,6},{8,9},{9,8},{10,11... | collective-permute-start | bytes 491528 | tf_op jit(solution)/shard_map/ppermute | solution.py:604
  138.0 11.9 %collective-permute-start.24 = (bf16[128,640]{1,0:T(8,128)(2,1)S(1)}, bf16[128,640]{1,0:T(8,128)(2,1)S(1)}, u32[]{:S(2)}, u32[]{:S(2)}) collective-permute-start(bf16[128,640]{1,0:T(8,128)(2,1)S(1)} %get-tuple-element.57), channel_id=1, source_target_pairs={{0,2},{1,3},{2,0},{3,1},{4,6},{5,7},{6,4},{7,5},{8,10},{9,11},{10,... | collective-permute-start | bytes 491528 | tf_op jit(solution)/shard_map/ppermute | solution.py:604
  140.6 9.3 %collective-permute-start.25 = (bf16[128,640]{1,0:T(8,128)(2,1)S(1)}, bf16[128,640]{1,0:T(8,128)(2,1)S(1)}, u32[]{:S(2)}, u32[]{:S(2)}) collective-permute-start(bf16[128,640]{1,0:T(8,128)(2,1)S(1)} %get-tuple-element.58), channel_id=1, source_target_pairs={{0,3},{1,2},{2,1},{3,0},{4,7},{5,6},{6,5},{7,4},{8,11},{9,10},{10,... | collective-permute-start | bytes 491528 | tf_op jit(solution)/shard_map/ppermute | solution.py:604
  145.1 18.5 %copy-start.7 = (bf16[640]{0:T(1024)(128)(2,1)S(1)}, bf16[640]{0:T(1024)(128)(2,1)}, u32[]{:S(2)}) copy-start(bf16[640]{0:T(1024)(128)(2,1)} %param.21) | copy-start | bytes 3844
  145.1 5.4 %collective-permute-start.29 = (bf16[128,640]{1,0:T(8,128)(2,1)S(1)}, bf16[128,640]{1,0:T(8,128)(2,1)S(1)}, u32[]{:S(2)}, u32[]{:S(2)}) collective-permute-start(bf16[128,640]{1,0:T(8,128)(2,1)S(1)} %get-tuple-element.65), channel_id=1, source_target_pairs={{0,1},{1,0},{2,3},{3,2},{4,5},{5,4},{6,7},{7,6},{8,9},{9,8},{10,11... | collective-permute-start | bytes 491528 | tf_op jit(solution)/shard_map/ppermute | solution.py:604
  145.6 8.6 %collective-permute-start.30 = (bf16[128,640]{1,0:T(8,128)(2,1)S(1)}, bf16[128,640]{1,0:T(8,128)(2,1)S(1)}, u32[]{:S(2)}, u32[]{:S(2)}) collective-permute-start(bf16[128,640]{1,0:T(8,128)(2,1)S(1)} %get-tuple-element.66), channel_id=1, source_target_pairs={{0,2},{1,3},{2,0},{3,1},{4,6},{5,7},{6,4},{7,5},{8,10},{9,11},{10,... | collective-permute-start | bytes 491528 | tf_op jit(solution)/shard_map/ppermute | solution.py:604
  149.1 6.8 %collective-permute-start.31 = (bf16[128,640]{1,0:T(8,128)(2,1)S(1)}, bf16[128,640]{1,0:T(8,128)(2,1)S(1)}, u32[]{:S(2)}, u32[]{:S(2)}) collective-permute-start(bf16[128,640]{1,0:T(8,128)(2,1)S(1)} %get-tuple-element.67), channel_id=1, source_target_pairs={{0,3},{1,2},{2,1},{3,0},{4,7},{5,6},{6,5},{7,4},{8,11},{9,10},{10,... | collective-permute-start | bytes 491528 | tf_op jit(solution)/shard_map/ppermute | solution.py:604
  157.2 12.2 %copy-start.6 = (bf16[256,640]{1,0:T(8,128)(2,1)}, bf16[256,640]{1,0:T(8,128)(2,1)S(1)}, u32[]{:S(2)}) copy-start(bf16[256,640]{1,0:T(8,128)(2,1)S(1)} %get-tuple-element.74) | copy-start | bytes 983044
  157.2 5.2 %collective-permute-start.32 = (f32[8,128]{1,0:T(8,128)S(1)}, f32[8,128]{1,0:T(8,128)S(1)}, u32[]{:S(2)}, u32[]{:S(2)}) collective-permute-start(f32[8,128]{1,0:T(8,128)S(1)} %pad.4), channel_id=1, source_target_pairs={{0,2},{1,3},{2,0},{3,1},{4,6},{5,7},{6,4},{7,5},{8,10},{9,11},{10,... | collective-permute-start | bytes 12296 | tf_op jit(solution)/shard_map/ppermute | solution.py:615
  157.6 4.9 %collective-permute-start.33 = (f32[8,128]{1,0:T(8,128)S(1)}, f32[8,128]{1,0:T(8,128)S(1)}, u32[]{:S(2)}, u32[]{:S(2)}) collective-permute-start(f32[8,128]{1,0:T(8,128)S(1)} %pad.4), channel_id=1, source_target_pairs={{0,3},{1,2},{2,1},{3,0},{4,7},{5,6},{6,5},{7,4},{8,11},{9,10},{10,... | collective-permute-start | bytes 12296 | tf_op jit(solution)/shard_map/ppermute | solution.py:615
  159.7 3.6 %collective-permute-start.34 = (f32[8,128]{1,0:T(8,128)S(1)}, f32[8,128]{1,0:T(8,128)S(1)}, u32[]{:S(2)}, u32[]{:S(2)}) collective-permute-start(f32[8,128]{1,0:T(8,128)S(1)} %pad.4), channel_id=1, source_target_pairs={{0,1},{1,0},{2,3},{3,2},{4,5},{5,4},{6,7},{7,6},{8,9},{9,8},{10,11... | collective-permute-start | bytes 12296 | tf_op jit(solution)/shard_map/ppermute | solution.py:615
  163.3 5.1 %collective-permute-start.35 = (f32[8,128]{1,0:T(8,128)S(1)}, f32[8,128]{1,0:T(8,128)S(1)}, u32[]{:S(2)}, u32[]{:S(2)}) collective-permute-start(f32[8,128]{1,0:T(8,128)S(1)} %add_add_fusion), channel_id=1, source_target_pairs={{0,4},{1,5},{2,6},{3,7},{4,0},{5,1},{6,2},{7,3},{8,12},{9,13},{10,... | collective-permute-start | bytes 12296 | tf_op jit(solution)/shard_map/ppermute | solution.py:616
